TPU v7x, 32 devices: a whole 2x2x4 slice. The times are simulated.
32 devices in a mesh: rep: 8 (over z, core), fsdp: 4 (over y, x).
Axes of the slice: x: 2, y: 2, z: 4, core: 2. Of those that a mesh axis runs over, the one named last changes fastest.
Arguments:
- tokens: bfloat16 [8192, 2048], P(('rep', 'fsdp')), may hold values from -6 to 6
- teacher: bfloat16 [8192, 2048], P(('rep', 'fsdp')), may hold values from -6 to 6
- lengths: int32 [64], replicated, may hold values from 1 to 255, as said below
- deal_order: int32 [64], replicated, may hold values from 0 to 63, as said below
- attention_gain: bfloat16 [2048], P('fsdp'), may hold values from 0.5 to 1.5
- query_gain: bfloat16 [128], P('fsdp'), may hold values from 1 to 2
- key_gain: bfloat16 [128], P('fsdp'), may hold values from 1 to 2
- w_query: bfloat16 [2048, 2048], P('fsdp'), may hold values from -0.125 to 0.125
- w_key: bfloat16 [2048, 1024], P('fsdp'), may hold values from -0.125 to 0.125
- w_value: bfloat16 [2048, 1024], P('fsdp'), may hold values from -0.125 to 0.125
- w_outgate: bfloat16 [2048, 2048], P('fsdp'), may hold values from -0.125 to 0.125
- w_output: bfloat16 [2048, 2048], P('fsdp'), may hold values from -0.75 to 0.75
- mlp_gain: bfloat16 [2048], P('fsdp'), may hold values from 0.5 to 1.5
- w_gate: bfloat16 [2048, 6144], P('fsdp'), may hold values from -0.125 to 0.125
- w_up: bfloat16 [2048, 6144], P('fsdp'), may hold values from -0.125 to 0.125
- w_down: bfloat16 [6144, 2048], P('fsdp'), may hold values from -0.078125 to 0.078125
Outputs:
- block_out: bfloat16 [8192, 2048], P(('rep', 'fsdp'))
- seq_loss: float32 [64], P(('rep', 'fsdp'))
- tokens_grad: bfloat16 [8192, 2048], P(('rep', 'fsdp'))
- attention_dgain: float32 [2048], P('fsdp')
- query_dgain: float32 [128], P('fsdp')
- key_dgain: float32 [128], P('fsdp')
- dw_query: float32 [2048, 2048], P('fsdp')
- dw_key: float32 [2048, 1024], P('fsdp')
- dw_value: float32 [2048, 1024], P('fsdp')
- dw_outgate: float32 [2048, 2048], P('fsdp')
- dw_output: float32 [2048, 2048], P('fsdp')
- mlp_dgain: float32 [2048], P('fsdp')
- dw_gate: float32 [2048, 6144], P('fsdp')
- dw_up: float32 [2048, 6144], P('fsdp')
- dw_down: float32 [6144, 2048], P('fsdp')
Inputs may be any that keep to these rules, and one draw needn't show every extreme that they name: `lengths`: each block of 256 rows holds 256 tokens or fewer of its two sequences together; in every draw one block holds exactly 256. `deal_order`: A permutation of the sequence numbers.
All inputs are finite; a program needn't handle non-finite values.
Results may differ from a plain program's by a relative error of at most 0.012.
The roundings to bfloat16 on the way count: a program that leaves them out, or rounds other values in their place, can miss the bound.
Values may be sent and summed in bfloat16 or wider, within the bound.
A program may use at most 512 MiB of HBM per device.

v0:
```python
import jax
import jax.numpy as jnp
from jax import lax
from jax.sharding import PartitionSpec as P

H = 16
KV = 8
HD = 128


EPS_NORM = 1e-06
ROPE_BASE = 1000000.0
NEG_FILL = -1e30


def rms_scale(values, gain_vec):
    return (
        values * lax.rsqrt(jnp.mean(values * values, axis=-1, keepdims=True) + EPS_NORM) * gain_vec
    )


def rotate(values, angle_cos, angle_sin):
    half_dim = values.shape[-1] // 2
    turned = jnp.concatenate([-values[..., half_dim:], values[..., :half_dim]], axis=-1)
    return values * angle_cos + turned * angle_sin


def row_layout(pair_len, row_count, head_dim):
    row_index = jnp.arange(row_count, dtype=jnp.int32)
    head_len = pair_len[0]
    both_len = pair_len[0] + pair_len[1]
    segment = (row_index >= head_len).astype(jnp.int32) + (row_index >= both_len).astype(jnp.int32)
    start_row = jnp.where(segment == 0, 0, jnp.where(segment == 1, head_len, both_len))
    position = (row_index - start_row).astype(jnp.float32)
    inv_freq = jnp.power(ROPE_BASE, -jnp.arange(0, head_dim, 2, dtype=jnp.float32) / head_dim)
    angles = position[:, None] * inv_freq[None, :]
    angles = jnp.concatenate([angles, angles], axis=-1)
    return (row_index, segment, jnp.cos(angles), jnp.sin(angles))


def times_trans(left_side, right_side):
    return lax.dot_general(
        left_side, right_side, (((1,), (1,)), ((), ())), preferred_element_type=jnp.float32
    )


def trans_times(left_side, right_side):
    return lax.dot_general(
        left_side, right_side, (((0,), (0,)), ((), ())), preferred_element_type=jnp.float32
    )


def rep_major(values, n_rep, n_fsdp):
    lead_shape = values.shape[:-1]
    width_all = values.shape[-1]
    blocked = values.reshape(lead_shape + (n_fsdp, n_rep, width_all // (n_rep * n_fsdp)))
    return blocked.swapaxes(-3, -2).reshape(lead_shape + (width_all,))


def gating(context, gate_heads):
    return context * jax.nn.sigmoid(gate_heads)


def swiglu(gate_pre, up_pre):
    return jax.nn.silu(gate_pre) * up_pre


def shards(
    tokens,
    teacher,
    lengths,
    deal_order,
    attention_gain,
    query_gain,
    key_gain,
    w_query,
    w_key,
    w_value,
    w_outgate,
    w_output,
    mlp_gain,
    w_gate,
    w_up,
    w_down,
):
    n_rep = lax.axis_size("rep")
    n_fsdp = lax.axis_size("fsdp")
    row_count = tokens.shape[0]
    device = lax.axis_index("rep") * n_fsdp + lax.axis_index("fsdp")
    slot_ids = device * 2 + jnp.arange(2, dtype=jnp.int32)
    seq_ids = jnp.arange(lengths.shape[0], dtype=jnp.int32)
    slot_seq = jnp.sum(
        jnp.where(seq_ids[None, :] == slot_ids[:, None], deal_order[None, :], 0), axis=1
    )
    pair_len = jnp.sum(
        jnp.where(seq_ids[None, :] == slot_seq[:, None], lengths[None, :], 0), axis=1
    )
    token_count = jnp.sum(lengths).astype(jnp.float32)
    factor = row_count * n_rep * n_fsdp / (2.0 * token_count)
    row_index, segment, angle_cos, angle_sin = row_layout(pair_len, row_count, HD)
    allowed = (segment[:, None] == segment[None, :]) & (row_index[None, :] <= row_index[:, None])
    valid_row = (segment < 2).astype(jnp.float32)
    score_scale = HD ** (-0.5)

    def arrange(values):
        return rep_major(values, n_rep, n_fsdp)

    attn_set = (
        lax.all_gather(attention_gain, "fsdp", axis=0, tiled=True),
        lax.all_gather(query_gain, "fsdp", axis=0, tiled=True),
        lax.all_gather(key_gain, "fsdp", axis=0, tiled=True),
        lax.all_gather(w_query, "fsdp", axis=0, tiled=True),
        lax.all_gather(w_key, "fsdp", axis=0, tiled=True),
        lax.all_gather(w_value, "fsdp", axis=0, tiled=True),
        lax.all_gather(w_outgate, "fsdp", axis=0, tiled=True),
        lax.all_gather(w_output, "fsdp", axis=0, tiled=True),
    )
    tokens_f = tokens.astype(jnp.float32)
    normed, norm_back = jax.vjp(rms_scale, tokens_f, attn_set[0].astype(jnp.float32))
    normed_b = normed.astype(jnp.bfloat16)
    query_raw = jnp.dot(normed_b, attn_set[3], preferred_element_type=jnp.float32)
    key_raw = jnp.dot(normed_b, attn_set[4], preferred_element_type=jnp.float32)
    value_raw = jnp.dot(normed_b, attn_set[5], preferred_element_type=jnp.float32)
    gate_raw = jnp.dot(normed_b, attn_set[6], preferred_element_type=jnp.float32)
    value_b = value_raw.astype(jnp.bfloat16).reshape(row_count, KV, HD)

    def prepare_heads(query_in, key_in, query_scale, key_scale):
        query_heads = rms_scale(query_in.reshape(row_count, KV, H // KV, HD), query_scale)
        query_heads = rotate(query_heads, angle_cos[:, None, None, :], angle_sin[:, None, None, :])
        key_heads = rms_scale(key_in.reshape(row_count, KV, HD), key_scale)
        key_heads = rotate(key_heads, angle_cos[:, None, :], angle_sin[:, None, :])
        return (query_heads, key_heads)

    head_pair, heads_back = jax.vjp(
        prepare_heads,
        query_raw,
        key_raw,
        attn_set[1].astype(jnp.float32),
        attn_set[2].astype(jnp.float32),
    )
    queries_b = head_pair[0].astype(jnp.bfloat16)
    keys_b = head_pair[1].astype(jnp.bfloat16)
    scores = (
        jnp.einsum("qkgd,pkd->kgqp", queries_b, keys_b, preferred_element_type=jnp.float32)
        * score_scale
    )
    scores = jnp.where(allowed, scores, NEG_FILL)
    row_top = jnp.max(scores, axis=-1, keepdims=True)
    exponent = jnp.exp(scores - row_top)
    row_total = jnp.sum(exponent, axis=-1, keepdims=True)
    probs_b = (exponent / row_total).astype(jnp.bfloat16)
    log_total = row_top + jnp.log(row_total)
    context = jnp.einsum("kgqp,pkd->qkgd", probs_b, value_b, preferred_element_type=jnp.float32)
    gate_heads = gate_raw.reshape(row_count, KV, H // KV, HD)
    gated_out, gating_back = jax.vjp(gating, context, gate_heads)
    gated_b = gated_out.reshape(row_count, H * HD).astype(jnp.bfloat16)
    middle = tokens_f + jnp.dot(gated_b, attn_set[7], preferred_element_type=jnp.float32)
    mlp_set = (
        lax.all_gather(mlp_gain, "fsdp", axis=0, tiled=True),
        lax.all_gather(w_gate, "fsdp", axis=0, tiled=True),
        lax.all_gather(w_up, "fsdp", axis=0, tiled=True),
        lax.all_gather(w_down, "fsdp", axis=0, tiled=True),
    )
    normed_mlp, mlp_norm_back = jax.vjp(rms_scale, middle, mlp_set[0].astype(jnp.float32))
    normed_mlp_b = normed_mlp.astype(jnp.bfloat16)
    gate_pre = jnp.dot(normed_mlp_b, mlp_set[1], preferred_element_type=jnp.float32)
    up_pre = jnp.dot(normed_mlp_b, mlp_set[2], preferred_element_type=jnp.float32)
    hidden, swiglu_back = jax.vjp(swiglu, gate_pre, up_pre)
    hidden_b = hidden.astype(jnp.bfloat16)
    result = middle + jnp.dot(hidden_b, mlp_set[3], preferred_element_type=jnp.float32)
    error_rows = (result - teacher.astype(jnp.float32)) * valid_row[:, None]
    row_sq = jnp.sum(error_rows * error_rows, axis=-1)
    slot_mask = (segment[:, None] == jnp.arange(2, dtype=jnp.int32)[None, :]).astype(jnp.float32)
    seq_loss = jnp.sum(row_sq[:, None] * slot_mask, axis=0) / (2.0 * token_count)
    block_out = (result * valid_row[:, None]).astype(jnp.bfloat16)
    grad_result = 2.0 * factor * error_rows
    grad_branch_b = grad_result.astype(jnp.bfloat16)
    mlp_back = (
        lax.all_gather(mlp_gain, "fsdp", axis=0, tiled=True),
        lax.all_gather(w_gate, "fsdp", axis=0, tiled=True),
        lax.all_gather(w_up, "fsdp", axis=0, tiled=True),
        lax.all_gather(w_down, "fsdp", axis=0, tiled=True),
    )
    grad_hidden = times_trans(grad_branch_b, mlp_back[3])
    grad_gate_pre, grad_up_pre = swiglu_back(grad_hidden)
    grad_gate_b = grad_gate_pre.astype(jnp.bfloat16)
    grad_up_b = grad_up_pre.astype(jnp.bfloat16)
    grad_normed_mlp = times_trans(grad_gate_b, mlp_back[1]) + times_trans(grad_up_b, mlp_back[2])
    grad_middle_norm, grad_mlp_gain = mlp_norm_back(grad_normed_mlp)
    grad_middle = grad_result + grad_middle_norm
    normed_mlp_cols = arrange(normed_mlp_b)
    mlp_pieces = (
        lax.psum_scatter(arrange(grad_mlp_gain), ("rep", "fsdp"), scatter_dimension=0, tiled=True),
        lax.psum_scatter(
            trans_times(normed_mlp_cols, grad_gate_b),
            ("rep", "fsdp"),
            scatter_dimension=0,
            tiled=True,
        ),
        lax.psum_scatter(
            trans_times(normed_mlp_cols, grad_up_b),
            ("rep", "fsdp"),
            scatter_dimension=0,
            tiled=True,
        ),
        lax.psum_scatter(
            trans_times(arrange(hidden_b), grad_branch_b),
            ("rep", "fsdp"),
            scatter_dimension=0,
            tiled=True,
        ),
    )
    grad_attn_b = grad_middle.astype(jnp.bfloat16)
    attn_back = (
        lax.all_gather(attention_gain, "fsdp", axis=0, tiled=True),
        lax.all_gather(query_gain, "fsdp", axis=0, tiled=True),
        lax.all_gather(key_gain, "fsdp", axis=0, tiled=True),
        lax.all_gather(w_query, "fsdp", axis=0, tiled=True),
        lax.all_gather(w_key, "fsdp", axis=0, tiled=True),
        lax.all_gather(w_value, "fsdp", axis=0, tiled=True),
        lax.all_gather(w_outgate, "fsdp", axis=0, tiled=True),
        lax.all_gather(w_output, "fsdp", axis=0, tiled=True),
    )
    grad_gated = times_trans(grad_attn_b, attn_back[7]).reshape(row_count, KV, H // KV, HD)
    grad_context, grad_gate_heads = gating_back(grad_gated)
    grad_context_b = grad_context.astype(jnp.bfloat16)
    grad_outgate_b = grad_gate_heads.reshape(row_count, H * HD).astype(jnp.bfloat16)
    scores_again = (
        jnp.einsum("qkgd,pkd->kgqp", queries_b, keys_b, preferred_element_type=jnp.float32)
        * score_scale
    )
    probs_again = jnp.where(allowed, jnp.exp(scores_again - log_total), 0.0)
    grad_value = jnp.einsum(
        "kgqp,qkgd->pkd",
        probs_again.astype(jnp.bfloat16),
        grad_context_b,
        preferred_element_type=jnp.float32,
    )
    grad_probs = jnp.einsum(
        "qkgd,pkd->kgqp", grad_context_b, value_b, preferred_element_type=jnp.float32
    )
    grad_scores = probs_again * (
        grad_probs - jnp.sum(probs_again * grad_probs, axis=-1, keepdims=True)
    )
    grad_scores_b = grad_scores.astype(jnp.bfloat16)
    grad_queries = (
        jnp.einsum("kgqp,pkd->qkgd", grad_scores_b, keys_b, preferred_element_type=jnp.float32)
        * score_scale
    )
    grad_keys = (
        jnp.einsum("kgqp,qkgd->pkd", grad_scores_b, queries_b, preferred_element_type=jnp.float32)
        * score_scale
    )
    grad_query_raw, grad_key_raw, grad_query_gain, grad_key_gain = heads_back(
        (grad_queries, grad_keys)
    )
    grad_query_b = grad_query_raw.astype(jnp.bfloat16)
    grad_key_b = grad_key_raw.astype(jnp.bfloat16)
    grad_value_b = grad_value.reshape(row_count, KV * HD).astype(jnp.bfloat16)
    grad_normed = (
        times_trans(grad_query_b, attn_back[3])
        + times_trans(grad_key_b, attn_back[4])
        + times_trans(grad_value_b, attn_back[5])
        + times_trans(grad_outgate_b, attn_back[6])
    )
    grad_tokens_norm, grad_attention_gain = norm_back(grad_normed)
    tokens_grad = (grad_middle + grad_tokens_norm).astype(jnp.bfloat16)
    normed_cols = arrange(normed_b)
    attn_pieces = (
        lax.psum_scatter(
            arrange(grad_attention_gain), ("rep", "fsdp"), scatter_dimension=0, tiled=True
        ),
        lax.psum_scatter(
            arrange(grad_query_gain), ("rep", "fsdp"), scatter_dimension=0, tiled=True
        ),
        lax.psum_scatter(arrange(grad_key_gain), ("rep", "fsdp"), scatter_dimension=0, tiled=True),
        lax.psum_scatter(
            trans_times(normed_cols, grad_query_b), ("rep", "fsdp"), scatter_dimension=0, tiled=True
        ),
        lax.psum_scatter(
            trans_times(normed_cols, grad_key_b), ("rep", "fsdp"), scatter_dimension=0, tiled=True
        ),
        lax.psum_scatter(
            trans_times(normed_cols, grad_value_b), ("rep", "fsdp"), scatter_dimension=0, tiled=True
        ),
        lax.psum_scatter(
            trans_times(normed_cols, grad_outgate_b),
            ("rep", "fsdp"),
            scatter_dimension=0,
            tiled=True,
        ),
        lax.psum_scatter(
            trans_times(arrange(gated_b), grad_attn_b),
            ("rep", "fsdp"),
            scatter_dimension=0,
            tiled=True,
        ),
    )
    grads_all = (
        lax.all_gather(attn_pieces[0], "rep", axis=0, tiled=True),
        lax.all_gather(attn_pieces[1], "rep", axis=0, tiled=True),
        lax.all_gather(attn_pieces[2], "rep", axis=0, tiled=True),
        lax.all_gather(attn_pieces[3], "rep", axis=0, tiled=True),
        lax.all_gather(attn_pieces[4], "rep", axis=0, tiled=True),
        lax.all_gather(attn_pieces[5], "rep", axis=0, tiled=True),
        lax.all_gather(attn_pieces[6], "rep", axis=0, tiled=True),
        lax.all_gather(attn_pieces[7], "rep", axis=0, tiled=True),
        lax.all_gather(mlp_pieces[0], "rep", axis=0, tiled=True),
        lax.all_gather(mlp_pieces[1], "rep", axis=0, tiled=True),
        lax.all_gather(mlp_pieces[2], "rep", axis=0, tiled=True),
        lax.all_gather(mlp_pieces[3], "rep", axis=0, tiled=True),
    )
    return (
        block_out,
        seq_loss,
        tokens_grad,
        grads_all[0],
        grads_all[1],
        grads_all[2],
        grads_all[3],
        grads_all[4],
        grads_all[5],
        grads_all[6],
        grads_all[7],
        grads_all[8],
        grads_all[9],
        grads_all[10],
        grads_all[11],
    )


def solution(mesh):
    return jax.shard_map(
        shards,
        mesh=mesh,
        in_specs=(
            P(("rep", "fsdp"), None),
            P(("rep", "fsdp"), None),
            P(),
            P(),
            P("fsdp"),
            P("fsdp"),
            P("fsdp"),
            P("fsdp", None),
            P("fsdp", None),
            P("fsdp", None),
            P("fsdp", None),
            P("fsdp", None),
            P("fsdp"),
            P("fsdp", None),
            P("fsdp", None),
            P("fsdp", None),
        ),
        out_specs=(
            P(("rep", "fsdp"), None),
            P(("rep", "fsdp")),
            P(("rep", "fsdp"), None),
            P("fsdp"),
            P("fsdp"),
            P("fsdp"),
            P("fsdp", None),
            P("fsdp", None),
            P("fsdp", None),
            P("fsdp", None),
            P("fsdp", None),
            P("fsdp"),
            P("fsdp", None),
            P("fsdp", None),
            P("fsdp", None),
        ),
        check_vma=False,
    )
```

profile of v0, /device:TPU:0, one launch (start us, length us, event | category | flops | bytes accessed | tf_op | source)
XLA Modules:
  0.0 4536.0 jit_solution(17574576630631297183)
XLA Ops:
  69.8 50.2 %all-gather.21.cloned.1.call-done = bf16[2048,1024]{1,0:T(8,128)(2,1)} async-done(((bf16[512,1024]{1,0:T(8,128)(2,1)}), bf16[2048,1024]{1,0:T(8,128)(2,1)}) %all-gather.21.cloned.1.call-update) | async-done | bytes 4194320 | tf_op jit(solution)/shard_map/all_gather | solution.py:113
  128.3 81.2 %all-gather.25.cloned.1.call-done = bf16[2048,2048]{1,0:T(8,128)(2,1)} async-done(((bf16[512,2048]{1,0:T(8,128)(2,1)}), bf16[2048,2048]{1,0:T(8,128)(2,1)}) %all-gather.25.cloned.1.call-update) | async-done | bytes 8388624 | tf_op jit(solution)/shard_map/all_gather | solution.py:115
  219.8 79.0 %all-gather.23.cloned.1.call-done = bf16[2048,2048]{1,0:T(8,128)(2,1)} async-done(((bf16[512,2048]{1,0:T(8,128)(2,1)}), bf16[2048,2048]{1,0:T(8,128)(2,1)}) %all-gather.23.cloned.1.call-update) | async-done | bytes 8388624 | tf_op jit(solution)/shard_map/all_gather | solution.py:112
  329.4 58.7 %all-gather.27.cloned.1.call-done = bf16[2048,2048]{1,0:T(8,128)(2,1)} async-done(((bf16[512,2048]{1,0:T(8,128)(2,1)}), bf16[2048,2048]{1,0:T(8,128)(2,1)}) %all-gather.27.cloned.1.call-update) | async-done | bytes 8388624 | tf_op jit(solution)/shard_map/all_gather | solution.py:116
  394.6 223.0 %all-gather.29.cloned.1.call-done = bf16[2048,6144]{1,0:T(8,128)(2,1)} async-done(((bf16[512,6144]{1,0:T(8,128)(2,1)}), bf16[2048,6144]{1,0:T(8,128)(2,1)}) %all-gather.29.cloned.1.call-update) | async-done | bytes 25165840 | tf_op jit(solution)/shard_map/all_gather | solution.py:160
  633.1 214.1 %all-gather.31.cloned.1.call-done = bf16[2048,6144]{1,0:T(8,128)(2,1)} async-done(((bf16[512,6144]{1,0:T(8,128)(2,1)}), bf16[2048,6144]{1,0:T(8,128)(2,1)}) %all-gather.31.cloned.1.call-update) | async-done | bytes 25165840 | tf_op jit(solution)/shard_map/all_gather | solution.py:161
  847.2 34.8 multiply_convert_fusion.1
  882.0 194.8 %all-gather.33.cloned.1.call-done = bf16[6144,2048]{1,0:T(8,128)(2,1)} async-done(((bf16[1536,2048]{1,0:T(8,128)(2,1)}), bf16[6144,2048]{1,0:T(8,128)(2,1)}) %all-gather.33.cloned.1.call-update) | async-done | bytes 25165840 | tf_op jit(solution)/shard_map/all_gather | solution.py:162
  1216.3 21.8 fusion.57
  1285.2 57.3 %reduce-scatter.13.cloned.1.call-done = f32[64,1024]{1,0:T(8,128)} async-done(((f32[2048,1024]{1,0:T(8,128)}), f32[64,1024]{1,0:T(8,128)}) %reduce-scatter.13.cloned.1.call-update) | async-done | bytes 262160 | tf_op jit(solution)/shard_map/reduce_scatter | solution.py:283
  1342.6 187.1 %reduce-scatter.11.cloned.1.call-done = f32[64,1024]{1,0:T(8,128)} async-done(((f32[2048,1024]{1,0:T(8,128)}), f32[64,1024]{1,0:T(8,128)}) %reduce-scatter.11.cloned.1.call-update) | async-done | bytes 262160 | tf_op jit(solution)/shard_map/reduce_scatter | solution.py:280
  1529.8 360.8 %reduce-scatter.17.cloned.1.call-done = f32[64,2048]{1,0:T(8,128)} async-done(((f32[2048,2048]{1,0:T(8,128)}), f32[64,2048]{1,0:T(8,128)}) %reduce-scatter.17.cloned.1.call-update) | async-done | bytes 524304 | tf_op jit(solution)/shard_map/reduce_scatter | solution.py:292
  1890.7 361.2 %reduce-scatter.15.cloned.1.call-done = f32[64,2048]{1,0:T(8,128)} async-done(((f32[2048,2048]{1,0:T(8,128)}), f32[64,2048]{1,0:T(8,128)}) %reduce-scatter.15.cloned.1.call-update) | async-done | bytes 524304 | tf_op jit(solution)/shard_map/reduce_scatter | solution.py:286
  2251.9 361.3 %reduce-scatter.9.cloned.1.call-done = f32[64,2048]{1,0:T(8,128)} async-done(((f32[2048,2048]{1,0:T(8,128)}), f32[64,2048]{1,0:T(8,128)}) %reduce-scatter.9.cloned.1.call-update) | async-done | bytes 524304 | tf_op jit(solution)/shard_map/reduce_scatter | solution.py:277
  2613.3 439.2 %reduce-scatter.23.cloned.1.call-done = f32[192,2048]{1,0:T(8,128)} async-done(((f32[6144,2048]{1,0:T(8,128)}), f32[192,2048]{1,0:T(8,128)}) %reduce-scatter.23.cloned.1.call-update) | async-done | bytes 1572880 | tf_op jit(solution)/shard_map/reduce_scatter | solution.py:206
  3052.6 436.8 %reduce-scatter.21.cloned.1.call-done = f32[64,6144]{1,0:T(8,128)} async-done(((f32[2048,6144]{1,0:T(8,128)}), f32[64,6144]{1,0:T(8,128)}) %reduce-scatter.21.cloned.1.call-update) | async-done | bytes 1572880 | tf_op jit(solution)/shard_map/reduce_scatter | solution.py:200
  3489.7 436.5 %reduce-scatter.19.cloned.1.call-done = f32[64,6144]{1,0:T(8,128)} async-done(((f32[2048,6144]{1,0:T(8,128)}), f32[64,6144]{1,0:T(8,128)}) %reduce-scatter.19.cloned.1.call-update) | async-done | bytes 1572880 | tf_op jit(solution)/shard_map/reduce_scatter | solution.py:194
  3943.4 40.5 all-reduce.14
  4004.7 29.8 all-gather.43.cloned.1.call-done
  4034.5 47.3 %all-gather.41.cloned.1.call-done = f32[512,2048]{1,0:T(8,128)} async-done(((f32[64,2048]{1,0:T(8,128)}), f32[512,2048]{1,0:T(8,128)}) %all-gather.41.cloned.1.call-update) | async-done | bytes 4194320 | tf_op jit(solution)/shard_map/all_gather | solution.py:306
  4081.8 47.5 %all-gather.35.cloned.1.call-done = f32[512,2048]{1,0:T(8,128)} async-done(((f32[64,2048]{1,0:T(8,128)}), f32[512,2048]{1,0:T(8,128)}) %all-gather.35.cloned.1.call-update) | async-done | bytes 4194320 | tf_op jit(solution)/shard_map/all_gather | solution.py:303
  4129.3 117.1 %all-gather.49.cloned.1.call-done = f32[1536,2048]{1,0:T(8,128)} async-done(((f32[192,2048]{1,0:T(8,128)}), f32[1536,2048]{1,0:T(8,128)}) %all-gather.49.cloned.1.call-update) | async-done | bytes 12582928 | tf_op jit(solution)/shard_map/all_gather | solution.py:311
  4246.4 116.6 %all-gather.47.cloned.1.call-done = f32[512,6144]{1,0:T(8,128)} async-done(((f32[64,6144]{1,0:T(8,128)}), f32[512,6144]{1,0:T(8,128)}) %all-gather.47.cloned.1.call-update) | async-done | bytes 12582928 | tf_op jit(solution)/shard_map/all_gather | solution.py:310
  4363.0 116.5 %all-gather.45.cloned.1.call-done = f32[512,6144]{1,0:T(8,128)} async-done(((f32[64,6144]{1,0:T(8,128)}), f32[512,6144]{1,0:T(8,128)}) %all-gather.45.cloned.1.call-update) | async-done | bytes 12582928 | tf_op jit(solution)/shard_map/all_gather | solution.py:309
  (332 shorter events, 402.9 us)
Async XLA Ops:
  7.2 58.2 %all-gather.19.cloned.1.call-start = ((), (), s32[]{:S(2)}) async-start(), calls=%async_computation.8 | async-start | bytes 5242880 | tf_op jit(solution)/shard_map/all_gather | solution.py:114
  7.9 112.1 %all-gather.21.cloned.1.call-start = ((), (), s32[]{:S(2)}) async-start(), calls=%async_computation.9 | async-start | bytes 5242880 | tf_op jit(solution)/shard_map/all_gather | solution.py:113
  8.7 200.8 %all-gather.25.cloned.1.call-start = ((), (), s32[]{:S(2)}) async-start(), calls=%async_computation.11 | async-start | bytes 10485760 | tf_op jit(solution)/shard_map/all_gather | solution.py:115
  9.4 289.4 %all-gather.23.cloned.1.call-start = ((), (), s32[]{:S(2)}) async-start(), calls=%async_computation.10 | async-start | bytes 10485760 | tf_op jit(solution)/shard_map/all_gather | solution.py:112
  10.0 378.2 %all-gather.27.cloned.1.call-start = ((), (), s32[]{:S(2)}) async-start(), calls=%async_computation.12 | async-start | bytes 10485760 | tf_op jit(solution)/shard_map/all_gather | solution.py:116
  10.6 607.1 %all-gather.29.cloned.1.call-start = ((), (), s32[]{:S(2)}) async-start(), calls=%async_computation.13 | async-start | bytes 31457280 | tf_op jit(solution)/shard_map/all_gather | solution.py:160
  11.1 836.1 %all-gather.31.cloned.1.call-start = ((), (), s32[]{:S(2)}) async-start(), calls=%async_computation.14 | async-start | bytes 31457280 | tf_op jit(solution)/shard_map/all_gather | solution.py:161
  12.0 1064.9 %all-gather.33.cloned.1.call-start = ((), (), s32[]{:S(2)}) async-start(), calls=%async_computation.15 | async-start | bytes 31457280 | tf_op jit(solution)/shard_map/all_gather | solution.py:162
  12.7 1329.8 %reduce-scatter.13.cloned.1.call-start = ((), (), s32[]{:S(2)}) async-start(), calls=%async_computation.20 | async-start | bytes 8650752 | tf_op jit(solution)/shard_map/reduce_scatter | solution.py:283
  1158.8 370.9 %reduce-scatter.11.cloned.1.call-start = ((), (), s32[]{:S(2)}) async-start(), calls=%async_computation.18 | async-start | bytes 8650752 | tf_op jit(solution)/shard_map/reduce_scatter | solution.py:280
  1173.4 717.2 %reduce-scatter.17.cloned.1.call-start = ((), (), s32[]{:S(2)}) async-start(), calls=%async_computation.24 | async-start | bytes 17301504 | tf_op jit(solution)/shard_map/reduce_scatter | solution.py:292
  1183.1 1068.7 %reduce-scatter.15.cloned.1.call-start = ((), (), s32[]{:S(2)}) async-start(), calls=%async_computation.22 | async-start | bytes 17301504 | tf_op jit(solution)/shard_map/reduce_scatter | solution.py:286
  1192.6 1420.6 %reduce-scatter.9.cloned.1.call-start = ((), (), s32[]{:S(2)}) async-start(), calls=%async_computation.16 | async-start | bytes 17301504 | tf_op jit(solution)/shard_map/reduce_scatter | solution.py:277
  1207.4 1845.1 %reduce-scatter.23.cloned.1.call-start = ((), (), s32[]{:S(2)}) async-start(), calls=%async_computation.30 | async-start | bytes 51904512 | tf_op jit(solution)/shard_map/reduce_scatter | solution.py:206
  1238.1 2251.2 %reduce-scatter.21.cloned.1.call-start = ((), (), s32[]{:S(2)}) async-start(), calls=%async_computation.28 | async-start | bytes 51904512 | tf_op jit(solution)/shard_map/reduce_scatter | solution.py:200
  1263.5 2662.7 %reduce-scatter.19.cloned.1.call-start = ((), (), s32[]{:S(2)}) async-start(), calls=%async_computation.26 | async-start | bytes 51904512 | tf_op jit(solution)/shard_map/reduce_scatter | solution.py:194
  1285.1 2719.6 %all-gather.39.cloned.1.call-start = ((), (), s32[]{:S(2)}) async-start(), calls=%async_computation.21 | async-start | bytes 2359296 | tf_op jit(solution)/shard_map/all_gather | solution.py:305
  1342.5 2662.2 %all-gather.37.cloned.1.call-start = ((), (), s32[]{:S(2)}) async-start(), calls=%async_computation.19 | async-start | bytes 2359296 | tf_op jit(solution)/shard_map/all_gather | solution.py:304
  1529.7 2504.8 %all-gather.43.cloned.1.call-start = ((), (), s32[]{:S(2)}) async-start(), calls=%async_computation.25 | async-start | bytes 4718592 | tf_op jit(solution)/shard_map/all_gather | solution.py:307
  1890.6 2191.1 %all-gather.41.cloned.1.call-start = ((), (), s32[]{:S(2)}) async-start(), calls=%async_computation.23 | async-start | bytes 4718592 | tf_op jit(solution)/shard_map/all_gather | solution.py:306
  2251.9 1877.4 %all-gather.35.cloned.1.call-start = ((), (), s32[]{:S(2)}) async-start(), calls=%async_computation.17 | async-start | bytes 4718592 | tf_op jit(solution)/shard_map/all_gather | solution.py:303
  2613.2 1633.2 %all-gather.49.cloned.1.call-start = ((), (), s32[]{:S(2)}) async-start(), calls=%async_computation.31 | async-start | bytes 14155776 | tf_op jit(solution)/shard_map/all_gather | solution.py:311
  3052.5 1310.5 %all-gather.47.cloned.1.call-start = ((), (), s32[]{:S(2)}) async-start(), calls=%async_computation.29 | async-start | bytes 14155776 | tf_op jit(solution)/shard_map/all_gather | solution.py:310
  3489.4 990.2 %all-gather.45.cloned.1.call-start = ((), (), s32[]{:S(2)}) async-start(), calls=%async_computation.27 | async-start | bytes 14155776 | tf_op jit(solution)/shard_map/all_gather | solution.py:309
  (73 other events, 4776.9 us)
Sparse Core Ops, SparseCore 0:
  9.9 55.5 all-gather.18
  67.3 52.6 all-gather.20
  121.8 87.5 all-gather.24
  211.2 87.5 all-gather.22
  300.5 87.5 all-gather.26
  389.9 227.7 all-gather.28
  619.5 227.7 all-gather.30
  849.1 227.7 all-gather.32
  1158.9 183.5 reduce-scatter.12
  1345.2 184.4 reduce-scatter.10
  1532.0 358.5 reduce-scatter.16
  1892.8 359.0 reduce-scatter.14
  2254.1 359.0 reduce-scatter.8
  2619.5 432.9 reduce-scatter.22
  3058.8 430.5 reduce-scatter.20
  3495.6 430.5 reduce-scatter.18
  3927.6 28.1 all-gather.38
  3957.3 28.8 all-gather.36
  3987.8 46.6 all-gather.42
  4036.0 45.7 all-gather.40
  4083.4 45.8 all-gather.34
  4130.9 115.4 all-gather.48
  4248.0 114.9 all-gather.46
  4364.5 114.9 all-gather.44
where the time goes:
time: 4550 us; the launch traced here: 4540 us
  waiting for transfers between devices  4040 us (89%)
  matrix products  270 us (6%)
  local copies, waits for them, and re-layouts  95.3 us (2%)
  blocking collectives  83.6 us (2%)
    reduce_scatter x1, waiting for transfers between devices, shards(): lax.psum_scatter(trans_times(arrange(hidden_b), grad_branch_b), ('rep', '...  439 us
    reduce_scatter x1, waiting for transfers between devices, shards(): lax.psum_scatter(trans_times(normed_mlp_cols, grad_up_b), ('rep', 'fsdp')...  437 us
    reduce_scatter x1, waiting for transfers between devices, shards(): lax.psum_scatter(trans_times(normed_mlp_cols, grad_gate_b), ('rep', 'fsdp...  437 us
    reduce_scatter x1, waiting for transfers between devices, shards(): lax.psum_scatter(trans_times(normed_cols, grad_query_b), ('rep', 'fsdp'),...  361 us
    reduce_scatter x1, waiting for transfers between devices, shards(): lax.psum_scatter(trans_times(normed_cols, grad_outgate_b), ('rep', 'fsdp'...  361 us
    reduce_scatter x1, waiting for transfers between devices, shards(): lax.psum_scatter(trans_times(arrange(gated_b), grad_attn_b), ('rep', 'fsd...  361 us
    all_gather x1, waiting for transfers between devices, shards(): lax.all_gather(w_gate, 'fsdp', axis=0, tiled=True)  223 us
    all_gather x1, waiting for transfers between devices, shards(): lax.all_gather(w_up, 'fsdp', axis=0, tiled=True)  214 us
  transfers between devices with their start and end apart: 24, of which 22 were waited for; matrix products, arithmetic and copies ran while one was open for 6% of the time, Pallas kernels for 0%

commit v1 on v0

v1 whole, which is shorter than its diff:
```python
import jax
import jax.numpy as jnp
from jax import lax
from jax.sharding import PartitionSpec as P

H = 16
KV = 8
HD = 128


EPS_NORM = 1e-06
ROPE_BASE = 1000000.0
NEG_FILL = -1e30


def rms_scale(values, gain_vec):
    return (
        values * lax.rsqrt(jnp.mean(values * values, axis=-1, keepdims=True) + EPS_NORM) * gain_vec
    )


def rotate(values, angle_cos, angle_sin):
    half_dim = values.shape[-1] // 2
    turned = jnp.concatenate([-values[..., half_dim:], values[..., :half_dim]], axis=-1)
    return values * angle_cos + turned * angle_sin


def row_layout(pair_len, row_count, head_dim):
    row_index = jnp.arange(row_count, dtype=jnp.int32)[None, :]
    head_len = pair_len[:, :1]
    both_len = pair_len[:, :1] + pair_len[:, 1:]
    segment = (row_index >= head_len).astype(jnp.int32) + (row_index >= both_len).astype(jnp.int32)
    start_row = jnp.where(segment == 0, 0, jnp.where(segment == 1, head_len, both_len))
    position = (row_index - start_row).astype(jnp.float32)
    inv_freq = jnp.power(ROPE_BASE, -jnp.arange(0, head_dim, 2, dtype=jnp.float32) / head_dim)
    angles = position[..., None] * inv_freq
    angle_cos, angle_sin = jnp.cos(angles), jnp.sin(angles)
    return (
        segment,
        jnp.concatenate([angle_cos, angle_cos], axis=-1),
        jnp.concatenate([angle_sin, angle_sin], axis=-1),
    )


def times(left_side, right_side, out=jnp.float32):
    return jnp.dot(left_side, right_side, preferred_element_type=jnp.float32).astype(out)


def times_trans(left_side, right_side, out=jnp.float32):
    return lax.dot_general(
        left_side, right_side, (((1,), (1,)), ((), ())), preferred_element_type=jnp.float32
    ).astype(out)


def trans_times(left_side, right_side, out=jnp.float32):
    return lax.dot_general(
        left_side, right_side, (((0,), (0,)), ((), ())), preferred_element_type=jnp.float32
    ).astype(out)


def gating(context, gate_heads):
    return context * jax.nn.sigmoid(gate_heads)


def swiglu(gate_pre, up_pre):
    return jax.nn.silu(gate_pre) * up_pre


def in_f32(values):
    return values.astype(jnp.float32)


def in_bf16(values):
    return values.astype(jnp.bfloat16)


def shift(values, step):
    n_fsdp = lax.axis_size("fsdp")
    return lax.ppermute(values, "fsdp", [(i, i ^ step) for i in range(n_fsdp)])


def sibling(values):
    n_rep = lax.axis_size("rep")
    return lax.ppermute(values, "rep", [(i, i ^ 1) for i in range(n_rep)])


def along_line(values, hops):
    return lax.ppermute(
        values, "rep", [(2 * a + core, 2 * b + core) for a, b in hops for core in range(2)]
    )


def line_sum(values):
    n_line = lax.axis_size("rep") // 2
    place = lax.axis_index("rep") // 2
    if n_line == 1:
        return in_bf16(values)
    half = n_line // 2
    total = in_bf16(values)
    for k in range(half - 1):
        got = along_line(total, [(k, k + 1), (n_line - 1 - k, n_line - 2 - k)])
        total = in_bf16(in_f32(total) + in_f32(got))
    got = along_line(total, [(half - 1, half), (half, half - 1)])
    total = in_bf16(in_f32(total) + in_f32(got))
    for k in range(half - 1, 0, -1):
        got = along_line(total, [(k, k - 1), (n_line - 1 - k, n_line - k)])
        total = jnp.where((place == k - 1) | (place == n_line - k), got, total)
    return total


def gather_rows(block):
    n_fsdp = lax.axis_size("fsdp")
    if n_fsdp != 4:
        return [block] + [shift(block, s) for s in range(1, n_fsdp)]
    half = block.shape[0] // 2
    top, low = block[:half], block[half:]
    x_top, y_low = shift(top, 1), shift(low, 2)
    x_low, y_top = shift(low, 1), shift(top, 2)
    d_top, d_low = shift(x_top, 2), shift(y_low, 1)
    return [
        block,
        jnp.concatenate([x_top, x_low]),
        jnp.concatenate([y_top, y_low]),
        jnp.concatenate([d_top, d_low]),
    ]


def scatter_rows(own, parts):
    n_fsdp = lax.axis_size("fsdp")
    if n_fsdp != 4:
        for s in range(1, n_fsdp):
            own = own + in_f32(shift(parts[s - 1], s))
        return own
    half = own.shape[0] // 2
    p_x, p_y, p_d = parts
    r_y = shift(p_d[:half], 1)
    r_x = shift(p_d[half:], 2)
    x_top = shift(p_x[:half], 1)
    y_low = shift(p_y[half:], 2)
    y_top = shift(in_bf16(in_f32(p_y[:half]) + in_f32(r_y)), 2)
    x_low = shift(in_bf16(in_f32(p_x[half:]) + in_f32(r_x)), 1)
    return own + jnp.concatenate(
        [in_f32(x_top) + in_f32(y_top), in_f32(y_low) + in_f32(x_low)]
    )


def shards(
    tokens,
    teacher,
    lengths,
    deal_order,
    attention_gain,
    query_gain,
    key_gain,
    w_query,
    w_key,
    w_value,
    w_outgate,
    w_output,
    mlp_gain,
    w_gate,
    w_up,
    w_down,
):
    n_rep = lax.axis_size("rep")
    n_fsdp = lax.axis_size("fsdp")
    rows, width = tokens.shape
    mine = lax.axis_index("fsdp")
    core = lax.axis_index("rep") % 2
    others = range(1, n_fsdp)
    heads_q, heads_k = H // n_fsdp, KV // n_fsdp
    cols_q, cols_k = heads_q * HD, heads_k * HD
    deep = w_query.shape[0]
    ff = w_down.shape[0]
    rows_all = rows * n_fsdp

    peers = mine ^ jnp.arange(n_fsdp, dtype=jnp.int32)
    devices = lax.axis_index("rep") * n_fsdp + peers
    slot_ids = (devices[:, None] * 2 + jnp.arange(2, dtype=jnp.int32)[None, :]).reshape(-1)
    seq_ids = jnp.arange(lengths.shape[0], dtype=jnp.int32)
    slot_seq = jnp.sum(
        jnp.where(seq_ids[None, :] == slot_ids[:, None], deal_order[None, :], 0), axis=1
    )
    pair_len = jnp.sum(
        jnp.where(seq_ids[None, :] == slot_seq[:, None], lengths[None, :], 0), axis=1
    ).reshape(n_fsdp, 2)
    token_count = jnp.sum(lengths).astype(jnp.float32)
    factor = rows * n_rep * n_fsdp / (2.0 * token_count)
    segments, angle_cos, angle_sin = row_layout(pair_len, rows, HD)
    row_index = jnp.arange(rows, dtype=jnp.int32)
    allowed = (segments[:, :, None] == segments[:, None, :]) & (
        row_index[None, None, :] <= row_index[None, :, None]
    )
    allowed = allowed[:, None, None]
    segment = segments[0]
    valid_row = (segment < 2).astype(jnp.float32)
    score_scale = HD ** (-0.5)

    def column_parts(weights, widths):
        def pick(start_of):
            return jnp.concatenate(
                [
                    lax.dynamic_slice(w, (0, start_of * cols), (deep, cols))
                    for w, cols in zip(weights, widths)
                ],
                axis=1,
            )

        return pick

    def by_columns(weights, widths):
        pick = column_parts(weights, widths)
        half = deep // 2
        cols = sum(widths)
        whole = jnp.zeros((n_fsdp * deep, cols), jnp.bfloat16)
        whole = lax.dynamic_update_slice(whole, pick(mine), (mine * deep, 0))
        for s in others:
            piece = lax.dynamic_slice(pick(mine ^ s), (core * half, 0), (half, cols))
            got = shift(piece, s)
            rest = sibling(got)
            start = (mine ^ s) * deep
            whole = lax.dynamic_update_slice(whole, got, (start + core * half, 0))
            whole = lax.dynamic_update_slice(whole, rest, (start + (1 - core) * half, 0))
        return whole

    gains_own = jnp.concatenate([attention_gain, mlp_gain, query_gain, key_gain])[None]
    gains = jnp.concatenate([gains_own] + [shift(gains_own, s) for s in others], axis=0)
    gains = in_f32(jnp.take(gains, mine ^ jnp.arange(n_fsdp), axis=0))
    small = query_gain.shape[0]
    attention_gain_f = gains[:, :deep].reshape(-1)
    mlp_gain_f = gains[:, deep : 2 * deep].reshape(-1)
    query_gain_f = gains[:, 2 * deep : 2 * deep + small].reshape(-1)
    key_gain_f = gains[:, 2 * deep + small :].reshape(-1)

    tokens_all = jnp.concatenate(gather_rows(tokens))
    w_attn = by_columns((w_query, w_key, w_outgate, w_value), (cols_q, cols_k, cols_q, cols_k))
    w_mlp = by_columns((w_gate, w_up), (ff, ff))

    tokens_f = in_f32(tokens)
    normed_all = in_bf16(rms_scale(in_f32(tokens_all), attention_gain_f))
    attn_raw = times(normed_all, w_attn)
    query_raw = attn_raw[:, :cols_q]
    key_raw = attn_raw[:, cols_q : cols_q + cols_k]
    gate_raw = attn_raw[:, cols_q + cols_k : 2 * cols_q + cols_k]
    value_b = in_bf16(attn_raw[:, 2 * cols_q + cols_k :]).reshape(n_fsdp, rows, heads_k, HD)

    def prepare_heads(query_in, key_in, query_scale, key_scale):
        query_heads = rms_scale(query_in.reshape(n_fsdp, rows, heads_q, HD), query_scale)
        query_heads = rotate(query_heads, angle_cos[:, :, None], angle_sin[:, :, None])
        key_heads = rms_scale(key_in.reshape(n_fsdp, rows, heads_k, HD), key_scale)
        key_heads = rotate(key_heads, angle_cos[:, :, None], angle_sin[:, :, None])
        return (query_heads, key_heads)

    head_pair, heads_back = jax.vjp(prepare_heads, query_raw, key_raw, query_gain_f, key_gain_f)
    queries_b = in_bf16(head_pair[0]).reshape(n_fsdp, rows, heads_k, H // KV, HD)
    keys_b = in_bf16(head_pair[1])

    def dots(spec, left, right):
        return jnp.einsum(spec, left, right, preferred_element_type=jnp.float32)

    scores = dots("sqkgd,spkd->skgqp", queries_b, keys_b) * score_scale
    scores = jnp.where(allowed, scores, NEG_FILL)
    row_top = jnp.max(scores, axis=-1, keepdims=True)
    exponent = jnp.exp(scores - row_top)
    row_total = jnp.sum(exponent, axis=-1, keepdims=True)
    probs_b = in_bf16(exponent / row_total)
    log_total = row_top + jnp.log(row_total)
    context = dots("skgqp,spkd->sqkgd", probs_b, value_b)
    gate_heads = gate_raw.reshape(n_fsdp, rows, heads_k, H // KV, HD)
    gated_out, gating_back = jax.vjp(gating, context, gate_heads)
    gated_b = in_bf16(gated_out.reshape(rows_all, cols_q))

    def summed(left, right, product):
        own = product(left[:rows], right, jnp.float32)
        parts = product(left[rows:], right, jnp.bfloat16)
        return scatter_rows(own, [parts[i * rows : (i + 1) * rows] for i in range(n_fsdp - 1)])

    middle = tokens_f + summed(gated_b, w_output, times)
    normed_mlp, mlp_norm_back = jax.vjp(rms_scale, middle, mlp_gain_f)
    normed_mlp_all = jnp.concatenate(gather_rows(in_bf16(normed_mlp)))
    gate_pre = times(normed_mlp_all, w_mlp[:, :ff])
    up_pre = times(normed_mlp_all, w_mlp[:, ff:])
    hidden, swiglu_back = jax.vjp(swiglu, gate_pre, up_pre)
    hidden_b = in_bf16(hidden)
    result = middle + summed(hidden_b, w_down, times)

    error_rows = (result - in_f32(teacher)) * valid_row[:, None]
    row_sq = jnp.sum(error_rows * error_rows, axis=-1)
    slot_mask = (segment[:, None] == jnp.arange(2, dtype=jnp.int32)[None, :]).astype(jnp.float32)
    seq_loss = jnp.sum(row_sq[:, None] * slot_mask, axis=0) / (2.0 * token_count)
    block_out = in_bf16(result * valid_row[:, None])
    grad_result = 2.0 * factor * error_rows

    def row_sharded(left, right):
        half = left.shape[1] // 2
        keep = trans_times(lax.dynamic_slice_in_dim(left, core * half, half, 1), right)
        send = trans_times(
            lax.dynamic_slice_in_dim(left, (1 - core) * half, half, 1), right, jnp.bfloat16
        )
        total = line_sum(keep + in_f32(sibling(send)))
        rest = sibling(total)
        first = jnp.where(core == 0, total, rest)
        second = jnp.where(core == 0, rest, total)
        return in_f32(jnp.concatenate([first, second], axis=0))

    def column_sharded(left, first, second, pieces):
        cols = first.shape[1] // pieces
        mine_side = jnp.where(core == 0, first, second)
        other_side = jnp.where(core == 0, second, first)
        totals = []
        for i in range(pieces):
            cut = slice(i * cols, (i + 1) * cols)
            keep = trans_times(left, mine_side[:, cut])
            send = trans_times(left, other_side[:, cut], jnp.bfloat16)
            totals.append(line_sum(keep + in_f32(sibling(send))))
        out = []
        for total in totals:
            got = [lax.dynamic_slice_in_dim(total, mine * deep, deep, 0)]
            for s in others:
                got.append(shift(lax.dynamic_slice_in_dim(total, (mine ^ s) * deep, deep, 0), s))
            out.append([(piece, sibling(piece)) for piece in got])
        return out

    def placed(pairs, which, starts, cols_of, cols):
        whole = jnp.zeros((deep, cols), jnp.float32)
        for piece_pairs, start, cut in zip(pairs, starts, cols_of):
            for s, (own, other) in enumerate(piece_pairs):
                chunk = in_f32(jnp.where(core == which, own, other)[:, cut])
                whole = lax.dynamic_update_slice(
                    whole, chunk, (0, (mine ^ s) * (cols // n_fsdp) + start)
                )
        return whole

    grad_branch_all = jnp.concatenate(gather_rows(in_bf16(grad_result)))
    dw_down = row_sharded(hidden_b, grad_branch_all)
    grad_hidden = times_trans(grad_branch_all, w_down)
    grad_gate_pre, grad_up_pre = swiglu_back(grad_hidden)
    grad_gate_b = in_bf16(grad_gate_pre)
    grad_up_b = in_bf16(grad_up_pre)
    grad_mlp_b = jnp.concatenate([grad_gate_b, grad_up_b], axis=1)
    grad_normed_mlp = summed(grad_mlp_b, w_mlp, times_trans)
    mlp_pieces = 2
    mlp_pairs = column_sharded(normed_mlp_all, grad_gate_b, grad_up_b, mlp_pieces)
    starts = [i * (ff // mlp_pieces) for i in range(mlp_pieces)]
    cuts = [slice(None)] * mlp_pieces
    dw_gate = placed(mlp_pairs, 0, starts, cuts, w_gate.shape[1])
    dw_up = placed(mlp_pairs, 1, starts, cuts, w_up.shape[1])
    grad_middle_norm, grad_mlp_gain = mlp_norm_back(grad_normed_mlp)
    grad_middle = grad_result + grad_middle_norm

    grad_attn_all = jnp.concatenate(gather_rows(in_bf16(grad_middle)))
    dw_output = row_sharded(gated_b, grad_attn_all)
    grad_gated = times_trans(grad_attn_all, w_output).reshape(
        n_fsdp, rows, heads_k, H // KV, HD
    )
    grad_context, grad_gate_heads = gating_back(grad_gated)
    grad_context_b = in_bf16(grad_context)
    grad_outgate_b = in_bf16(grad_gate_heads.reshape(rows_all, cols_q))
    scores_again = dots("sqkgd,spkd->skgqp", queries_b, keys_b) * score_scale
    probs_again = jnp.where(allowed, jnp.exp(scores_again - log_total), 0.0)
    grad_value = dots("skgqp,sqkgd->spkd", in_bf16(probs_again), grad_context_b)
    grad_probs = dots("sqkgd,spkd->skgqp", grad_context_b, value_b)
    grad_scores = probs_again * (
        grad_probs - jnp.sum(probs_again * grad_probs, axis=-1, keepdims=True)
    )
    grad_scores_b = in_bf16(grad_scores)
    grad_queries = dots("skgqp,spkd->sqkgd", grad_scores_b, keys_b) * score_scale
    grad_keys = dots("skgqp,sqkgd->spkd", grad_scores_b, queries_b) * score_scale
    grad_query_raw, grad_key_raw, grad_query_gain, grad_key_gain = heads_back(
        (grad_queries.reshape(n_fsdp, rows, heads_q, HD), grad_keys)
    )
    grad_query_b = in_bf16(grad_query_raw)
    grad_key_b = in_bf16(grad_key_raw)
    grad_value_b = in_bf16(grad_value.reshape(rows_all, cols_k))
    first = jnp.concatenate([grad_query_b, grad_key_b], axis=1)
    second = jnp.concatenate([grad_outgate_b, grad_value_b], axis=1)
    attn_pairs = column_sharded(normed_all, first, second, 1)
    query_cut, key_cut = slice(0, cols_q), slice(cols_q, None)
    dw_query = placed(attn_pairs, 0, [0], [query_cut], w_query.shape[1])
    dw_key = placed(attn_pairs, 0, [0], [key_cut], w_key.shape[1])
    dw_outgate = placed(attn_pairs, 1, [0], [query_cut], w_outgate.shape[1])
    dw_value = placed(attn_pairs, 1, [0], [key_cut], w_value.shape[1])
    grad_normed = summed(jnp.concatenate([first, second], axis=1), w_attn, times_trans)
    _, norm_back = jax.vjp(rms_scale, tokens_f, attention_gain_f)
    grad_tokens_norm, grad_attention_gain = norm_back(grad_normed)
    tokens_grad = in_bf16(grad_middle + grad_tokens_norm)

    dgains = lax.psum(
        jnp.concatenate([grad_attention_gain, grad_mlp_gain, grad_query_gain, grad_key_gain]),
        ("rep", "fsdp"),
    )

    def own_part(start, cols):
        return lax.dynamic_slice(dgains, (start + mine * cols,), (cols,))

    return (
        block_out,
        seq_loss,
        tokens_grad,
        own_part(0, deep),
        own_part(2 * width, small),
        own_part(2 * width + HD, small),
        dw_query,
        dw_key,
        dw_value,
        dw_outgate,
        dw_output,
        own_part(width, deep),
        dw_gate,
        dw_up,
        dw_down,
    )


def solution(mesh):
    return jax.shard_map(
        shards,
        mesh=mesh,
        in_specs=(
            P(("rep", "fsdp"), None),
            P(("rep", "fsdp"), None),
            P(),
            P(),
            P("fsdp"),
            P("fsdp"),
            P("fsdp"),
            P("fsdp", None),
            P("fsdp", None),
            P("fsdp", None),
            P("fsdp", None),
            P("fsdp", None),
            P("fsdp"),
            P("fsdp", None),
            P("fsdp", None),
            P("fsdp", None),
        ),
        out_specs=(
            P(("rep", "fsdp"), None),
            P(("rep", "fsdp")),
            P(("rep", "fsdp"), None),
            P("fsdp"),
            P("fsdp"),
            P("fsdp"),
            P("fsdp", None),
            P("fsdp", None),
            P("fsdp", None),
            P("fsdp", None),
            P("fsdp", None),
            P("fsdp"),
            P("fsdp", None),
            P("fsdp", None),
            P("fsdp", None),
        ),
        check_vma=False,
    )
```

time: 4550 us -> 1350 us (0.30)
  waiting for transfers between devices: 4040 us -> 557 us
  blocking collectives: 83.6 us -> 224 us
  starting transfers between devices: 1.58 us -> 111 us
  matrix products: 270 us -> 168 us
  other arithmetic: 30 us -> 128 us
  local copies, waits for them, and re-layouts: 95.3 us -> 151 us
    reduce_scatter x8 -> x0, waiting for transfers between devices: 2640 us -> none  [the longest x1 439 us: shards(): lax.psum_scatter(trans_times(arrange(hidden_b), grad_branch_b), ('rep', '...]
    all_gather x16 -> x0, waiting for transfers between devices: 1390 us -> none  [the longest x1 223 us: shards(): lax.all_gather(w_gate, 'fsdp', axis=0, tiled=True)]
    ppermute x0 -> x106, waiting for transfers between devices: none -> 557 us  [the longest x15 294 us: along_line(): lax.ppermute(values, 'rep', [(2 * a + core, 2 * b + core) for a, b in hop...]
    psum x0 -> x1, blocking collectives: none -> 224 us  [shards(): lax.psum(jnp.concatenate([grad_attention_gain, grad_mlp_gain, grad_query_...]
    ppermute x0 -> x106, starting transfers between devices: none -> 111 us  [the longest x66 73.3 us: shift(): return lax.ppermute(values, 'fsdp', [(i, i ^ step) for i in range(n_fsdp)])]
    unnamed x3 -> x0, blocking collectives: 68.4 us -> none
    dot_general x8 -> x10, matrix products: 100 us -> 50.6 us  [trans_times(): lax.dot_general(left_side, right_side, (((0,), (0,)), ((), ())), preferre...]
    dot_general x14 -> x13, matrix products: 103 us -> 57.9 us  [the longest x7 45.4 us: times(): jnp.dot(left_side, right_side, preferred_element_type=jnp.float32)]
  transfers between devices with their start and end apart: 24 -> 106, of which waited for: 22 -> 44; matrix products, arithmetic and copies ran while one was open for 6% -> 26% of each run, Pallas kernels for 0% -> 0%
where the time goes in v1:
time: 1350 us; the launch traced here: 1340 us
  waiting for transfers between devices  557 us (41%)
  blocking collectives  224 us (17%)
  matrix products  168 us (12%)
  local copies, waits for them, and re-layouts  151 us (11%)
  other arithmetic  128 us (9%)
  starting transfers between devices  111 us (8%)
    ppermute x15, waiting for transfers between devices, along_line(): lax.ppermute(values, 'rep', [(2 * a + core, 2 * b + core) for a, b in hop...  294 us
    ppermute x66, waiting for transfers between devices, shift(): return lax.ppermute(values, 'fsdp', [(i, i ^ step) for i in range(n_fsdp)])  263 us
    psum x1, blocking collectives, shards(): lax.psum(jnp.concatenate([grad_attention_gain, grad_mlp_gain, grad_query_...  224 us
    ppermute x66, starting transfers between devices, shift(): return lax.ppermute(values, 'fsdp', [(i, i ^ step) for i in range(n_fsdp)])  73.3 us
    dot_general x6, matrix products, times_trans(): lax.dot_general(left_side, right_side, (((1,), (1,)), ((), ())), preferre...  59.3 us
    dot_general x10, matrix products, trans_times(): lax.dot_general(left_side, right_side, (((0,), (0,)), ((), ())), preferre...  50.6 us
    dot_general x7, matrix products, times(): jnp.dot(left_side, right_side, preferred_element_type=jnp.float32)  45.4 us
    unnamed x238, local copies, waits for them, and re-layouts  40.3 us
  transfers between devices with their start and end apart: 106, of which 44 were waited for; matrix products, arithmetic and copies ran while one was open for 26% of the time, Pallas kernels for 0%

profile of v1, /device:TPU:0, one launch (start us, length us, event | category | flops | bytes accessed | tf_op | source)
XLA Modules:
  0.0 1342.9 jit_solution(18177016021465984579)
XLA Ops:
  74.8 23.0 %collective-permute-done.4 = bf16[128,2048]{1,0:T(8,128)(2,1)S(1)} collective-permute-done((bf16[128,2048]{1,0:T(8,128)(2,1)}, bf16[128,2048]{1,0:T(8,128)(2,1)S(1)}, u32[]{:S(2)}, u32[]{:S(2)}) %collective-permute-start.4) | collective-permute-done | bytes 524320 | tf_op jit(solution)/shard_map/ppermute | solution.py:79
  108.8 9.0 fusion.119
  192.5 9.9 collective-permute-done.16
  203.4 32.9 %collective-permute-done.19 = bf16[128,2048]{1,0:T(8,128)(2,1)S(1)} collective-permute-done((bf16[128,2048]{1,0:T(8,128)(2,1)S(1)}, bf16[128,2048]{1,0:T(8,128)(2,1)S(1)}, u32[]{:S(2)}, u32[]{:S(2)}) %collective-permute-start.19) | collective-permute-done | bytes 524320 | tf_op jit(solution)/shard_map/ppermute | solution.py:79
  266.8 16.5 %collective-permute-done.21 = bf16[128,2048]{1,0:T(8,128)(2,1)S(1)} collective-permute-done((bf16[128,2048]{1,0:T(8,128)(2,1)S(1)}, bf16[128,2048]{1,0:T(8,128)(2,1)S(1)}, u32[]{:S(2)}, u32[]{:S(2)}) %collective-permute-start.21) | collective-permute-done | bytes 524320 | tf_op jit(solution)/shard_map/ppermute | solution.py:79
  288.6 9.5 collective-permute-done.23
  306.2 8.6 fusion.8
  314.8 12.3 multiply_convert_fusion.1
  380.5 9.6 collective-permute-done.39
  407.3 15.8 %broadcast_select_fusion.4 = (bf16[1024,1536]{1,0:T(8,128)(2,1)}, bf16[1024,1536]{1,0:T(8,128)(2,1)S(1)}, bf16[1024,1536]{1,0:T(8,128)(2,1)S(1)}) fusion(pred[]{:T(512)S(6)} %eq.70, f32[1024,1536]{1,0:T(8,128)} %fusion.8, f32[1024,1536]{1,0:T(8,128)} %get-tuple-element.175, bf16[1024,2048]{1,0:T(8,128)(2,1)} %copy-done.37, bf16[1536,2048]{1,0:T(8,128)(2,1)} %param.31), kind=kOutput, calls=%fused_computation.75 | convolution fusion | flops 6466043904 | bytes 32505856 | tf_op jit(solution)/shard_map/dot_general | solution.py:50
  423.1 16.3 %fusion.19 = bf16[768,2048]{1,0:T(8,128)(2,1)} fusion(bf16[2048,3072]{1,0:T(8,128)(2,1)} %copy-done.5, bf16[1024,1536]{1,0:T(8,128)(2,1)S(1)} %get-tuple-element.27, bf16[1024,1536]{1,0:T(8,128)(2,1)S(1)} %get-tuple-element.26), kind=kOutput, calls=%fused_computation.51 | convolution fusion | flops 9674686464 | bytes 22020096 | tf_op jit(solution)/shard_map/dot_general | solution.py:50
  472.4 9.6 multiply_reduce_fusion.1
  576.6 8.5 convolution_convert_fusion.5
  648.6 224.4 %psum.7 = f32[4352]{0:T(1024)S(1)} all-reduce(f32[4352]{0:T(1024)S(1)} %pad_maximum_fusion.6), channel_id=1, replica_groups=mesh['rep'=8,'fsdp'=4] {'rep','fsdp'}, use_global_device_ids=true, to_apply=%region_21.22 | all-reduce | flops 4352 | bytes 34816 | tf_op jit(solution)/shard_map/psum | solution.py:388
  904.8 47.2 %collective-permute-done.64 = bf16[2048,768]{1,0:T(8,128)(2,1)S(1)} collective-permute-done((bf16[2048,768]{1,0:T(8,128)(2,1)S(1)}, bf16[2048,768]{1,0:T(8,128)(2,1)S(1)}, u32[]{:S(2)}, u32[]{:S(2)}) %collective-permute-start.64) | collective-permute-done | bytes 3145760 | tf_op jit(solution)/shard_map/ppermute | solution.py:88
  956.1 53.5 %collective-permute-done.77 = bf16[256,2048]{1,0:T(8,128)(2,1)S(1)} collective-permute-done((bf16[256,2048]{1,0:T(8,128)(2,1)S(1)}, bf16[256,2048]{1,0:T(8,128)(2,1)S(1)}, u32[]{:S(2)}, u32[]{:S(2)}) %collective-permute-start.77) | collective-permute-done | bytes 1048608 | tf_op jit(solution)/shard_map/ppermute | solution.py:88
  1022.4 54.7 %collective-permute-done.82 = bf16[2048,768]{1,0:T(8,128)(2,1)} collective-permute-done((bf16[2048,768]{1,0:T(8,128)(2,1)S(1)}, bf16[2048,768]{1,0:T(8,128)(2,1)}, u32[]{:S(2)}, u32[]{:S(2)}) %collective-permute-start.82) | collective-permute-done | bytes 3145760 | tf_op jit(solution)/shard_map/ppermute | solution.py:88
  1083.1 61.3 %collective-permute-done.93 = bf16[2048,768]{1,0:T(8,128)(2,1)S(1)} collective-permute-done((bf16[2048,768]{1,0:T(8,128)(2,1)S(1)}, bf16[2048,768]{1,0:T(8,128)(2,1)S(1)}, u32[]{:S(2)}, u32[]{:S(2)}) %collective-permute-start.93) | collective-permute-done | bytes 3145760 | tf_op jit(solution)/shard_map/ppermute | solution.py:88
  1147.5 64.2 %collective-permute-done.104 = bf16[768,2048]{1,0:T(8,128)(2,1)S(1)} collective-permute-done((bf16[768,2048]{1,0:T(8,128)(2,1)S(1)}, bf16[768,2048]{1,0:T(8,128)(2,1)S(1)}, u32[]{:S(2)}, u32[]{:S(2)}) %collective-permute-start.104) | collective-permute-done | bytes 3145760 | tf_op jit(solution)/shard_map/ppermute | solution.py:88
  1230.2 11.3 collective-permute-done.95
  1241.5 18.0 %collective-permute-done.97 = bf16[512,768]{1,0:T(8,128)(2,1)S(1)} collective-permute-done((bf16[512,768]{1,0:T(8,128)(2,1)S(1)}, bf16[512,768]{1,0:T(8,128)(2,1)S(1)}, u32[]{:S(2)}, u32[]{:S(2)}) %collective-permute-start.97) | collective-permute-done | bytes 786464 | tf_op jit(solution)/shard_map/ppermute | solution.py:79
  1261.6 13.2 collective-permute-done.66
  1285.7 12.1 collective-permute-done.68
  1297.9 17.5 %collective-permute-done.70 = bf16[512,768]{1,0:T(8,128)(2,1)} collective-permute-done((bf16[512,768]{1,0:T(8,128)(2,1)S(1)}, bf16[512,768]{1,0:T(8,128)(2,1)}, u32[]{:S(2)}, u32[]{:S(2)}) %collective-permute-start.70) | collective-permute-done | bytes 786464 | tf_op jit(solution)/shard_map/ppermute | solution.py:79
  (663 shorter events, 580.1 us)
Async XLA Ops:
  72.2 174.1 %collective-permute-start.27 = (bf16[256,3072]{1,0:T(8,128)(2,1)}, bf16[256,3072]{1,0:T(8,128)(2,1)}, u32[]{:S(2)}, u32[]{:S(2)}) collective-permute-start(bf16[256,3072]{1,0:T(8,128)(2,1)} %fusion.51), channel_id=1, source_target_pairs={{0,1},{1,0},{2,3},{3,2},{4,5},{5,4},{6,7},{7,6},{8,9},{9,8},{10,11... | collective-permute-start | bytes 4718600 | tf_op jit(solution)/shard_map/ppermute | solution.py:79
  97.8 150.6 %collective-permute-start.29 = (bf16[256,3072]{1,0:T(8,128)(2,1)}, bf16[256,3072]{1,0:T(8,128)(2,1)}, u32[]{:S(2)}, u32[]{:S(2)}) collective-permute-start(bf16[256,3072]{1,0:T(8,128)(2,1)} %fusion.50), channel_id=1, source_target_pairs={{0,2},{1,3},{2,0},{3,1},{4,6},{5,7},{6,4},{7,5},{8,10},{9,11},{10,... | collective-permute-start | bytes 4718600 | tf_op jit(solution)/shard_map/ppermute | solution.py:79
  465.1 135.7 %collective-permute-start.79 = (bf16[2048,768]{1,0:T(8,128)(2,1)}, bf16[2048,768]{1,0:T(8,128)(2,1)}, u32[]{:S(2)}, u32[]{:S(2)}) collective-permute-start(bf16[2048,768]{1,0:T(8,128)(2,1)} %convolution_convert_fusion.3), channel_id=1, source_target_pairs={{0,4},{4,0},{8,12},{12,8},{16,20},{20,16},{24,28},{28,24},{1,5},{5... | collective-permute-start | bytes 9437192 | tf_op jit(solution)/shard_map/ppermute | solution.py:84
  501.3 106.0 %collective-permute-start.90 = (bf16[2048,768]{1,0:T(8,128)(2,1)}, bf16[2048,768]{1,0:T(8,128)(2,1)}, u32[]{:S(2)}, u32[]{:S(2)}) collective-permute-start(bf16[2048,768]{1,0:T(8,128)(2,1)} %convolution_convert_fusion.2), channel_id=1, source_target_pairs={{0,4},{4,0},{8,12},{12,8},{16,20},{20,16},{24,28},{28,24},{1,5},{5... | collective-permute-start | bytes 9437192 | tf_op jit(solution)/shard_map/ppermute | solution.py:84
  508.2 106.3 %collective-permute-start.101 = (bf16[768,2048]{1,0:T(8,128)(2,1)}, bf16[768,2048]{1,0:T(8,128)(2,1)}, u32[]{:S(2)}, u32[]{:S(2)}) collective-permute-start(bf16[768,2048]{1,0:T(8,128)(2,1)} %convolution_convert_fusion.1), channel_id=1, source_target_pairs={{0,4},{4,0},{8,12},{12,8},{16,20},{20,16},{24,28},{28,24},{1,5},{5... | collective-permute-start | bytes 9437192 | tf_op jit(solution)/shard_map/ppermute | solution.py:84
  600.8 272.3 %collective-permute-start.63 = (bf16[2048,768]{1,0:T(8,128)(2,1)}, bf16[2048,768]{1,0:T(8,128)(2,1)}, u32[]{:S(2)}, u32[]{:S(2)}) collective-permute-start(bf16[2048,768]{1,0:T(8,128)(2,1)} %convolution_convert_fusion.4), channel_id=1, source_target_pairs={{0,4},{4,0},{8,12},{12,8},{16,20},{20,16},{24,28},{28,24},{1,5},{5... | collective-permute-start | bytes 9437192 | tf_op jit(solution)/shard_map/ppermute | solution.py:84
  624.6 265.4 %collective-permute-start.75 = (bf16[256,2048]{1,0:T(8,128)(2,1)S(1)}, bf16[256,2048]{1,0:T(8,128)(2,1)S(1)}, u32[]{:S(2)}, u32[]{:S(2)}) collective-permute-start(bf16[256,2048]{1,0:T(8,128)(2,1)S(1)} %fusion.21), channel_id=1, source_target_pairs={{0,8},{4,12},{24,16},{28,20},{1,9},{5,13},{25,17},{29,21},{2,10},{... | collective-permute-start | bytes 3145736 | tf_op jit(solution)/shard_map/ppermute | solution.py:88
  628.5 257.1 %collective-permute-start.80 = (bf16[2048,768]{1,0:T(8,128)(2,1)}, bf16[2048,768]{1,0:T(8,128)(2,1)}, u32[]{:S(2)}, u32[]{:S(2)}) collective-permute-start(bf16[2048,768]{1,0:T(8,128)(2,1)} %add_convert_fusion.8), channel_id=1, source_target_pairs={{0,8},{4,12},{24,16},{28,20},{1,9},{5,13},{25,17},{29,21},{2,10},{... | collective-permute-start | bytes 9437192 | tf_op jit(solution)/shard_map/ppermute | solution.py:88
  634.8 256.4 %collective-permute-start.91 = (bf16[2048,768]{1,0:T(8,128)(2,1)}, bf16[2048,768]{1,0:T(8,128)(2,1)}, u32[]{:S(2)}, u32[]{:S(2)}) collective-permute-start(bf16[2048,768]{1,0:T(8,128)(2,1)} %add_convert_fusion.5), channel_id=1, source_target_pairs={{0,8},{4,12},{24,16},{28,20},{1,9},{5,13},{25,17},{29,21},{2,10},{... | collective-permute-start | bytes 9437192 | tf_op jit(solution)/shard_map/ppermute | solution.py:88
  637.8 258.1 %collective-permute-start.102 = (bf16[768,2048]{1,0:T(8,128)(2,1)}, bf16[768,2048]{1,0:T(8,128)(2,1)}, u32[]{:S(2)}, u32[]{:S(2)}) collective-permute-start(bf16[768,2048]{1,0:T(8,128)(2,1)} %add_convert_fusion.2), channel_id=1, source_target_pairs={{0,8},{4,12},{24,16},{28,20},{1,9},{5,13},{25,17},{29,21},{2,10},{... | collective-permute-start | bytes 9437192 | tf_op jit(solution)/shard_map/ppermute | solution.py:88
  880.6 71.4 %collective-permute-start.64 = (bf16[2048,768]{1,0:T(8,128)(2,1)S(1)}, bf16[2048,768]{1,0:T(8,128)(2,1)S(1)}, u32[]{:S(2)}, u32[]{:S(2)}) collective-permute-start(bf16[2048,768]{1,0:T(8,128)(2,1)S(1)} %add_convert_fusion.11), channel_id=1, source_target_pairs={{0,8},{4,12},{24,16},{28,20},{1,9},{5,13},{25,17},{29,21},{2,10},{... | collective-permute-start | bytes 9437192 | tf_op jit(solution)/shard_map/ppermute | solution.py:88
  889.2 64.6 %collective-permute-start.81 = (bf16[2048,768]{1,0:T(8,128)(2,1)S(1)}, bf16[2048,768]{1,0:T(8,128)(2,1)S(1)}, u32[]{:S(2)}, u32[]{:S(2)}) collective-permute-start(bf16[2048,768]{1,0:T(8,128)(2,1)S(1)} %add_convert_fusion.7), channel_id=1, source_target_pairs={{8,16},{12,20},{16,8},{20,12},{9,17},{13,21},{17,9},{21,13},{10,18... | collective-permute-start | bytes 9437192 | tf_op jit(solution)/shard_map/ppermute | solution.py:88
  894.9 114.9 %collective-permute-start.92 = (bf16[2048,768]{1,0:T(8,128)(2,1)S(1)}, bf16[2048,768]{1,0:T(8,128)(2,1)S(1)}, u32[]{:S(2)}, u32[]{:S(2)}) collective-permute-start(bf16[2048,768]{1,0:T(8,128)(2,1)S(1)} %add_convert_fusion.4), channel_id=1, source_target_pairs={{8,16},{12,20},{16,8},{20,12},{9,17},{13,21},{17,9},{21,13},{10,18... | collective-permute-start | bytes 9437192 | tf_op jit(solution)/shard_map/ppermute | solution.py:88
  900.1 111.9 %collective-permute-start.103 = (bf16[768,2048]{1,0:T(8,128)(2,1)S(1)}, bf16[768,2048]{1,0:T(8,128)(2,1)}, u32[]{:S(2)}, u32[]{:S(2)}) collective-permute-start(bf16[768,2048]{1,0:T(8,128)(2,1)S(1)} %add_convert_fusion.1), channel_id=1, source_target_pairs={{8,16},{12,20},{16,8},{20,12},{9,17},{13,21},{17,9},{21,13},{10,18... | collective-permute-start | bytes 9437192 | tf_op jit(solution)/shard_map/ppermute | solution.py:88
  903.5 106.0 %collective-permute-start.77 = (bf16[256,2048]{1,0:T(8,128)(2,1)S(1)}, bf16[256,2048]{1,0:T(8,128)(2,1)S(1)}, u32[]{:S(2)}, u32[]{:S(2)}) collective-permute-start(bf16[256,2048]{1,0:T(8,128)(2,1)S(1)} %add_convert_fusion.12), channel_id=1, source_target_pairs={{8,0},{12,4},{16,24},{20,28},{9,1},{13,5},{17,25},{21,29},{10,2},{... | collective-permute-start | bytes 3145736 | tf_op jit(solution)/shard_map/ppermute | solution.py:88
  952.9 67.0 %collective-permute-start.65 = (bf16[2048,768]{1,0:T(8,128)(2,1)S(1)}, bf16[2048,768]{1,0:T(8,128)(2,1)S(1)}, u32[]{:S(2)}, u32[]{:S(2)}) collective-permute-start(bf16[2048,768]{1,0:T(8,128)(2,1)S(1)} %add_convert_fusion.10), channel_id=1, source_target_pairs={{8,16},{12,20},{16,8},{20,12},{9,17},{13,21},{17,9},{21,13},{10,18... | collective-permute-start | bytes 9437192 | tf_op jit(solution)/shard_map/ppermute | solution.py:88
  954.8 122.3 %collective-permute-start.82 = (bf16[2048,768]{1,0:T(8,128)(2,1)S(1)}, bf16[2048,768]{1,0:T(8,128)(2,1)}, u32[]{:S(2)}, u32[]{:S(2)}) collective-permute-start(bf16[2048,768]{1,0:T(8,128)(2,1)S(1)} %add_convert_fusion.6), channel_id=1, source_target_pairs={{8,0},{12,4},{16,24},{20,28},{9,1},{13,5},{17,25},{21,29},{10,2},{... | collective-permute-start | bytes 9437192 | tf_op jit(solution)/shard_map/ppermute | solution.py:88
  1010.7 133.6 %collective-permute-start.93 = (bf16[2048,768]{1,0:T(8,128)(2,1)S(1)}, bf16[2048,768]{1,0:T(8,128)(2,1)S(1)}, u32[]{:S(2)}, u32[]{:S(2)}) collective-permute-start(bf16[2048,768]{1,0:T(8,128)(2,1)S(1)} %add_convert_fusion.3), channel_id=1, source_target_pairs={{8,0},{12,4},{16,24},{20,28},{9,1},{13,5},{17,25},{21,29},{10,2},{... | collective-permute-start | bytes 9437192 | tf_op jit(solution)/shard_map/ppermute | solution.py:88
  1015.3 196.5 %collective-permute-start.104 = (bf16[768,2048]{1,0:T(8,128)(2,1)S(1)}, bf16[768,2048]{1,0:T(8,128)(2,1)S(1)}, u32[]{:S(2)}, u32[]{:S(2)}) collective-permute-start(bf16[768,2048]{1,0:T(8,128)(2,1)S(1)} %add_convert_fusion), channel_id=1, source_target_pairs={{8,0},{12,4},{16,24},{20,28},{9,1},{13,5},{17,25},{21,29},{10,2},{... | collective-permute-start | bytes 9437192 | tf_op jit(solution)/shard_map/ppermute | solution.py:88
  1020.9 253.9 %collective-permute-start.66 = (bf16[2048,768]{1,0:T(8,128)(2,1)S(1)}, bf16[2048,768]{1,0:T(8,128)(2,1)}, u32[]{:S(2)}, u32[]{:S(2)}) collective-permute-start(bf16[2048,768]{1,0:T(8,128)(2,1)S(1)} %add_convert_fusion.9), channel_id=1, source_target_pairs={{8,0},{12,4},{16,24},{20,28},{9,1},{13,5},{17,25},{21,29},{10,2},{... | collective-permute-start | bytes 9437192 | tf_op jit(solution)/shard_map/ppermute | solution.py:88
  1079.6 134.2 %collective-permute-start.84 = (bf16[512,768]{1,0:T(8,128)(2,1)S(1)}, bf16[512,768]{1,0:T(8,128)(2,1)S(1)}, u32[]{:S(2)}, u32[]{:S(2)}) collective-permute-start(bf16[512,768]{1,0:T(8,128)(2,1)S(1)} %get-tuple-element.57), channel_id=1, source_target_pairs={{0,1},{1,0},{2,3},{3,2},{4,5},{5,4},{6,7},{7,6},{8,9},{9,8},{10,11... | collective-permute-start | bytes 2359304 | tf_op jit(solution)/shard_map/ppermute | solution.py:79
  1081.9 132.4 %collective-permute-start.86 = (bf16[512,768]{1,0:T(8,128)(2,1)S(1)}, bf16[512,768]{1,0:T(8,128)(2,1)}, u32[]{:S(2)}, u32[]{:S(2)}) collective-permute-start(bf16[512,768]{1,0:T(8,128)(2,1)S(1)} %get-tuple-element.56), channel_id=1, source_target_pairs={{0,2},{1,3},{2,0},{3,1},{4,6},{5,7},{6,4},{7,5},{8,10},{9,11},{10,... | collective-permute-start | bytes 2359304 | tf_op jit(solution)/shard_map/ppermute | solution.py:79
  1144.4 70.0 %collective-permute-start.88 = (bf16[512,768]{1,0:T(8,128)(2,1)S(1)}, bf16[512,768]{1,0:T(8,128)(2,1)}, u32[]{:S(2)}, u32[]{:S(2)}) collective-permute-start(bf16[512,768]{1,0:T(8,128)(2,1)S(1)} %get-tuple-element.55), channel_id=1, source_target_pairs={{0,3},{1,2},{2,1},{3,0},{4,7},{5,6},{6,5},{7,4},{8,11},{9,10},{10,... | collective-permute-start | bytes 2359304 | tf_op jit(solution)/shard_map/ppermute | solution.py:79
  1230.1 91.7 %collective-permute-start.105 = (bf16[768,2048]{1,0:T(8,128)(2,1)}, bf16[768,2048]{1,0:T(8,128)(2,1)}, u32[]{:S(2)}, u32[]{:S(2)}) collective-permute-start(bf16[768,2048]{1,0:T(8,128)(2,1)} %broadcast_select_fusion), channel_id=1, source_target_pairs={{0,4},{4,0},{8,12},{12,8},{16,20},{20,16},{24,28},{28,24},{1,5},{5... | collective-permute-start | bytes 9437192 | tf_op jit(solution)/shard_map/ppermute | solution.py:84
  (188 other events, 3241.9 us)

commit v2 on v1

--- a/solution.py
+++ b/solution.py
@@ -1,7 +1,13 @@
+import functools
+
 import jax
 import jax.numpy as jnp
 from jax import lax
+from jax.experimental import pallas as pl
+from jax.experimental.pallas import tpu as pltpu
 from jax.sharding import PartitionSpec as P
+
+MESH = pl.DeviceIdType.MESH
 
 H = 16
 KV = 8
@@ -84,28 +90,387 @@
     return lax.ppermute(values, "rep", [(i, i ^ 1) for i in range(n_rep)])
 
 
-def along_line(values, hops):
-    return lax.ppermute(
-        values, "rep", [(2 * a + core, 2 * b + core) for a, b in hops for core in range(2)]
-    )
-
-
-def line_sum(values):
-    n_line = lax.axis_size("rep") // 2
-    place = lax.axis_index("rep") // 2
-    if n_line == 1:
-        return in_bf16(values)
+def sum_everywhere(values):
+    for axis in ("fsdp", "rep"):
+        n = lax.axis_size(axis)
+        step = 1
+        while step < n:
+            values = values + lax.ppermute(values, axis, [(i, i ^ step) for i in range(n)])
+            step *= 2
+    return values
+
+
+def flipped(index, step, n):
+    out, bit = index, 1
+    while bit < n:
+        has = (step // bit) % 2
+        out = out + has * bit * (1 - 2 * ((index // bit) % 2))
+        bit *= 2
+    return out
+
+
+def at_least(value, bound, span):
+    span = max(span, bound)
+    return (value + (span - bound)) // span
+
+
+class Unit:
+    def __init__(self, base, by_owner, row_blocks, col_blocks):
+        self.base, self.by_owner = base, by_owner
+        self.row_blocks, self.col_blocks = row_blocks, col_blocks
+        self.count = row_blocks * col_blocks
+
+
+LAG_B, LAG_C, LAG_D, LAG_E, LAG_G = 2, 4, 6, 8, 11
+RING = 4
+
+
+def reduce_kernel(
+    n_fsdp, n_rep, units, piece_rows, piece_cols, *refs
+):
+    lefts, rights = refs[: len(units)], refs[len(units) : 2 * len(units)]
+    out = refs[2 * len(units)]
+    (lm, lo, rh, sb, kb, r1, inb, xb) = refs[2 * len(units) + 1 : 2 * len(units) + 9]
+    (tile_sem, r1s, r1r, ins, inr, xs, xr, os_, fs, fr, gs, gr, ls) = refs[2 * len(units) + 9 :]
+    total = sum(unit.count for unit in units)
+    rep, mine = lax.axis_index("rep"), lax.axis_index("fsdp")
+    core, place = rep % 2, rep // 2
+    n_line = n_rep // 2
     half = n_line // 2
-    total = in_bf16(values)
-    for k in range(half - 1):
-        got = along_line(total, [(k, k + 1), (n_line - 1 - k, n_line - 2 - k)])
-        total = in_bf16(in_f32(total) + in_f32(got))
-    got = along_line(total, [(half - 1, half), (half, half - 1)])
-    total = in_bf16(in_f32(total) + in_f32(got))
-    for k in range(half - 1, 0, -1):
-        got = along_line(total, [(k, k - 1), (n_line - 1 - k, n_line - k)])
-        total = jnp.where((place == k - 1) | (place == n_line - k), got, total)
-    return total
+    side = place // half
+    depth = place * (1 - side) + (n_line - 1 - place) * side
+    inward = (place + 1 - 2 * side) * 2 + core
+    outward = (place - 1 + 2 * side) * 2 + core
+    sib = rep + 1 - 2 * core
+    middle = depth == half - 1
+
+    barrier = pltpu.get_barrier_semaphore()
+
+    def greet(device):
+        pl.semaphore_signal(barrier, inc=1, device_id=device, device_id_type=MESH)
+
+    greet({"rep": sib, "fsdp": mine})
+    greet({"rep": inward, "fsdp": mine})
+    for s in range(1, n_fsdp):
+        greet({"rep": rep, "fsdp": flipped(mine, s, n_fsdp)})
+
+    @pl.when(depth == 0)
+    def _():
+        pl.semaphore_wait(barrier, 1 + n_fsdp)
+
+    @pl.when(depth > 0)
+    def _():
+        greet({"rep": outward, "fsdp": mine})
+        pl.semaphore_wait(barrier, 2 + n_fsdp)
+
+    def remote(src, dst, send, recv, to_rep, to_fsdp):
+        return pltpu.make_async_remote_copy(
+            src_ref=src,
+            dst_ref=dst,
+            send_sem=send,
+            recv_sem=recv,
+            device_id={"rep": to_rep, "fsdp": to_fsdp},
+            device_id_type=MESH,
+        )
+
+    def r1_copy(p):
+        return remote(sb.at[p % RING], r1.at[p], r1s.at[p], r1r.at[p], sib, mine)
+
+    def in_copy(p):
+        return remote(r1.at[p], inb.at[p], ins.at[p], inr.at[p], inward, mine)
+
+    def x_copy(p):
+        return remote(r1.at[p], xb.at[p], xs.at[p], xr.at[p], inward, mine)
+
+    def o_copy(p, src):
+        return remote(src.at[p], xb.at[p], os_.at[p], xr.at[p], outward, mine)
+
+    def owner_of(p):
+        step, place_at, keep = 0, p, 1
+        for u, unit in enumerate(units):
+            if unit.by_owner:
+                inside = at_least(p, unit.base, total - unit.base)
+                if unit.base + unit.count < total:
+                    stop = unit.base + unit.count
+                    inside = inside * (1 - at_least(p, stop, total - stop))
+                i = p - unit.base
+                step = step + inside * (n_fsdp - 1 - i // unit.col_blocks)
+        return step
+
+    def spot(p, source):
+        where = p
+        for unit in units:
+            if unit.by_owner:
+                inside = at_least(p, unit.base, total - unit.base)
+                if unit.base + unit.count < total:
+                    stop = unit.base + unit.count
+                    inside = inside * (1 - at_least(p, stop, total - stop))
+                i = p - unit.base
+                spread = unit.base + source * unit.col_blocks + i % unit.col_blocks
+                where = where + inside * (spread - p)
+        return where
+
+    def f_copy(p, step):
+        return remote(
+            r1.at[p],
+            out.at[spot(p, mine), core],
+            fs.at[p],
+            fr.at[p],
+            rep,
+            flipped(mine, step, n_fsdp),
+        )
+
+    def g_copy(p, src, where):
+        return remote(src, out.at[where, core], gs.at[p], gr.at[p], sib, mine)
+
+    def l_copy(p):
+        return pltpu.make_async_copy(r1.at[p], out.at[spot(p, mine), core], ls.at[p])
+
+    def add_into(p, other):
+        r1[p] = (r1[p].astype(jnp.float32) + other.astype(jnp.float32)).astype(jnp.bfloat16)
+
+    def stage_b(p):
+        r1_copy(p).wait_recv()
+        add_into(p, kb[p % RING])
+        if half > 1:
+
+            @pl.when(depth == 0)
+            def _():
+                in_copy(p).start()
+        else:
+            x_copy(p).start()
+
+    def stage_c(p):
+        @pl.when(depth > 0)
+        def _():
+            in_copy(p).wait_recv()
+            add_into(p, inb[p])
+
+            @pl.when(depth < half - 1)
+            def _():
+                in_copy(p).start()
+
+            @pl.when(middle)
+            def _():
+                x_copy(p).start()
+
+    def stage_d(p):
+        @pl.when(middle)
+        def _():
+            x_copy(p).wait()
+            add_into(p, xb[p])
+
+            @pl.when(depth > 0)
+            def _():
+                o_copy(p, r1).start()
+
+    def stage_e(p):
+        @pl.when(depth < half - 1)
+        def _():
+            o_copy(p, xb).wait_recv()
+
+            @pl.when(depth > 0)
+            def _():
+                o_copy(p, xb).start()
+
+            in_copy(p).wait_send()
+            r1[p] = xb[p]
+
+        step = owner_of(p)
+
+        @pl.when(step == 0)
+        def _():
+            l_copy(p).start()
+            g_copy(p, r1.at[p], spot(p, mine)).start()
+
+        @pl.when(step > 0)
+        def _():
+            f_copy(p, step).start()
+
+    def stage_g(p):
+        step = owner_of(p)
+
+        @pl.when(step > 0)
+        def _():
+            f_copy(p, step).wait_recv()
+            where = spot(p, flipped(mine, step, n_fsdp))
+            g_copy(p, out.at[where, core], where).start()
+
+    stages = [(LAG_B, stage_b), (LAG_C, stage_c), (LAG_D, stage_d), (LAG_E, stage_e), (LAG_G, stage_g)]
+
+    def service(t):
+        for lag, stage in stages:
+            pl.when((t >= lag) & (t < total + lag))(functools.partial(stage, t - lag))
+
+    def tiles(u, i, slot):
+        unit = units[u]
+        r, j = i // unit.col_blocks, i % unit.col_blocks
+        if unit.by_owner:
+            owner = flipped(mine, n_fsdp - 1 - r, n_fsdp)
+            first = owner * 2 * piece_rows + core * piece_rows
+            second = owner * 2 * piece_rows + (1 - core) * piece_rows
+        else:
+            first = core * unit.row_blocks * piece_rows + r * piece_rows
+            second = (1 - core) * unit.row_blocks * piece_rows + r * piece_rows
+        first = pl.multiple_of(first, piece_rows)
+        second = pl.multiple_of(second, piece_rows)
+        cols = pl.multiple_of(j * piece_cols, piece_cols)
+        return [
+            pltpu.make_async_copy(
+                lefts[u].at[:, pl.ds(first, piece_rows)], lm.at[slot], tile_sem.at[slot, 0]
+            ),
+            pltpu.make_async_copy(
+                lefts[u].at[:, pl.ds(second, piece_rows)], lo.at[slot], tile_sem.at[slot, 1]
+            ),
+            pltpu.make_async_copy(
+                rights[u].at[:, pl.ds(cols, piece_cols)], rh.at[slot], tile_sem.at[slot, 2]
+            ),
+        ]
+
+    def product(left, right):
+        return lax.dot_general(
+            left, right, (((0,), (0,)), ((), ())), preferred_element_type=jnp.float32
+        )
+
+    for copy in tiles(0, 0, 0):
+        copy.start()
+    for u, unit in enumerate(units):
+
+        def step(i, carry, u=u, unit=unit):
+            t = unit.base + i
+            slot = t % 2
+            for copy in tiles(u, i, slot):
+                copy.wait()
+
+            @pl.when(i + 1 < unit.count)
+            def _():
+                for copy in tiles(u, i + 1, 1 - slot):
+                    copy.start()
+
+            if u + 1 < len(units):
+
+                @pl.when(i + 1 == unit.count)
+                def _():
+                    for copy in tiles(u + 1, 0, 1 - slot):
+                        copy.start()
+
+            @pl.when(t >= RING)
+            def _():
+                r1_copy(t - RING).wait_send()
+
+            sb[t % RING] = product(lo[slot], rh[slot]).astype(jnp.bfloat16)
+            r1_copy(t).start()
+            kb[t % RING] = product(lm[slot], rh[slot])
+            service(t)
+            return carry
+
+        lax.fori_loop(0, unit.count, step, 0)
+
+    def drain(t, carry):
+        service(t)
+        return carry
+
+    lax.fori_loop(total, total + LAG_G, drain, 0)
+
+    def finish(p, carry):
+        @pl.when(p >= total - RING)
+        def _():
+            r1_copy(p).wait_send()
+
+        @pl.when(depth > 0)
+        def _():
+            o_copy(p, r1).wait_send()
+
+        step = owner_of(p)
+
+        @pl.when(step == 0)
+        def _():
+            l_copy(p).wait()
+
+        @pl.when(step > 0)
+        def _():
+            f_copy(p, step).wait_send()
+
+        g_copy(p, r1.at[p], p).wait()
+        return carry
+
+    lax.fori_loop(0, total, finish, 0)
+
+
+def reduced(n_fsdp, n_rep, units, piece_rows, piece_cols, lefts, rights):
+    total = sum(unit.count for unit in units)
+    rows = lefts[0].shape[0]
+    half = n_rep // 4
+    dma = pltpu.SemaphoreType.DMA
+    piece = (piece_rows, piece_cols)
+    any_spec = pl.BlockSpec(memory_space=pl.ANY)
+    flops = sum(4 * unit.count for unit in units) * rows * piece_rows * piece_cols
+    return pl.pallas_call(
+        functools.partial(reduce_kernel, n_fsdp, n_rep, units, piece_rows, piece_cols),
+        out_shape=jax.ShapeDtypeStruct((total, 2) + piece, jnp.bfloat16),
+        in_specs=[any_spec] * (2 * len(units)),
+        out_specs=any_spec,
+        scratch_shapes=[
+            pltpu.VMEM((2, rows, piece_rows), jnp.bfloat16),
+            pltpu.VMEM((2, rows, piece_rows), jnp.bfloat16),
+            pltpu.VMEM((2, rows, piece_cols), jnp.bfloat16),
+            pltpu.VMEM((RING,) + piece, jnp.bfloat16),
+            pltpu.VMEM((RING,) + piece, jnp.float32),
+            pltpu.VMEM((total,) + piece, jnp.bfloat16),
+            pltpu.VMEM((total,) + piece, jnp.bfloat16),
+            pltpu.VMEM((total,) + piece, jnp.bfloat16),
+            dma((2, 3)),
+        ]
+        + [dma((total,)) for _ in range(12)],
+        compiler_params=pltpu.CompilerParams(
+            collective_id=0, has_side_effects=True, vmem_limit_bytes=60 << 20
+        ),
+        cost_estimate=pl.CostEstimate(flops=flops, bytes_accessed=1 << 30, transcendentals=0),
+        name="reduce_weight_gradients",
+    )(*lefts, *rights)
+
+
+def widen_kernel(in_ref, out_ref):
+    cols = in_ref.shape[-1]
+    for i in range(in_ref.shape[0]):
+        out_ref[:, i * cols : (i + 1) * cols] = in_ref[i, 0].astype(jnp.float32)
+
+
+def widened(pieces, grid, together, where, shape, place):
+    rows, cols = pieces.shape[2:]
+    return pl.pallas_call(
+        widen_kernel,
+        grid=grid,
+        out_shape=jax.ShapeDtypeStruct(shape, jnp.float32),
+        in_specs=[pl.BlockSpec((together, 1, rows, cols), where)],
+        out_specs=pl.BlockSpec((rows, together * cols), place),
+        name="widen",
+    )(pieces)
+
+
+def widen_heads_kernel(query_in, gate_in, pair_in, query_out, gate_out, key_out, value_out):
+    half = key_out.shape[1]
+    query_out[...] = query_in[0, 0].astype(jnp.float32)
+    gate_out[...] = gate_in[0, 0].astype(jnp.float32)
+    key_out[...] = pair_in[0, 0, :, :half].astype(jnp.float32)
+    value_out[...] = pair_in[0, 0, :, half:].astype(jnp.float32)
+
+
+def widened_heads(pieces, base, n_fsdp, shapes):
+    rows, cols = pieces.shape[2:]
+
+    def where(j):
+        return lambda c, f: (base + 3 * f + j, c, 0, 0)
+
+    widths = (cols, cols, cols // 2, cols // 2)
+    return pl.pallas_call(
+        widen_heads_kernel,
+        grid=(2, n_fsdp),
+        out_shape=[jax.ShapeDtypeStruct(shape, jnp.float32) for shape in shapes],
+        in_specs=[pl.BlockSpec((1, 1, rows, cols), where(j)) for j in range(3)],
+        out_specs=[pl.BlockSpec((rows, wide), lambda c, f: (c, f)) for wide in widths],
+        name="widen_heads",
+    )(pieces, pieces, pieces)
 
 
 def gather_rows(block):
@@ -233,15 +598,15 @@
     key_gain_f = gains[:, 2 * deep + small :].reshape(-1)
 
     tokens_all = jnp.concatenate(gather_rows(tokens))
-    w_attn = by_columns((w_query, w_key, w_outgate, w_value), (cols_q, cols_k, cols_q, cols_k))
+    w_attn = by_columns((w_query, w_outgate, w_key, w_value), (cols_q, cols_q, cols_k, cols_k))
     w_mlp = by_columns((w_gate, w_up), (ff, ff))
 
     tokens_f = in_f32(tokens)
     normed_all = in_bf16(rms_scale(in_f32(tokens_all), attention_gain_f))
     attn_raw = times(normed_all, w_attn)
     query_raw = attn_raw[:, :cols_q]
-    key_raw = attn_raw[:, cols_q : cols_q + cols_k]
-    gate_raw = attn_raw[:, cols_q + cols_k : 2 * cols_q + cols_k]
+    gate_raw = attn_raw[:, cols_q : 2 * cols_q]
+    key_raw = attn_raw[:, 2 * cols_q : 2 * cols_q + cols_k]
     value_b = in_bf16(attn_raw[:, 2 * cols_q + cols_k :]).reshape(n_fsdp, rows, heads_k, HD)
 
     def prepare_heads(query_in, key_in, query_scale, key_scale):
@@ -291,65 +656,17 @@
     block_out = in_bf16(result * valid_row[:, None])
     grad_result = 2.0 * factor * error_rows
 
-    def row_sharded(left, right):
-        half = left.shape[1] // 2
-        keep = trans_times(lax.dynamic_slice_in_dim(left, core * half, half, 1), right)
-        send = trans_times(
-            lax.dynamic_slice_in_dim(left, (1 - core) * half, half, 1), right, jnp.bfloat16
-        )
-        total = line_sum(keep + in_f32(sibling(send)))
-        rest = sibling(total)
-        first = jnp.where(core == 0, total, rest)
-        second = jnp.where(core == 0, rest, total)
-        return in_f32(jnp.concatenate([first, second], axis=0))
-
-    def column_sharded(left, first, second, pieces):
-        cols = first.shape[1] // pieces
-        mine_side = jnp.where(core == 0, first, second)
-        other_side = jnp.where(core == 0, second, first)
-        totals = []
-        for i in range(pieces):
-            cut = slice(i * cols, (i + 1) * cols)
-            keep = trans_times(left, mine_side[:, cut])
-            send = trans_times(left, other_side[:, cut], jnp.bfloat16)
-            totals.append(line_sum(keep + in_f32(sibling(send))))
-        out = []
-        for total in totals:
-            got = [lax.dynamic_slice_in_dim(total, mine * deep, deep, 0)]
-            for s in others:
-                got.append(shift(lax.dynamic_slice_in_dim(total, (mine ^ s) * deep, deep, 0), s))
-            out.append([(piece, sibling(piece)) for piece in got])
-        return out
-
-    def placed(pairs, which, starts, cols_of, cols):
-        whole = jnp.zeros((deep, cols), jnp.float32)
-        for piece_pairs, start, cut in zip(pairs, starts, cols_of):
-            for s, (own, other) in enumerate(piece_pairs):
-                chunk = in_f32(jnp.where(core == which, own, other)[:, cut])
-                whole = lax.dynamic_update_slice(
-                    whole, chunk, (0, (mine ^ s) * (cols // n_fsdp) + start)
-                )
-        return whole
-
     grad_branch_all = jnp.concatenate(gather_rows(in_bf16(grad_result)))
-    dw_down = row_sharded(hidden_b, grad_branch_all)
     grad_hidden = times_trans(grad_branch_all, w_down)
     grad_gate_pre, grad_up_pre = swiglu_back(grad_hidden)
     grad_gate_b = in_bf16(grad_gate_pre)
     grad_up_b = in_bf16(grad_up_pre)
     grad_mlp_b = jnp.concatenate([grad_gate_b, grad_up_b], axis=1)
     grad_normed_mlp = summed(grad_mlp_b, w_mlp, times_trans)
-    mlp_pieces = 2
-    mlp_pairs = column_sharded(normed_mlp_all, grad_gate_b, grad_up_b, mlp_pieces)
-    starts = [i * (ff // mlp_pieces) for i in range(mlp_pieces)]
-    cuts = [slice(None)] * mlp_pieces
-    dw_gate = placed(mlp_pairs, 0, starts, cuts, w_gate.shape[1])
-    dw_up = placed(mlp_pairs, 1, starts, cuts, w_up.shape[1])
     grad_middle_norm, grad_mlp_gain = mlp_norm_back(grad_normed_mlp)
     grad_middle = grad_result + grad_middle_norm
 
     grad_attn_all = jnp.concatenate(gather_rows(in_bf16(grad_middle)))
-    dw_output = row_sharded(gated_b, grad_attn_all)
     grad_gated = times_trans(grad_attn_all, w_output).reshape(
         n_fsdp, rows, heads_k, H // KV, HD
     )
@@ -372,22 +689,70 @@
     grad_query_b = in_bf16(grad_query_raw)
     grad_key_b = in_bf16(grad_key_raw)
     grad_value_b = in_bf16(grad_value.reshape(rows_all, cols_k))
-    first = jnp.concatenate([grad_query_b, grad_key_b], axis=1)
-    second = jnp.concatenate([grad_outgate_b, grad_value_b], axis=1)
-    attn_pairs = column_sharded(normed_all, first, second, 1)
-    query_cut, key_cut = slice(0, cols_q), slice(cols_q, None)
-    dw_query = placed(attn_pairs, 0, [0], [query_cut], w_query.shape[1])
-    dw_key = placed(attn_pairs, 0, [0], [key_cut], w_key.shape[1])
-    dw_outgate = placed(attn_pairs, 1, [0], [query_cut], w_outgate.shape[1])
-    dw_value = placed(attn_pairs, 1, [0], [key_cut], w_value.shape[1])
-    grad_normed = summed(jnp.concatenate([first, second], axis=1), w_attn, times_trans)
+    grad_raw_b = jnp.concatenate(
+        [grad_query_b, grad_outgate_b, grad_key_b, grad_value_b], axis=1
+    )
+    grad_normed = summed(grad_raw_b, w_attn, times_trans)
     _, norm_back = jax.vjp(rms_scale, tokens_f, attention_gain_f)
     grad_tokens_norm, grad_attention_gain = norm_back(grad_normed)
     tokens_grad = in_bf16(grad_middle + grad_tokens_norm)
 
-    dgains = lax.psum(
-        jnp.concatenate([grad_attention_gain, grad_mlp_gain, grad_query_gain, grad_key_gain]),
-        ("rep", "fsdp"),
+    dgains = sum_everywhere(
+        jnp.concatenate([grad_attention_gain, grad_mlp_gain, grad_query_gain, grad_key_gain])[None]
+    )[0]
+
+    piece_rows, piece_cols = deep // 2, width // n_fsdp
+    units, base = [], 0
+    for by_owner, row_blocks, cols in (
+        (False, ff // 2 // piece_rows, width),
+        (True, n_fsdp, 2 * ff),
+        (False, cols_q // 2 // piece_rows, width),
+        (True, n_fsdp, 2 * cols_q + 2 * cols_k),
+    ):
+        units.append(Unit(base, by_owner, row_blocks, cols // piece_cols))
+        base += units[-1].count
+    pieces = reduced(
+        n_fsdp,
+        n_rep,
+        units,
+        piece_rows,
+        piece_cols,
+        (hidden_b, normed_mlp_all, gated_b, normed_all),
+        (grad_branch_all, grad_mlp_b, grad_attn_all, grad_raw_b),
+    )
+    down, mlp, outp, attn = units
+
+    def by_rows(unit, weight):
+        blocks, together = unit.row_blocks, unit.col_blocks
+        return widened(
+            pieces,
+            (2, blocks),
+            together,
+            lambda c, r: (unit.base // together + r, c, 0, 0),
+            weight.shape,
+            lambda c, r: (c * blocks + r, 0),
+        )
+
+    def by_owners(unit, weight, which):
+        together = unit.col_blocks // 2
+        return widened(
+            pieces,
+            (2, n_fsdp),
+            together,
+            lambda c, f: (unit.base // together + 2 * f + which, c, 0, 0),
+            weight.shape,
+            lambda c, f: (c, f),
+        )
+
+    dw_down = by_rows(down, w_down)
+    dw_output = by_rows(outp, w_output)
+    dw_gate = by_owners(mlp, w_gate, 0)
+    dw_up = by_owners(mlp, w_up, 1)
+    dw_query, dw_outgate, dw_key, dw_value = widened_heads(
+        pieces,
+        attn.base,
+        n_fsdp,
+        (w_query.shape, w_outgate.shape, w_key.shape, w_value.shape),
     )
 
     def own_part(start, cols):

time: 1350 us -> 1000 us (0.74)
  Pallas kernels: 0 us -> 367 us
  waiting for transfers between devices: 557 us -> 237 us
  blocking collectives: 224 us -> 0 us
  other arithmetic: 128 us -> 74.8 us
  matrix products: 168 us -> 119 us
  starting transfers between devices: 111 us -> 67 us
  local copies, waits for them, and re-layouts: 151 us -> 129 us
    pallas_call x0 -> x6, Pallas kernels: none -> 367 us  [the longest x1 329 us: reduced(): pl.pallas_call(functools.partial(reduce_kernel, n_fsdp, n_rep, units, pie...]
    ppermute x15 -> x5, waiting for transfers between devices: 294 us -> 5.67 us  [sum_everywhere(): lax.ppermute(values, axis, [(i, i ^ step) for i in range(n)])]
    psum x1 -> x0, blocking collectives: 224 us -> none  [shards(): lax.psum(jnp.concatenate([grad_attention_gain, grad_mlp_gain, grad_query_...]
    dot_general x10 -> x0, matrix products: 50.6 us -> none  [trans_times(): lax.dot_general(left_side, right_side, (((0,), (0,)), ((), ())), preferre...]
    ppermute x66 -> x57, waiting for transfers between devices: 263 us -> 231 us  [shift(): return lax.ppermute(values, 'fsdp', [(i, i ^ step) for i in range(n_fsdp)])]
    ppermute x15 -> x5, starting transfers between devices: 33 us -> 4.51 us  [sum_everywhere(): lax.ppermute(values, axis, [(i, i ^ step) for i in range(n)])]
    convert_element_type x22 -> x13, other arithmetic: 40.2 us -> 23.2 us  [in_bf16(): return values.astype(jnp.bfloat16)]
    dynamic_update_slice x25 -> x0, other arithmetic: 16.6 us -> none  [placed(): lax.dynamic_update_slice(whole, chunk, (0, (mine ^ s) * (cols // n_fsdp)...]
  transfers between devices with their start and end apart: 106 -> 68, of which waited for: 44 -> 36; matrix products, arithmetic and copies ran while one was open for 26% -> 16% of each run, Pallas kernels for 0% -> 37%
where the time goes in v2:
time: 1000 us; the launch traced here: 996 us
  Pallas kernels  367 us (37%)
  waiting for transfers between devices  237 us (24%)
  local copies, waits for them, and re-layouts  129 us (13%)
  matrix products  119 us (12%)
  other arithmetic  74.8 us (7%)
  starting transfers between devices  67 us (7%)
    pallas_call x1, Pallas kernels, reduced(): pl.pallas_call(functools.partial(reduce_kernel, n_fsdp, n_rep, units, pie...  329 us
    ppermute x57, waiting for transfers between devices, shift(): return lax.ppermute(values, 'fsdp', [(i, i ^ step) for i in range(n_fsdp)])  231 us
    ppermute x57, starting transfers between devices, shift(): return lax.ppermute(values, 'fsdp', [(i, i ^ step) for i in range(n_fsdp)])  61.3 us
    dot_general x6, matrix products, times_trans(): lax.dot_general(left_side, right_side, (((1,), (1,)), ((), ())), preferre...  60.2 us
    dot_general x7, matrix products, times(): jnp.dot(left_side, right_side, preferred_element_type=jnp.float32)  46 us
    unnamed x173, local copies, waits for them, and re-layouts  29.4 us
    pallas_call x4, Pallas kernels, widened(): pl.pallas_call(widen_kernel, grid=grid, out_shape=jax.ShapeDtypeStruct(sh...  29.2 us
    convert_element_type x13, other arithmetic, in_bf16(): return values.astype(jnp.bfloat16)  23.2 us
  transfers between devices with their start and end apart: 68, of which 36 were waited for; matrix products, arithmetic and copies ran while one was open for 16% of the time, Pallas kernels for 37%

profile of v2, /device:TPU:0, one launch (start us, length us, event | category | flops | bytes accessed | tf_op | source)
XLA Modules:
  0.0 996.4 jit_solution(11441395452977455050)
XLA Ops:
  19.9 7.8 constant_dynamic-slice_fusion.4
  47.2 8.3 collective-permute-done.1
  64.6 7.7 collective-permute-done.9
  74.9 23.0 %collective-permute-done.4 = bf16[128,2048]{1,0:T(8,128)(2,1)S(1)} collective-permute-done((bf16[128,2048]{1,0:T(8,128)(2,1)}, bf16[128,2048]{1,0:T(8,128)(2,1)S(1)}, u32[]{:S(2)}, u32[]{:S(2)}) %collective-permute-start.4) | collective-permute-done | bytes 524320 | tf_op jit(solution)/shard_map/ppermute | solution.py:85
  110.9 8.7 fusion.114
  194.6 9.9 collective-permute-done.16
  205.6 33.0 %collective-permute-done.19 = bf16[128,2048]{1,0:T(8,128)(2,1)S(1)} collective-permute-done((bf16[128,2048]{1,0:T(8,128)(2,1)S(1)}, bf16[128,2048]{1,0:T(8,128)(2,1)S(1)}, u32[]{:S(2)}, u32[]{:S(2)}) %collective-permute-start.19) | collective-permute-done | bytes 524320 | tf_op jit(solution)/shard_map/ppermute | solution.py:85
  269.5 16.6 %collective-permute-done.21 = bf16[128,2048]{1,0:T(8,128)(2,1)S(1)} collective-permute-done((bf16[128,2048]{1,0:T(8,128)(2,1)S(1)}, bf16[128,2048]{1,0:T(8,128)(2,1)S(1)}, u32[]{:S(2)}, u32[]{:S(2)}) %collective-permute-start.21) | collective-permute-done | bytes 524320 | tf_op jit(solution)/shard_map/ppermute | solution.py:85
  291.4 9.5 collective-permute-done.23
  309.0 8.6 fusion.8
  317.5 12.2 %multiply_convert_fusion.1 = (bf16[1024,1536]{1,0:T(8,128)(2,1)S(1)}, f32[1024,1536]{1,0:T(8,128)}) fusion(f32[1024,1536]{1,0:T(8,128)} %fusion.8, bf16[1024,2048]{1,0:T(8,128)(2,1)} %copy-done.52, bf16[2048,3072]{1,0:T(8,128)(2,1)S(1)} %constant_dynamic-update-slice_fusion.29), kind=kOutput, calls=%fused_computation.20 | convolution fusion | flops 6451888128 | bytes 26214400 | tf_op jit(solution)/shard_map/dot_general | solution.py:52
  381.2 10.8 %collective-permute-done.39 = bf16[128,2048]{1,0:T(8,128)(2,1)S(1)} collective-permute-done((bf16[128,2048]{1,0:T(8,128)(2,1)S(1)}, bf16[128,2048]{1,0:T(8,128)(2,1)S(1)}, u32[]{:S(2)}, u32[]{:S(2)}) %collective-permute-start.39) | collective-permute-done | bytes 524320 | tf_op jit(solution)/shard_map/ppermute | solution.py:85
  407.4 16.2 %multiply_convert_fusion = (bf16[1024,1536]{1,0:T(8,128)(2,1)S(1)}, bf16[1024,1536]{1,0:T(8,128)(2,1)}) fusion(f32[1024,1536]{1,0:T(8,128)} %fusion.8, f32[1024,1536]{1,0:T(8,128)} %get-tuple-element.136, bf16[1024,2048]{1,0:T(8,128)(2,1)S(1)} %constant_dynamic-update-slice_fusion.14.refs_4_, bf16[1536,2048]{1,0:T(8,128)(2,1)} %param.31), kind=kOutput, calls=%fused_computation.19 | convolution fusion | flops 6464471040 | bytes 29360128 | tf_op jit(solution)/shard_map/dot_general | solution.py:56
  423.6 15.2 %fusion.20 = bf16[768,2048]{1,0:T(8,128)(2,1)S(1)} fusion(bf16[2048,3072]{1,0:T(8,128)(2,1)} %copy-done.13, bf16[1024,1536]{1,0:T(8,128)(2,1)} %get-tuple-element.45, bf16[1024,1536]{1,0:T(8,128)(2,1)S(1)} %get-tuple-element.44), kind=kOutput, calls=%fused_computation.42 | convolution fusion | flops 9674686464 | bytes 22020096 | tf_op jit(solution)/shard_map/dot_general | solution.py:56
  442.5 10.3 %collective-permute-done.46 = bf16[128,2048]{1,0:T(8,128)(2,1)S(1)} collective-permute-done((bf16[128,2048]{1,0:T(8,128)(2,1)S(1)}, bf16[128,2048]{1,0:T(8,128)(2,1)S(1)}, u32[]{:S(2)}, u32[]{:S(2)}) %collective-permute-start.46) | collective-permute-done | bytes 524320 | tf_op jit(solution)/shard_map/ppermute | solution.py:85
  471.8 10.8 %multiply_reduce_fusion.1 = (f32[2048]{0:T(1024)S(1)}, f32[256]{0:T(256)S(1)}, f32[256,2048]{1,0:T(8,128)}) fusion(f32[256,2048]{1,0:T(8,128)S(1)} %copy-done.25, f32[256]{0:T(256)S(1)} %fusion.90, f32[2048]{0:T(1024)S(1)} %bitcast.145, f32[128,2048]{1,0:T(8,128)} %convert_add_fusion.3, f32[128,2048]{1,0:T(8,128)} %convert_add_fusion.4, ...), kind=kOutput, calls=%fused_computation.88 | convolution fusion | flops 3228563200 | bytes 25184256 | tf_op jit(solution)/shard_map/dot_general | solution.py:56
  491.0 10.5 %collective-permute-done.51 = bf16[128,2048]{1,0:T(8,128)(2,1)S(1)} collective-permute-done((bf16[128,2048]{1,0:T(8,128)(2,1)S(1)}, bf16[128,2048]{1,0:T(8,128)(2,1)S(1)}, u32[]{:S(2)}, u32[]{:S(2)}) %collective-permute-start.51) | collective-permute-done | bytes 524320 | tf_op jit(solution)/shard_map/ppermute | solution.py:85
  562.7 7.9 convolution_convert_fusion.1
  574.1 12.5 %collective-permute-done.58 = bf16[128,2048]{1,0:T(8,128)(2,1)S(1)} collective-permute-done((bf16[128,2048]{1,0:T(8,128)(2,1)S(1)}, bf16[128,2048]{1,0:T(8,128)(2,1)S(1)}, u32[]{:S(2)}, u32[]{:S(2)}) %collective-permute-start.58) | collective-permute-done | bytes 524320 | tf_op jit(solution)/shard_map/ppermute | solution.py:85
  618.3 328.7 %reduce_weight_gradients.1.query_in.gate_in.pair_in.in_ref = bf16[52,2,256,512]{3,2,1,0:T(8,128)(2,1)} custom-call(bf16[1024,1536]{1,0:T(8,128)(2,1)} %copy-done.70, bf16[1024,2048]{1,0:T(8,128)(2,1)} %copy-done.52, bf16[1024,512]{1,0:T(8,128)(2,1)} %convert_element_type.347.refs_2_, bf16[1024,2048]{1,0:T(8,128)(2,1)} %copy-done.34, ...), custom_call_target="tpu_custom_call" | custom-call | flops 27917287424 | bytes 1073741824 | tf_op jit(solution)/shard_map/reduce_weight_gradients/pallas_call | solution.py:408
  947.0 8.7 widen_heads.1
  959.1 8.8 widen.5
  967.9 8.8 widen.6
  976.8 8.2 widen.7
  (466 shorter events, 390.7 us)
Async XLA Ops:
  3.1 40.6 %collective-permute-start = (bf16[128,2048]{1,0:T(8,128)(2,1)}, bf16[128,2048]{1,0:T(8,128)(2,1)}, u32[]{:S(2)}, u32[]{:S(2)}) collective-permute-start(bf16[128,2048]{1,0:T(8,128)(2,1)} %get-tuple-element.114), channel_id=1, source_target_pairs={{0,1},{1,0},{2,3},{3,2},{4,5},{5,4},{6,7},{7,6},{8,9},{9,8},{10,11... | collective-permute-start | bytes 1572872 | tf_op jit(solution)/shard_map/ppermute | solution.py:85
  6.0 51.4 %collective-permute-start.2 = (bf16[128,2048]{1,0:T(8,128)(2,1)}, bf16[128,2048]{1,0:T(8,128)(2,1)}, u32[]{:S(2)}, u32[]{:S(2)}) collective-permute-start(bf16[128,2048]{1,0:T(8,128)(2,1)} %get-tuple-element.114), channel_id=1, source_target_pairs={{0,2},{1,3},{2,0},{3,1},{4,6},{5,7},{6,4},{7,5},{8,10},{9,11},{10,... | collective-permute-start | bytes 1572872 | tf_op jit(solution)/shard_map/ppermute | solution.py:85
  10.4 29.8 %collective-permute-start.8 = (bf16[1,1088]{1,0:T(2,128)(2,1)S(1)}, bf16[1,1088]{1,0:T(2,128)(2,1)S(1)}, u32[]{:S(2)}, u32[]{:S(2)}) collective-permute-start(bf16[1,1088]{1,0:T(2,128)(2,1)S(1)} %broadcast_in_dim.116), channel_id=1, source_target_pairs={{0,3},{1,2},{2,1},{3,0},{4,7},{5,6},{6,5},{7,4},{8,11},{9,10},{10,... | collective-permute-start | bytes 6536 | tf_op jit(solution)/shard_map/ppermute | solution.py:85
  10.4 30.4 %collective-permute-start.7 = (bf16[1,1088]{1,0:T(2,128)(2,1)S(1)}, bf16[1,1088]{1,0:T(2,128)(2,1)S(1)}, u32[]{:S(2)}, u32[]{:S(2)}) collective-permute-start(bf16[1,1088]{1,0:T(2,128)(2,1)S(1)} %broadcast_in_dim.116), channel_id=1, source_target_pairs={{0,2},{1,3},{2,0},{3,1},{4,6},{5,7},{6,4},{7,5},{8,10},{9,11},{10,... | collective-permute-start | bytes 6536 | tf_op jit(solution)/shard_map/ppermute | solution.py:85
  12.4 28.5 %collective-permute-start.6 = (bf16[1,1088]{1,0:T(2,128)(2,1)S(1)}, bf16[1,1088]{1,0:T(2,128)(2,1)S(1)}, u32[]{:S(2)}, u32[]{:S(2)}) collective-permute-start(bf16[1,1088]{1,0:T(2,128)(2,1)S(1)} %broadcast_in_dim.116), channel_id=1, source_target_pairs={{0,1},{1,0},{2,3},{3,2},{4,5},{5,4},{6,7},{7,6},{8,9},{9,8},{10,11... | collective-permute-start | bytes 6536 | tf_op jit(solution)/shard_map/ppermute | solution.py:85
  40.9 31.4 %collective-permute-start.9 = (bf16[256,1536]{1,0:T(8,128)(2,1)}, bf16[256,1536]{1,0:T(8,128)(2,1)}, u32[]{:S(2)}, u32[]{:S(2)}) collective-permute-start(bf16[256,1536]{1,0:T(8,128)(2,1)} %fusion.76), channel_id=1, source_target_pairs={{0,1},{1,0},{2,3},{3,2},{4,5},{5,4},{6,7},{7,6},{8,9},{9,8},{10,11... | collective-permute-start | bytes 2359304 | tf_op jit(solution)/shard_map/ppermute | solution.py:85
  43.7 55.4 %collective-permute-start.11 = (bf16[256,1536]{1,0:T(8,128)(2,1)}, bf16[256,1536]{1,0:T(8,128)(2,1)S(1)}, u32[]{:S(2)}, u32[]{:S(2)}) collective-permute-start(bf16[256,1536]{1,0:T(8,128)(2,1)} %fusion.73), channel_id=1, source_target_pairs={{0,2},{1,3},{2,0},{3,1},{4,6},{5,7},{6,4},{7,5},{8,10},{9,11},{10,... | collective-permute-start | bytes 2359304 | tf_op jit(solution)/shard_map/ppermute | solution.py:85
  55.4 43.7 %collective-permute-start.13 = (bf16[256,1536]{1,0:T(8,128)(2,1)S(1)}, bf16[256,1536]{1,0:T(8,128)(2,1)S(1)}, u32[]{:S(2)}, u32[]{:S(2)}) collective-permute-start(bf16[256,1536]{1,0:T(8,128)(2,1)S(1)} %fusion.70), channel_id=1, source_target_pairs={{0,3},{1,2},{2,1},{3,0},{4,7},{5,6},{6,5},{7,4},{8,11},{9,10},{10,... | collective-permute-start | bytes 2359304 | tf_op jit(solution)/shard_map/ppermute | solution.py:85
  57.4 40.5 %collective-permute-start.4 = (bf16[128,2048]{1,0:T(8,128)(2,1)}, bf16[128,2048]{1,0:T(8,128)(2,1)S(1)}, u32[]{:S(2)}, u32[]{:S(2)}) collective-permute-start(bf16[128,2048]{1,0:T(8,128)(2,1)} %collective-permute-done), channel_id=1, source_target_pairs={{0,2},{1,3},{2,0},{3,1},{4,6},{5,7},{6,4},{7,5},{8,10},{9,11},{10,... | collective-permute-start | bytes 1572872 | tf_op jit(solution)/shard_map/ppermute | solution.py:85
  59.3 41.0 %collective-permute-start.5 = (bf16[128,2048]{1,0:T(8,128)(2,1)}, bf16[128,2048]{1,0:T(8,128)(2,1)S(1)}, u32[]{:S(2)}, u32[]{:S(2)}) collective-permute-start(bf16[128,2048]{1,0:T(8,128)(2,1)} %collective-permute-done.3), channel_id=1, source_target_pairs={{0,1},{1,0},{2,3},{3,2},{4,5},{5,4},{6,7},{7,6},{8,9},{9,8},{10,11... | collective-permute-start | bytes 1572872 | tf_op jit(solution)/shard_map/ppermute | solution.py:85
  72.3 176.2 %collective-permute-start.27 = (bf16[256,3072]{1,0:T(8,128)(2,1)}, bf16[256,3072]{1,0:T(8,128)(2,1)}, u32[]{:S(2)}, u32[]{:S(2)}) collective-permute-start(bf16[256,3072]{1,0:T(8,128)(2,1)} %fusion.53), channel_id=1, source_target_pairs={{0,1},{1,0},{2,3},{3,2},{4,5},{5,4},{6,7},{7,6},{8,9},{9,8},{10,11... | collective-permute-start | bytes 4718600 | tf_op jit(solution)/shard_map/ppermute | solution.py:85
  97.9 152.6 %collective-permute-start.29 = (bf16[256,3072]{1,0:T(8,128)(2,1)}, bf16[256,3072]{1,0:T(8,128)(2,1)}, u32[]{:S(2)}, u32[]{:S(2)}) collective-permute-start(bf16[256,3072]{1,0:T(8,128)(2,1)} %fusion.52), channel_id=1, source_target_pairs={{0,2},{1,3},{2,0},{3,1},{4,6},{5,7},{6,4},{7,5},{8,10},{9,11},{10,... | collective-permute-start | bytes 4718600 | tf_op jit(solution)/shard_map/ppermute | solution.py:85
  190.8 47.8 %collective-permute-start.19 = (bf16[128,2048]{1,0:T(8,128)(2,1)S(1)}, bf16[128,2048]{1,0:T(8,128)(2,1)S(1)}, u32[]{:S(2)}, u32[]{:S(2)}) collective-permute-start(bf16[128,2048]{1,0:T(8,128)(2,1)S(1)} %get-tuple-element.75), channel_id=1, source_target_pairs={{0,2},{1,3},{2,0},{3,1},{4,6},{5,7},{6,4},{7,5},{8,10},{9,11},{10,... | collective-permute-start | bytes 1572872 | tf_op jit(solution)/shard_map/ppermute | solution.py:85
  193.7 61.6 %collective-permute-start.31 = (bf16[256,3072]{1,0:T(8,128)(2,1)}, bf16[256,3072]{1,0:T(8,128)(2,1)}, u32[]{:S(2)}, u32[]{:S(2)}) collective-permute-start(bf16[256,3072]{1,0:T(8,128)(2,1)} %fusion.51), channel_id=1, source_target_pairs={{0,3},{1,2},{2,1},{3,0},{4,7},{5,6},{6,5},{7,4},{8,11},{9,10},{10,... | collective-permute-start | bytes 4718600 | tf_op jit(solution)/shard_map/ppermute | solution.py:85
  204.5 50.9 %collective-permute-start.18 = (bf16[128,2048]{1,0:T(8,128)(2,1)}, bf16[128,2048]{1,0:T(8,128)(2,1)}, u32[]{:S(2)}, u32[]{:S(2)}) collective-permute-start(bf16[128,2048]{1,0:T(8,128)(2,1)} %get-tuple-element.76), channel_id=1, source_target_pairs={{0,2},{1,3},{2,0},{3,1},{4,6},{5,7},{6,4},{7,5},{8,10},{9,11},{10,... | collective-permute-start | bytes 1572872 | tf_op jit(solution)/shard_map/ppermute | solution.py:85
  255.4 32.7 %collective-permute-start.30 = (bf16[256,3072]{1,0:T(8,128)(2,1)}, bf16[256,3072]{1,0:T(8,128)(2,1)S(1)}, u32[]{:S(2)}, u32[]{:S(2)}) collective-permute-start(bf16[256,3072]{1,0:T(8,128)(2,1)} %collective-permute-done.29), channel_id=1, source_target_pairs={{0,4},{4,0},{8,12},{12,8},{16,20},{20,16},{24,28},{28,24},{1,5},{5... | collective-permute-start | bytes 4718600 | tf_op jit(solution)/shard_map/ppermute | solution.py:90
  255.9 35.2 %collective-permute-start.32 = (bf16[256,3072]{1,0:T(8,128)(2,1)}, bf16[256,3072]{1,0:T(8,128)(2,1)S(1)}, u32[]{:S(2)}, u32[]{:S(2)}) collective-permute-start(bf16[256,3072]{1,0:T(8,128)(2,1)} %collective-permute-done.31), channel_id=1, source_target_pairs={{0,4},{4,0},{8,12},{12,8},{16,20},{20,16},{24,28},{28,24},{1,5},{5... | collective-permute-start | bytes 4718600 | tf_op jit(solution)/shard_map/ppermute | solution.py:90
  264.2 27.1 %collective-permute-start.22 = (bf16[128,2048]{1,0:T(8,128)(2,1)S(1)}, bf16[128,2048]{1,0:T(8,128)(2,1)S(1)}, u32[]{:S(2)}, u32[]{:S(2)}) collective-permute-start(bf16[128,2048]{1,0:T(8,128)(2,1)S(1)} %get-tuple-element.101), channel_id=1, source_target_pairs={{0,1},{1,0},{2,3},{3,2},{4,5},{5,4},{6,7},{7,6},{8,9},{9,8},{10,11... | collective-permute-start | bytes 1572872 | tf_op jit(solution)/shard_map/ppermute | solution.py:85
  286.1 20.8 %collective-permute-start.25 = (bf16[128,2048]{1,0:T(8,128)(2,1)S(1)}, bf16[128,2048]{1,0:T(8,128)(2,1)S(1)}, u32[]{:S(2)}, u32[]{:S(2)}) collective-permute-start(bf16[128,2048]{1,0:T(8,128)(2,1)S(1)} %collective-permute-done.21), channel_id=1, source_target_pairs={{0,2},{1,3},{2,0},{3,1},{4,6},{5,7},{6,4},{7,5},{8,10},{9,11},{10,... | collective-permute-start | bytes 1572872 | tf_op jit(solution)/shard_map/ppermute | solution.py:85
  337.8 25.0 %collective-permute-start.36 = (bf16[128,2048]{1,0:T(8,128)(2,1)}, bf16[128,2048]{1,0:T(8,128)(2,1)S(1)}, u32[]{:S(2)}, u32[]{:S(2)}) collective-permute-start(bf16[128,2048]{1,0:T(8,128)(2,1)} %get-tuple-element.70), channel_id=1, source_target_pairs={{0,2},{1,3},{2,0},{3,1},{4,6},{5,7},{6,4},{7,5},{8,10},{9,11},{10,... | collective-permute-start | bytes 1572872 | tf_op jit(solution)/shard_map/ppermute | solution.py:85
  378.2 23.2 %collective-permute-start.40 = (bf16[128,2048]{1,0:T(8,128)(2,1)S(1)}, bf16[128,2048]{1,0:T(8,128)(2,1)S(1)}, u32[]{:S(2)}, u32[]{:S(2)}) collective-permute-start(bf16[128,2048]{1,0:T(8,128)(2,1)S(1)} %get-tuple-element.99), channel_id=1, source_target_pairs={{0,1},{1,0},{2,3},{3,2},{4,5},{5,4},{6,7},{7,6},{8,9},{9,8},{10,11... | collective-permute-start | bytes 1572872 | tf_op jit(solution)/shard_map/ppermute | solution.py:85
  379.6 22.1 %collective-permute-start.41 = (bf16[128,2048]{1,0:T(8,128)(2,1)S(1)}, bf16[128,2048]{1,0:T(8,128)(2,1)S(1)}, u32[]{:S(2)}, u32[]{:S(2)}) collective-permute-start(bf16[128,2048]{1,0:T(8,128)(2,1)S(1)} %get-tuple-element.100), channel_id=1, source_target_pairs={{0,2},{1,3},{2,0},{3,1},{4,6},{5,7},{6,4},{7,5},{8,10},{9,11},{10,... | collective-permute-start | bytes 1572872 | tf_op jit(solution)/shard_map/ppermute | solution.py:85
  441.3 21.9 %collective-permute-start.48 = (bf16[128,2048]{1,0:T(8,128)(2,1)S(1)}, bf16[128,2048]{1,0:T(8,128)(2,1)S(1)}, u32[]{:S(2)}, u32[]{:S(2)}) collective-permute-start(bf16[128,2048]{1,0:T(8,128)(2,1)S(1)} %get-tuple-element.64), channel_id=1, source_target_pairs={{0,2},{1,3},{2,0},{3,1},{4,6},{5,7},{6,4},{7,5},{8,10},{9,11},{10,... | collective-permute-start | bytes 1572872 | tf_op jit(solution)/shard_map/ppermute | solution.py:85
  618.2 366.7 %collective-permute-start.65 = (f32[1,4352]{1,0:T(1,128)S(1)}, f32[1,4352]{1,0:T(1,128)S(1)}, u32[]{:S(2)}, u32[]{:S(2)}) collective-permute-start(f32[1,4352]{1,0:T(1,128)S(1)} %add.445), channel_id=1, source_target_pairs={{0,4},{4,0},{8,12},{12,8},{16,20},{20,16},{24,28},{28,24},{1,5},{5... | collective-permute-start | bytes 52232 | tf_op jit(solution)/shard_map/ppermute | solution.py:98
  (117 other events, 1575.4 us)

commit v3 on v2

--- a/solution.py
+++ b/solution.py
@@ -23,12 +23,6 @@
     return (
         values * lax.rsqrt(jnp.mean(values * values, axis=-1, keepdims=True) + EPS_NORM) * gain_vec
     )
-
-
-def rotate(values, angle_cos, angle_sin):
-    half_dim = values.shape[-1] // 2
-    turned = jnp.concatenate([-values[..., half_dim:], values[..., :half_dim]], axis=-1)
-    return values * angle_cos + turned * angle_sin
 
 
 def row_layout(pair_len, row_count, head_dim):
@@ -62,10 +56,6 @@
     return lax.dot_general(
         left_side, right_side, (((0,), (0,)), ((), ())), preferred_element_type=jnp.float32
     ).astype(out)
-
-
-def gating(context, gate_heads):
-    return context * jax.nn.sigmoid(gate_heads)
 
 
 def swiglu(gate_pre, up_pre):
@@ -473,6 +463,416 @@
     )(pieces, pieces, pieces)
 
 
+def block_mask(pair_ref, rows):
+    block = pl.program_id(0)
+    head_len = pair_ref[block, 0]
+    both_len = head_len + pair_ref[block, 1]
+    query_row = lax.broadcasted_iota(jnp.int32, (rows, rows), 0)
+    key_row = lax.broadcasted_iota(jnp.int32, (rows, rows), 1)
+
+    def segment(index):
+        return (index >= head_len).astype(jnp.int32) + (index >= both_len).astype(jnp.int32)
+
+    return (segment(query_row) == segment(key_row)) & (key_row <= query_row)
+
+
+def turn(values):
+    half_dim = values.shape[-1] // 2
+    return jnp.concatenate([-values[:, half_dim:], values[:, :half_dim]], axis=-1)
+
+
+def head_forward(raw, gain, angle_cos, angle_sin):
+    values = raw * lax.rsqrt(jnp.mean(raw * raw, axis=-1, keepdims=True) + EPS_NORM) * gain
+    return in_bf16(values * angle_cos + turn(values) * angle_sin)
+
+
+def head_backward(grad, raw, gain, angle_cos, angle_sin):
+    grad = grad * angle_cos - turn(grad * angle_sin)
+    scale = lax.rsqrt(jnp.mean(raw * raw, axis=-1, keepdims=True) + EPS_NORM)
+    unit = raw * scale
+    gain_rows = grad * unit
+    inner = grad * gain
+    return scale * (inner - unit * jnp.mean(inner * unit, axis=-1, keepdims=True)), gain_rows
+
+
+def product_of(left, right, left_dim, right_dim):
+    return lax.dot_general(
+        left, right, (((left_dim,), (right_dim,)), ((), ())), preferred_element_type=jnp.float32
+    )
+
+
+def softmax_of(queries, keys, allowed):
+    scores = jnp.where(allowed, product_of(queries, keys, 1, 1) * HD ** (-0.5), NEG_FILL)
+    exponent = jnp.exp(scores - jnp.max(scores, axis=-1, keepdims=True))
+    return exponent / jnp.sum(exponent, axis=-1, keepdims=True)
+
+
+def attend_kernel(
+    heads_k, pair_ref, raw_ref, cos_ref, sin_ref, qg_ref, kg_ref, q_ref, k_ref, v_ref, gated_ref
+):
+    group = H // KV
+    cols_q, cols_k = heads_k * group * HD, heads_k * HD
+    allowed = block_mask(pair_ref, raw_ref.shape[0])
+    angle_cos, angle_sin = cos_ref[...], sin_ref[...]
+    for j in range(heads_k):
+        own = slice(j * HD, (j + 1) * HD)
+        keys = head_forward(
+            raw_ref[:, 2 * cols_q + j * HD : 2 * cols_q + (j + 1) * HD],
+            kg_ref[...],
+            angle_cos,
+            angle_sin,
+        )
+        start = 2 * cols_q + cols_k + j * HD
+        values = in_bf16(raw_ref[:, start : start + HD])
+        k_ref[:, own] = keys
+        v_ref[:, own] = values
+        for h in range(j * group, (j + 1) * group):
+            cut = slice(h * HD, (h + 1) * HD)
+            queries = head_forward(raw_ref[:, cut], qg_ref[...], angle_cos, angle_sin)
+            q_ref[:, cut] = queries
+            probs = in_bf16(softmax_of(queries, keys, allowed))
+            context = product_of(probs, values, 1, 0)
+            gate = raw_ref[:, cols_q + h * HD : cols_q + (h + 1) * HD]
+            gated_ref[:, cut] = in_bf16(context * jax.nn.sigmoid(gate))
+
+
+def attend_back_kernel(
+    heads_k,
+    pair_ref,
+    raw_ref,
+    cos_ref,
+    sin_ref,
+    qg_ref,
+    kg_ref,
+    q_ref,
+    k_ref,
+    v_ref,
+    grad_ref,
+    out_ref,
+    gain_ref,
+):
+    group = H // KV
+    cols_q, cols_k = heads_k * group * HD, heads_k * HD
+    allowed = block_mask(pair_ref, raw_ref.shape[0])
+    angle_cos, angle_sin = cos_ref[...], sin_ref[...]
+
+    @pl.when(pl.program_id(0) == 0)
+    def _():
+        gain_ref[...] = jnp.zeros_like(gain_ref)
+
+    for j in range(heads_k):
+        own = slice(j * HD, (j + 1) * HD)
+        keys, values = k_ref[:, own], v_ref[:, own]
+        grad_keys, grad_values = 0.0, 0.0
+        for h in range(j * group, (j + 1) * group):
+            cut = slice(h * HD, (h + 1) * HD)
+            gate_cut = slice(cols_q + h * HD, cols_q + (h + 1) * HD)
+            queries, grad_gated = q_ref[:, cut], grad_ref[:, cut]
+            probs = softmax_of(queries, keys, allowed)
+            probs_b = in_bf16(probs)
+            context = product_of(probs_b, values, 1, 0)
+            gate = jax.nn.sigmoid(raw_ref[:, gate_cut])
+            grad_context = in_bf16(grad_gated * gate)
+            out_ref[:, gate_cut] = in_bf16(grad_gated * context * gate * (1.0 - gate))
+            grad_probs = product_of(grad_context, values, 1, 1)
+            grad_scores = in_bf16(
+                probs * (grad_probs - jnp.sum(probs * grad_probs, axis=-1, keepdims=True))
+            )
+            grad_values += product_of(probs_b, grad_context, 0, 0)
+            grad_keys += product_of(grad_scores, queries, 0, 0)
+            grad_queries = product_of(grad_scores, keys, 1, 0) * HD ** (-0.5)
+            grad_raw, gain_rows = head_backward(
+                grad_queries, raw_ref[:, cut], qg_ref[...], angle_cos, angle_sin
+            )
+            out_ref[:, cut] = in_bf16(grad_raw)
+            gain_ref[0:1, :] += jnp.sum(gain_rows, axis=0, keepdims=True)
+        key_start = 2 * cols_q + j * HD
+        grad_raw, gain_rows = head_backward(
+            grad_keys * HD ** (-0.5),
+            raw_ref[:, key_start : key_start + HD],
+            kg_ref[...],
+            angle_cos,
+            angle_sin,
+        )
+        out_ref[:, key_start : key_start + HD] = in_bf16(grad_raw)
+        gain_ref[1:2, :] += jnp.sum(gain_rows, axis=0, keepdims=True)
+        value_start = 2 * cols_q + cols_k + j * HD
+        out_ref[:, value_start : value_start + HD] = in_bf16(grad_values)
+
+
+def rows_spec(rows, cols):
+    return pl.BlockSpec((rows, cols), lambda s: (s, 0))
+
+
+def whole_spec(shape):
+    return pl.BlockSpec(shape, lambda s: (0, 0))
+
+
+def attend(heads_k, rows, pair_len, raw, angle_cos, angle_sin, query_gain, key_gain):
+    rows_all, cols = raw.shape
+    cols_q, cols_k = heads_k * (H // KV) * HD, heads_k * HD
+    outs = (cols_q, cols_k, cols_k, cols_q)
+    return pl.pallas_call(
+        functools.partial(attend_kernel, heads_k),
+        grid=(rows_all // rows,),
+        in_specs=[
+            pl.BlockSpec(memory_space=pltpu.SMEM),
+            rows_spec(rows, cols),
+            rows_spec(rows, HD),
+            rows_spec(rows, HD),
+            whole_spec((1, HD)),
+            whole_spec((1, HD)),
+        ],
+        out_shape=[jax.ShapeDtypeStruct((rows_all, c), jnp.bfloat16) for c in outs],
+        out_specs=[rows_spec(rows, c) for c in outs],
+        cost_estimate=pl.CostEstimate(
+            flops=4 * rows_all * rows * cols_q,
+            bytes_accessed=8 * rows_all * cols,
+            transcendentals=rows_all * rows * heads_k * 2,
+        ),
+        compiler_params=pltpu.CompilerParams(vmem_limit_bytes=32 << 20),
+        name="attend",
+    )(pair_len, raw, angle_cos, angle_sin, query_gain, key_gain)
+
+
+def attend_back(
+    heads_k, rows, pair_len, raw, angle_cos, angle_sin, query_gain, key_gain, q, k, v, grad_gated
+):
+    rows_all, cols = raw.shape
+    cols_q, cols_k = heads_k * (H // KV) * HD, heads_k * HD
+    return pl.pallas_call(
+        functools.partial(attend_back_kernel, heads_k),
+        grid=(rows_all // rows,),
+        in_specs=[
+            pl.BlockSpec(memory_space=pltpu.SMEM),
+            rows_spec(rows, cols),
+            rows_spec(rows, HD),
+            rows_spec(rows, HD),
+            whole_spec((1, HD)),
+            whole_spec((1, HD)),
+            rows_spec(rows, cols_q),
+            rows_spec(rows, cols_k),
+            rows_spec(rows, cols_k),
+            rows_spec(rows, cols_q),
+        ],
+        out_shape=[
+            jax.ShapeDtypeStruct((rows_all, cols), jnp.bfloat16),
+            jax.ShapeDtypeStruct((8, HD), jnp.float32),
+        ],
+        out_specs=[rows_spec(rows, cols), whole_spec((8, HD))],
+        cost_estimate=pl.CostEstimate(
+            flops=14 * rows_all * rows * cols_q,
+            bytes_accessed=10 * rows_all * cols,
+            transcendentals=rows_all * rows * heads_k * 2,
+        ),
+        compiler_params=pltpu.CompilerParams(vmem_limit_bytes=32 << 20),
+        name="attend_back",
+    )(pair_len, raw, angle_cos, angle_sin, query_gain, key_gain, q, k, v, grad_gated)
+
+
+def after(values, *others):
+    return lax.optimization_barrier((values, *others))[0]
+
+
+def remote_copy(src, dst, send, recv, to_rep, to_fsdp):
+    return pltpu.make_async_remote_copy(
+        src_ref=src,
+        dst_ref=dst,
+        send_sem=send,
+        recv_sem=recv,
+        device_id={"rep": to_rep, "fsdp": to_fsdp},
+        device_id_type=MESH,
+    )
+
+
+def greet_all(peers):
+    barrier = pltpu.get_barrier_semaphore()
+    for to_rep, to_fsdp in peers:
+        pl.semaphore_signal(
+            barrier, inc=1, device_id={"rep": to_rep, "fsdp": to_fsdp}, device_id_type=MESH
+        )
+    pl.semaphore_wait(barrier, len(peers))
+
+
+class GatherRows:
+    def __init__(self, n_fsdp, rep, mine, source, target, sems):
+        self.n_fsdp, self.rep, self.mine = n_fsdp, rep, mine
+        self.source, self.target = source, target
+        self.send, self.recv, self.local = sems
+        self.half = source.shape[0] // 2
+
+    def copy(self, s, h, to=None, src=None):
+        rows = pl.ds(h * self.half, self.half)
+        to = s if to is None else to
+        return remote_copy(
+            self.source.at[rows] if src is None else self.target.at[src, rows],
+            self.target.at[s, rows],
+            self.send.at[s, h],
+            self.recv.at[s, h],
+            self.rep,
+            flipped(self.mine, to, self.n_fsdp),
+        )
+
+    def own(self):
+        return pltpu.make_async_copy(self.source, self.target.at[0], self.local)
+
+    def start(self):
+        for s, h in ((1, 0), (2, 1), (1, 1), (2, 0)):
+            if s < self.n_fsdp:
+                self.copy(s, h).start()
+        if self.n_fsdp != 4:
+            for s in range(3, self.n_fsdp):
+                for h in range(2):
+                    self.copy(s, h).start()
+        self.own().start()
+
+    def forward(self):
+        if self.n_fsdp == 4:
+            self.copy(1, 0).wait_recv()
+            self.copy(3, 0, to=2, src=1).start()
+            self.copy(2, 1).wait_recv()
+            self.copy(3, 1, to=1, src=2).start()
+
+    def finish(self):
+        for s in range(1, self.n_fsdp):
+            for h in range(2):
+                copy = self.copy(s, h)
+                if self.n_fsdp == 4 and (s, h) in ((1, 0), (2, 1)):
+                    copy.wait_send()
+                else:
+                    copy.wait()
+        self.own().wait()
+
+
+def fetch_kernel(n_fsdp, n_rep, widths, ff, *refs):
+    (tokens, gains, wq, wg, wk, wv, w_gate, w_up) = refs[:8]
+    (tokens_all, gains_all, w_attn, mlp_part) = refs[8:12]
+    (ts, tr, tl, gs, gr, ws, wr, zs, zr, cs, cr, ms, mr, ls) = refs[12:]
+    rep, mine = lax.axis_index("rep"), lax.axis_index("fsdp")
+    core, place = rep % 2, rep // 2
+    sib = rep + 1 - 2 * core
+    partner = (place + 1 - 2 * (place % 2)) * 2 + core
+    deep = wq.shape[0]
+    block, part_rows = deep // 4, deep // n_rep
+    others = range(1, n_fsdp)
+    greet_all([(sib, mine), (partner, mine)] + [(rep, flipped(mine, s, n_fsdp)) for s in others])
+
+    weights = (wq, wg, wk, wv)
+    starts = [sum(widths[:i]) for i in range(4)]
+    band = (place % 2) * 2 + core
+    other_band = (1 - place % 2) * 2 + core
+
+    def gain_copy(s):
+        return remote_copy(
+            gains, gains_all.at[mine], gs.at[s], gr.at[s], rep, flipped(mine, s, n_fsdp)
+        )
+
+    def weight_copy(s, i):
+        peer = flipped(mine, s, n_fsdp)
+        cols = pl.ds(pl.multiple_of(peer * widths[i], widths[i]), widths[i])
+        return remote_copy(
+            weights[i].at[pl.ds(band * block, block), cols],
+            w_attn.at[pl.ds(mine * deep + band * block, block), pl.ds(starts[i], widths[i])],
+            ws.at[s, i],
+            wr.at[s, i],
+            rep,
+            peer,
+        )
+
+    def band_at(s, which):
+        return w_attn.at[pl.ds(flipped(mine, s, n_fsdp) * deep + which * block, block)]
+
+    def partner_copy(s):
+        return remote_copy(band_at(s, band), band_at(s, band), zs.at[s], zr.at[s], partner, mine)
+
+    def sibling_copy(s, k):
+        which = band if k == 0 else other_band
+        return remote_copy(
+            band_at(s, which), band_at(s, which), cs.at[s, k], cr.at[s, k], sib, mine
+        )
+
+    def mlp_copy(s, i):
+        peer = flipped(mine, s, n_fsdp)
+        cols = pl.ds(pl.multiple_of(peer * ff, ff), ff)
+        return remote_copy(
+            (w_gate, w_up)[i].at[pl.ds(rep * part_rows, part_rows), cols],
+            mlp_part.at[s - 1, :, pl.ds(i * ff, ff)],
+            ms.at[s, i],
+            mr.at[s, i],
+            rep,
+            peer,
+        )
+
+    def own_copy(i):
+        cols = pl.ds(pl.multiple_of(mine * widths[i], widths[i]), widths[i])
+        return pltpu.make_async_copy(
+            weights[i].at[:, cols],
+            w_attn.at[pl.ds(mine * deep, deep), pl.ds(starts[i], widths[i])],
+            ls.at[i],
+        )
+
+    own_gain = pltpu.make_async_copy(gains, gains_all.at[mine], ls.at[4])
+    rows = GatherRows(n_fsdp, rep, mine, tokens, tokens_all, (ts, tr, tl))
+    for s in others:
+        gain_copy(s).start()
+        for i in range(4):
+            weight_copy(s, i).start()
+    rows.start()
+    own_gain.start()
+    for i in range(4):
+        own_copy(i).start()
+    for s in others:
+        for i in range(4):
+            weight_copy(s, i).wait_recv()
+        partner_copy(s).start()
+        sibling_copy(s, 0).start()
+    rows.forward()
+    for s in others:
+        for i in range(2):
+            mlp_copy(s, i).start()
+    for s in others:
+        partner_copy(s).wait_recv()
+        sibling_copy(s, 1).start()
+    rows.finish()
+    for s in others:
+        gain_copy(s).wait()
+        partner_copy(s).wait_send()
+        for i in range(4):
+            weight_copy(s, i).wait_send()
+        for i in range(2):
+            sibling_copy(s, i).wait()
+            mlp_copy(s, i).wait()
+    own_gain.wait()
+    for i in range(4):
+        own_copy(i).wait()
+
+
+def fetched(n_fsdp, n_rep, widths, ff, tokens, gains, *weights):
+    deep = weights[0].shape[0]
+    rows, width = tokens.shape
+    dma = pltpu.SemaphoreType.DMA
+    any_spec = pl.BlockSpec(memory_space=pl.ANY)
+    shapes = (
+        (n_fsdp, rows, width),
+        (n_fsdp,) + gains.shape,
+        (n_fsdp * deep, sum(widths)),
+        (n_fsdp - 1, deep // n_rep, 2 * ff),
+    )
+    pair, four = dma((n_fsdp, 2)), dma((n_fsdp, 4))
+    one = dma((n_fsdp,))
+    return pl.pallas_call(
+        functools.partial(fetch_kernel, n_fsdp, n_rep, widths, ff),
+        out_shape=[jax.ShapeDtypeStruct(shape, jnp.bfloat16) for shape in shapes],
+        in_specs=[any_spec] * 8,
+        out_specs=[any_spec] * 4,
+        scratch_shapes=[
+            pair, pair, dma, one, one, four, four, one, one, pair, pair, pair, pair, dma((5,))
+        ],
+        compiler_params=pltpu.CompilerParams(collective_id=1, has_side_effects=True),
+        name="fetch",
+    )(tokens, gains, *weights)
+
+
 def gather_rows(block):
     n_fsdp = lax.axis_size("fsdp")
     if n_fsdp != 4:
@@ -552,88 +952,57 @@
     token_count = jnp.sum(lengths).astype(jnp.float32)
     factor = rows * n_rep * n_fsdp / (2.0 * token_count)
     segments, angle_cos, angle_sin = row_layout(pair_len, rows, HD)
-    row_index = jnp.arange(rows, dtype=jnp.int32)
-    allowed = (segments[:, :, None] == segments[:, None, :]) & (
-        row_index[None, None, :] <= row_index[None, :, None]
-    )
-    allowed = allowed[:, None, None]
+    angle_cos, angle_sin = angle_cos.reshape(rows_all, HD), angle_sin.reshape(rows_all, HD)
     segment = segments[0]
     valid_row = (segment < 2).astype(jnp.float32)
-    score_scale = HD ** (-0.5)
-
-    def column_parts(weights, widths):
-        def pick(start_of):
-            return jnp.concatenate(
-                [
-                    lax.dynamic_slice(w, (0, start_of * cols), (deep, cols))
-                    for w, cols in zip(weights, widths)
-                ],
-                axis=1,
-            )
-
-        return pick
-
-    def by_columns(weights, widths):
-        pick = column_parts(weights, widths)
-        half = deep // 2
-        cols = sum(widths)
-        whole = jnp.zeros((n_fsdp * deep, cols), jnp.bfloat16)
-        whole = lax.dynamic_update_slice(whole, pick(mine), (mine * deep, 0))
-        for s in others:
-            piece = lax.dynamic_slice(pick(mine ^ s), (core * half, 0), (half, cols))
-            got = shift(piece, s)
-            rest = sibling(got)
-            start = (mine ^ s) * deep
-            whole = lax.dynamic_update_slice(whole, got, (start + core * half, 0))
-            whole = lax.dynamic_update_slice(whole, rest, (start + (1 - core) * half, 0))
-        return whole
-
-    gains_own = jnp.concatenate([attention_gain, mlp_gain, query_gain, key_gain])[None]
-    gains = jnp.concatenate([gains_own] + [shift(gains_own, s) for s in others], axis=0)
-    gains = in_f32(jnp.take(gains, mine ^ jnp.arange(n_fsdp), axis=0))
+
     small = query_gain.shape[0]
+    gains_own = jnp.concatenate([attention_gain, mlp_gain, query_gain, key_gain])
+    gains_own = jnp.pad(gains_own, (0, 16 * HD - gains_own.shape[0])).reshape(16, HD)
+    tokens_all, gains, w_attn, mlp_part = fetched(
+        n_fsdp,
+        n_rep,
+        (cols_q, cols_q, cols_k, cols_k),
+        ff,
+        tokens,
+        gains_own,
+        w_query,
+        w_outgate,
+        w_key,
+        w_value,
+        w_gate,
+        w_up,
+    )
+    tokens_all = tokens_all.reshape(rows_all, width)
+    gains = in_f32(gains.reshape(n_fsdp, 16 * HD))
     attention_gain_f = gains[:, :deep].reshape(-1)
     mlp_gain_f = gains[:, deep : 2 * deep].reshape(-1)
     query_gain_f = gains[:, 2 * deep : 2 * deep + small].reshape(-1)
-    key_gain_f = gains[:, 2 * deep + small :].reshape(-1)
-
-    tokens_all = jnp.concatenate(gather_rows(tokens))
-    w_attn = by_columns((w_query, w_outgate, w_key, w_value), (cols_q, cols_q, cols_k, cols_k))
-    w_mlp = by_columns((w_gate, w_up), (ff, ff))
+    key_gain_f = gains[:, 2 * deep + small : 2 * deep + 2 * small].reshape(-1)
+
+    mlp_parts = lax.all_gather(mlp_part, "rep", axis=0)
+    w_mlp = jnp.zeros((n_fsdp * deep, 2 * ff), jnp.bfloat16)
+    for i, weight in enumerate((w_gate, w_up)):
+        own = lax.dynamic_slice(weight, (0, mine * ff), (deep, ff))
+        w_mlp = lax.dynamic_update_slice(w_mlp, own, (mine * deep, i * ff))
+    for s in others:
+        rows_of = mlp_parts[:, s - 1].reshape(deep, 2 * ff)
+        w_mlp = lax.dynamic_update_slice(w_mlp, rows_of, ((mine ^ s) * deep, 0))
 
     tokens_f = in_f32(tokens)
     normed_all = in_bf16(rms_scale(in_f32(tokens_all), attention_gain_f))
     attn_raw = times(normed_all, w_attn)
-    query_raw = attn_raw[:, :cols_q]
-    gate_raw = attn_raw[:, cols_q : 2 * cols_q]
-    key_raw = attn_raw[:, 2 * cols_q : 2 * cols_q + cols_k]
-    value_b = in_bf16(attn_raw[:, 2 * cols_q + cols_k :]).reshape(n_fsdp, rows, heads_k, HD)
-
-    def prepare_heads(query_in, key_in, query_scale, key_scale):
-        query_heads = rms_scale(query_in.reshape(n_fsdp, rows, heads_q, HD), query_scale)
-        query_heads = rotate(query_heads, angle_cos[:, :, None], angle_sin[:, :, None])
-        key_heads = rms_scale(key_in.reshape(n_fsdp, rows, heads_k, HD), key_scale)
-        key_heads = rotate(key_heads, angle_cos[:, :, None], angle_sin[:, :, None])
-        return (query_heads, key_heads)
-
-    head_pair, heads_back = jax.vjp(prepare_heads, query_raw, key_raw, query_gain_f, key_gain_f)
-    queries_b = in_bf16(head_pair[0]).reshape(n_fsdp, rows, heads_k, H // KV, HD)
-    keys_b = in_bf16(head_pair[1])
-
-    def dots(spec, left, right):
-        return jnp.einsum(spec, left, right, preferred_element_type=jnp.float32)
-
-    scores = dots("sqkgd,spkd->skgqp", queries_b, keys_b) * score_scale
-    scores = jnp.where(allowed, scores, NEG_FILL)
-    row_top = jnp.max(scores, axis=-1, keepdims=True)
-    exponent = jnp.exp(scores - row_top)
-    row_total = jnp.sum(exponent, axis=-1, keepdims=True)
-    probs_b = in_bf16(exponent / row_total)
-    log_total = row_top + jnp.log(row_total)
-    context = dots("skgqp,spkd->sqkgd", probs_b, value_b)
-    gate_heads = gate_raw.reshape(n_fsdp, rows, heads_k, H // KV, HD)
-    gated_out, gating_back = jax.vjp(gating, context, gate_heads)
-    gated_b = in_bf16(gated_out.reshape(rows_all, cols_q))
+    head_args = (
+        heads_k,
+        rows,
+        pair_len,
+        attn_raw,
+        angle_cos,
+        angle_sin,
+        query_gain_f[None],
+        key_gain_f[None],
+    )
+    queries_b, keys_b, values_b, gated_b = attend(*head_args)
 
     def summed(left, right, product):
         own = product(left[:rows], right, jnp.float32)
@@ -667,31 +1036,9 @@
     grad_middle = grad_result + grad_middle_norm
 
     grad_attn_all = jnp.concatenate(gather_rows(in_bf16(grad_middle)))
-    grad_gated = times_trans(grad_attn_all, w_output).reshape(
-        n_fsdp, rows, heads_k, H // KV, HD
-    )
-    grad_context, grad_gate_heads = gating_back(grad_gated)
-    grad_context_b = in_bf16(grad_context)
-    grad_outgate_b = in_bf16(grad_gate_heads.reshape(rows_all, cols_q))
-    scores_again = dots("sqkgd,spkd->skgqp", queries_b, keys_b) * score_scale
-    probs_again = jnp.where(allowed, jnp.exp(scores_again - log_total), 0.0)
-    grad_value = dots("skgqp,sqkgd->spkd", in_bf16(probs_again), grad_context_b)
-    grad_probs = dots("sqkgd,spkd->skgqp", grad_context_b, value_b)
-    grad_scores = probs_again * (
-        grad_probs - jnp.sum(probs_again * grad_probs, axis=-1, keepdims=True)
-    )
-    grad_scores_b = in_bf16(grad_scores)
-    grad_queries = dots("skgqp,spkd->sqkgd", grad_scores_b, keys_b) * score_scale
-    grad_keys = dots("skgqp,sqkgd->spkd", grad_scores_b, queries_b) * score_scale
-    grad_query_raw, grad_key_raw, grad_query_gain, grad_key_gain = heads_back(
-        (grad_queries.reshape(n_fsdp, rows, heads_q, HD), grad_keys)
-    )
-    grad_query_b = in_bf16(grad_query_raw)
-    grad_key_b = in_bf16(grad_key_raw)
-    grad_value_b = in_bf16(grad_value.reshape(rows_all, cols_k))
-    grad_raw_b = jnp.concatenate(
-        [grad_query_b, grad_outgate_b, grad_key_b, grad_value_b], axis=1
-    )
+    grad_gated = times_trans(grad_attn_all, w_output)
+    grad_raw_b, head_gains = attend_back(*head_args, queries_b, keys_b, values_b, grad_gated)
+    grad_query_gain, grad_key_gain = head_gains[0], head_gains[1]
     grad_normed = summed(grad_raw_b, w_attn, times_trans)
     _, norm_back = jax.vjp(rms_scale, tokens_f, attention_gain_f)
     grad_tokens_norm, grad_attention_gain = norm_back(grad_normed)

time: 1000 us -> 909 us (0.909)
  Pallas kernels: 367 us -> 484 us
  local copies, waits for them, and re-layouts: 129 us -> 49.7 us
  waiting for transfers between devices: 237 us -> 161 us
  other arithmetic: 74.8 us -> 37.8 us
  starting transfers between devices: 67 us -> 49.1 us
  matrix products: 119 us -> 103 us
  between operations: 2.97 us -> 15.8 us
    pallas_call x0 -> x3, Pallas kernels: none -> 114 us  [the longest x1 85.5 us: fetched(): pl.pallas_call(functools.partial(fetch_kernel, n_fsdp, n_rep, widths, ff)...]
    ppermute x57 -> x42, waiting for transfers between devices: 231 us -> 155 us  [shift(): return lax.ppermute(values, 'fsdp', [(i, i ^ step) for i in range(n_fsdp)])]
    reshape x9 -> x1, local copies, waits for them, and re-layouts: 26.6 us -> 0.6 us  [shards(): jnp.pad(gains_own, (0, 16 * HD - gains_own.shape[0])).reshape(16, HD)]
    ppermute x57 -> x42, starting transfers between devices: 61.3 us -> 44.9 us  [shift(): return lax.ppermute(values, 'fsdp', [(i, i ^ step) for i in range(n_fsdp)])]
    dot_general x6 -> x0, matrix products: 12.3 us -> none  [dots(): return jnp.einsum(spec, left, right, preferred_element_type=jnp.float32)]
    unnamed x173 -> x101, local copies, waits for them, and re-layouts: 29.4 us -> 17.2 us
    convert_element_type x13 -> x6, other arithmetic: 23.2 us -> 12.6 us  [in_bf16(): return values.astype(jnp.bfloat16)]
  transfers between devices with their start and end apart: 68 -> 48, of which waited for: 36 -> 33; matrix products, arithmetic and copies ran while one was open for 16% -> 7% of each run, Pallas kernels for 37% -> 42%
where the time goes in v3:
time: 909 us; the launch traced here: 901 us
  Pallas kernels  484 us (53%)
  waiting for transfers between devices  161 us (18%)
  matrix products  103 us (11%)
  local copies, waits for them, and re-layouts  49.7 us (5%)
  starting transfers between devices  49.1 us (5%)
  other arithmetic  37.8 us (4%)
  between operations  15.8 us (2%)
    pallas_call x1, Pallas kernels, reduced(): pl.pallas_call(functools.partial(reduce_kernel, n_fsdp, n_rep, units, pie...  332 us
    ppermute x42, waiting for transfers between devices, shift(): return lax.ppermute(values, 'fsdp', [(i, i ^ step) for i in range(n_fsdp)])  155 us
    pallas_call x1, Pallas kernels, fetched(): pl.pallas_call(functools.partial(fetch_kernel, n_fsdp, n_rep, widths, ff)...  85.5 us
    dot_general x6, matrix products, times_trans(): lax.dot_general(left_side, right_side, (((1,), (1,)), ((), ())), preferre...  56.2 us
    dot_general x7, matrix products, times(): jnp.dot(left_side, right_side, preferred_element_type=jnp.float32)  47 us
    ppermute x42, starting transfers between devices, shift(): return lax.ppermute(values, 'fsdp', [(i, i ^ step) for i in range(n_fsdp)])  44.9 us
    pallas_call x4, Pallas kernels, widened(): pl.pallas_call(widen_kernel, grid=grid, out_shape=jax.ShapeDtypeStruct(sh...  29.4 us
  transfers between devices with their start and end apart: 48, of which 33 were waited for; matrix products, arithmetic and copies ran while one was open for 7% of the time, Pallas kernels for 42%

profile of v3, /device:TPU:0, one launch (start us, length us, event | category | flops | bytes accessed | tf_op | source)
XLA Modules:
  0.0 900.6 jit_solution(6989291961645011673)
XLA Ops:
  10.8 85.5 %fetch.1 = (bf16[4,256,2048]{2,1,0:T(8,128)(2,1)}, bf16[4,16,128]{2,1,0:T(8,128)(2,1)}, bf16[2048,1536]{1,0:T(8,128)(2,1)}, bf16[3,64,3072]{2,1,0:T(8,128)(2,1)}) custom-call(bf16[256,2048]{1,0:T(8,128)(2,1)} %refs_0_.1, bf16[16,128]{1,0:T(8,128)(2,1)} %pad_bitcast_fusion.refs_1_, bf16[512,2048]{1,0:T(8,128)(2,1)} %refs_2_.1, bf16[512,2048]{1,0:T(8,128)(2,1)} %refs_3_.1, ...), custom_call_target="tpu_custom_call" | custom-call | tf_op jit(solution)/shard_map/fetch/pallas_call | solution.py:863
  109.8 6.6 fusion.64.raw_ref
  116.4 12.8 %attend.1 = (bf16[1024,512]{1,0:T(8,128)(2,1)S(1)}, bf16[1024,256]{1,0:T(8,128)(2,1)S(1)}, bf16[1024,256]{1,0:T(8,128)(2,1)S(1)}, bf16[1024,512]{1,0:T(8,128)(2,1)S(1)}) custom-call(s32[4,2]{1,0:T(4,128)S(1)} %reshape.230.pair_ref, f32[1024,1536]{1,0:T(8,128)S(1)} %fusion.64.raw_ref, f32[1024,128]{1,0:T(8,128)S(1)} %pad_maximum_fusion.1.cos_ref, ...), custom_call_target="tpu_custom_call" | custom-call | flops 536870912 | bytes 12582912 | tf_op jit(solution)/shard_map/attend/pallas_call | solution.py:615
  134.6 10.7 %collective-permute-done.1 = bf16[128,2048]{1,0:T(8,128)(2,1)S(1)} collective-permute-done((bf16[128,2048]{1,0:T(8,128)(2,1)S(1)}, bf16[128,2048]{1,0:T(8,128)(2,1)S(1)}, u32[]{:S(2)}, u32[]{:S(2)}) %collective-permute-start.1) | collective-permute-done | bytes 524320 | tf_op jit(solution)/shard_map/ppermute | solution.py:75
  152.4 6.4 collective-permute-done.3
  223.9 10.5 %fusion.7 = f32[1024,1536]{1,0:T(8,128)} fusion(bf16[1024,2048]{1,0:T(8,128)(2,1)S(1)} %copy-done.24, bf16[2048,3072]{1,0:T(8,128)(2,1)} %constant_dynamic-update-slice_fusion.21), kind=kOutput, calls=%fused_computation.15 | convolution fusion | flops 6442450944 | bytes 16777216 | tf_op jit(solution)/shard_map/dot_general | solution.py:46
  234.5 10.7 %multiply_convert_fusion.1 = (bf16[1024,1536]{1,0:T(8,128)(2,1)S(1)}, f32[1024,1536]{1,0:T(8,128)}) fusion(f32[1024,1536]{1,0:T(8,128)} %fusion.7, bf16[1024,2048]{1,0:T(8,128)(2,1)S(1)} %copy-done.24, bf16[2048,3072]{1,0:T(8,128)(2,1)S(1)} %copy-done.15), kind=kOutput, calls=%fused_computation.18 | convolution fusion | flops 6451888128 | bytes 26214400 | tf_op jit(solution)/shard_map/dot_general | solution.py:46
  245.2 9.1 %convolution_convert_fusion.2 = bf16[768,2048]{1,0:T(8,128)(2,1)S(1)} fusion(bf16[1536,2048]{1,0:T(8,128)(2,1)} %param.31, bf16[1024,1536]{1,0:T(8,128)(2,1)S(1)} %get-tuple-element.107.refs_0_), kind=kOutput, calls=%fused_computation.31 | convolution fusion | flops 4833411072 | bytes 11796480 | tf_op jit(solution)/shard_map/dot_general | solution.py:46
  258.5 6.8 collective-permute-done.13
  300.6 10.8 %collective-permute-done.18 = bf16[128,2048]{1,0:T(8,128)(2,1)S(1)} collective-permute-done((bf16[128,2048]{1,0:T(8,128)(2,1)S(1)}, bf16[128,2048]{1,0:T(8,128)(2,1)S(1)}, u32[]{:S(2)}, u32[]{:S(2)}) %collective-permute-start.18) | collective-permute-done | bytes 524320 | tf_op jit(solution)/shard_map/ppermute | solution.py:75
  313.5 8.3 collective-permute-done.19
  328.1 16.3 %multiply_convert_fusion = (bf16[1024,1536]{1,0:T(8,128)(2,1)S(1)}, bf16[1024,1536]{1,0:T(8,128)(2,1)}) fusion(f32[1024,1536]{1,0:T(8,128)} %fusion.7, f32[1024,1536]{1,0:T(8,128)} %get-tuple-element.108, bf16[1024,2048]{1,0:T(8,128)(2,1)S(1)} %constant_dynamic-update-slice_fusion.7.refs_4_, bf16[1536,2048]{1,0:T(8,128)(2,1)} %param.31), kind=kOutput, calls=%fused_computation.17 | convolution fusion | flops 6464471040 | bytes 29360128 | tf_op jit(solution)/shard_map/dot_general | solution.py:50
  344.4 15.2 %fusion.13 = bf16[768,2048]{1,0:T(8,128)(2,1)S(1)} fusion(bf16[2048,3072]{1,0:T(8,128)(2,1)} %constant_dynamic-update-slice_fusion.21, bf16[1024,1536]{1,0:T(8,128)(2,1)} %get-tuple-element.57, bf16[1024,1536]{1,0:T(8,128)(2,1)S(1)} %get-tuple-element.56), kind=kOutput, calls=%fused_computation.28 | convolution fusion | flops 9674686464 | bytes 22020096 | tf_op jit(solution)/shard_map/dot_general | solution.py:50
  363.0 9.9 %collective-permute-done.25 = bf16[128,2048]{1,0:T(8,128)(2,1)S(1)} collective-permute-done((bf16[128,2048]{1,0:T(8,128)(2,1)S(1)}, bf16[128,2048]{1,0:T(8,128)(2,1)S(1)}, u32[]{:S(2)}, u32[]{:S(2)}) %collective-permute-start.25) | collective-permute-done | bytes 524320 | tf_op jit(solution)/shard_map/ppermute | solution.py:75
  392.6 10.5 %multiply_reduce_fusion.1 = (f32[2048]{0:T(1024)S(1)}, f32[256]{0:T(256)S(1)}, f32[256,2048]{1,0:T(8,128)}) fusion(f32[256,2048]{1,0:T(8,128)S(1)} %copy-done.12, f32[256]{0:T(256)S(1)} %fusion.48, f32[2048]{0:T(1024)S(1)} %bitcast.76, f32[128,2048]{1,0:T(8,128)S(1)} %convert_add_fusion.3, f32[128,2048]{1,0:T(8,128)} %convert_add_fusion.4, ...), kind=kOutput, calls=%fused_computation.48 | convolution fusion | flops 3228563200 | bytes 25184256 | tf_op jit(solution)/shard_map/dot_general | solution.py:50
  411.9 10.8 %collective-permute-done.30 = bf16[128,2048]{1,0:T(8,128)(2,1)S(1)} collective-permute-done((bf16[128,2048]{1,0:T(8,128)(2,1)S(1)}, bf16[128,2048]{1,0:T(8,128)(2,1)S(1)}, u32[]{:S(2)}, u32[]{:S(2)}) %collective-permute-start.30) | collective-permute-done | bytes 524320 | tf_op jit(solution)/shard_map/ppermute | solution.py:75
  440.6 16.0 %attend_back.1 = (bf16[1024,1536]{1,0:T(8,128)(2,1)S(1)}, f32[8,128]{1,0:T(8,128)S(1)}) custom-call(s32[4,2]{1,0:T(4,128)S(1)} %reshape.230.pair_ref, f32[1024,1536]{1,0:T(8,128)S(1)} %bitcast.65, f32[1024,128]{1,0:T(8,128)S(1)} %pad_maximum_fusion.1.cos_ref, f32[1024,128]{1,0:T(8,128)S(1)} %pad_maximum_fusion.2.sin_ref, ...), custom_call_target="tpu_custom_call" | custom-call | flops 1879048192 | bytes 15728640 | tf_op jit(solution)/shard_map/attend_back/pallas_call | solution.py:643
  468.0 11.2 %collective-permute-done.37 = bf16[128,2048]{1,0:T(8,128)(2,1)S(1)} collective-permute-done((bf16[128,2048]{1,0:T(8,128)(2,1)}, bf16[128,2048]{1,0:T(8,128)(2,1)S(1)}, u32[]{:S(2)}, u32[]{:S(2)}) %collective-permute-start.37) | collective-permute-done | bytes 524320 | tf_op jit(solution)/shard_map/ppermute | solution.py:75
  497.2 6.5 fusion.24
  512.6 331.8 %reduce_weight_gradients.1.query_in.gate_in.pair_in.in_ref = bf16[52,2,256,512]{3,2,1,0:T(8,128)(2,1)} custom-call(bf16[1024,1536]{1,0:T(8,128)(2,1)} %copy-done.31, bf16[1024,2048]{1,0:T(8,128)(2,1)} %constant_dynamic-update-slice_fusion.refs_1_, bf16[1024,512]{1,0:T(8,128)(2,1)} %copy-done.9, bf16[1024,2048]{1,0:T(8,128)(2,1)} %copy-done.17, ...), custom_call_target="tpu_custom_call" | custom-call | flops 27917287424 | bytes 1073741824 | tf_op jit(solution)/shard_map/reduce_weight_gradients/pallas_call | solution.py:398
  844.4 8.7 widen_heads.1
  856.4 8.8 widen.5
  865.3 8.8 widen.6
  874.1 8.3 widen.7
  (274 shorter events, 243.7 us)
Async XLA Ops:
  7.2 205.5 %all-gather.3.cloned.1.call-start = ((), (), s32[]{:S(2)}) async-start(), calls=%async_computation | async-start | bytes 10616832 | tf_op jit(solution)/shard_map/all_gather | solution.py:983
  134.1 24.7 %collective-permute-start.3 = (bf16[128,2048]{1,0:T(8,128)(2,1)}, bf16[128,2048]{1,0:T(8,128)(2,1)}, u32[]{:S(2)}, u32[]{:S(2)}) collective-permute-start(bf16[128,2048]{1,0:T(8,128)(2,1)} %get-tuple-element.81), channel_id=1, source_target_pairs={{0,2},{1,3},{2,0},{3,1},{4,6},{5,7},{6,4},{7,5},{8,10},{9,11},{10,... | collective-permute-start | bytes 1572872 | tf_op jit(solution)/shard_map/ppermute | solution.py:75
  148.8 15.2 %collective-permute-start.5 = (bf16[128,2048]{1,0:T(8,128)(2,1)}, bf16[128,2048]{1,0:T(8,128)(2,1)}, u32[]{:S(2)}, u32[]{:S(2)}) collective-permute-start(bf16[128,2048]{1,0:T(8,128)(2,1)} %get-tuple-element.84), channel_id=1, source_target_pairs={{0,1},{1,0},{2,3},{3,2},{4,5},{5,4},{6,7},{7,6},{8,9},{9,8},{10,11... | collective-permute-start | bytes 1572872 | tf_op jit(solution)/shard_map/ppermute | solution.py:75
  150.5 20.5 %collective-permute-start = (bf16[128,2048]{1,0:T(8,128)(2,1)}, bf16[128,2048]{1,0:T(8,128)(2,1)}, u32[]{:S(2)}, u32[]{:S(2)}) collective-permute-start(bf16[128,2048]{1,0:T(8,128)(2,1)} %get-tuple-element.79), channel_id=1, source_target_pairs={{0,1},{1,0},{2,3},{3,2},{4,5},{5,4},{6,7},{7,6},{8,9},{9,8},{10,11... | collective-permute-start | bytes 1572872 | tf_op jit(solution)/shard_map/ppermute | solution.py:75
  150.8 20.1 %collective-permute-start.2 = (bf16[128,2048]{1,0:T(8,128)(2,1)}, bf16[128,2048]{1,0:T(8,128)(2,1)}, u32[]{:S(2)}, u32[]{:S(2)}) collective-permute-start(bf16[128,2048]{1,0:T(8,128)(2,1)} %get-tuple-element.83), channel_id=1, source_target_pairs={{0,2},{1,3},{2,0},{3,1},{4,6},{5,7},{6,4},{7,5},{8,10},{9,11},{10,... | collective-permute-start | bytes 1572872 | tf_op jit(solution)/shard_map/ppermute | solution.py:75
  177.8 26.9 %collective-permute-start.7 = (bf16[128,2048]{1,0:T(8,128)(2,1)}, bf16[128,2048]{1,0:T(8,128)(2,1)}, u32[]{:S(2)}, u32[]{:S(2)}) collective-permute-start(bf16[128,2048]{1,0:T(8,128)(2,1)} %get-tuple-element.91), channel_id=1, source_target_pairs={{0,1},{1,0},{2,3},{3,2},{4,5},{5,4},{6,7},{7,6},{8,9},{9,8},{10,11... | collective-permute-start | bytes 1572872 | tf_op jit(solution)/shard_map/ppermute | solution.py:75
  178.8 23.6 %collective-permute-start.9 = (bf16[128,2048]{1,0:T(8,128)(2,1)}, bf16[128,2048]{1,0:T(8,128)(2,1)}, u32[]{:S(2)}, u32[]{:S(2)}) collective-permute-start(bf16[128,2048]{1,0:T(8,128)(2,1)} %get-tuple-element.91), channel_id=1, source_target_pairs={{0,2},{1,3},{2,0},{3,1},{4,6},{5,7},{6,4},{7,5},{8,10},{9,11},{10,... | collective-permute-start | bytes 1572872 | tf_op jit(solution)/shard_map/ppermute | solution.py:75
  179.9 20.0 %collective-permute-start.6 = (bf16[128,2048]{1,0:T(8,128)(2,1)}, bf16[128,2048]{1,0:T(8,128)(2,1)}, u32[]{:S(2)}, u32[]{:S(2)}) collective-permute-start(bf16[128,2048]{1,0:T(8,128)(2,1)} %get-tuple-element.92), channel_id=1, source_target_pairs={{0,1},{1,0},{2,3},{3,2},{4,5},{5,4},{6,7},{7,6},{8,9},{9,8},{10,11... | collective-permute-start | bytes 1572872 | tf_op jit(solution)/shard_map/ppermute | solution.py:75
  190.4 16.2 %collective-permute-start.8 = (bf16[128,2048]{1,0:T(8,128)(2,1)}, bf16[128,2048]{1,0:T(8,128)(2,1)}, u32[]{:S(2)}, u32[]{:S(2)}) collective-permute-start(bf16[128,2048]{1,0:T(8,128)(2,1)} %get-tuple-element.92), channel_id=1, source_target_pairs={{0,2},{1,3},{2,0},{3,1},{4,6},{5,7},{6,4},{7,5},{8,10},{9,11},{10,... | collective-permute-start | bytes 1572872 | tf_op jit(solution)/shard_map/ppermute | solution.py:75
  257.9 24.8 %collective-permute-start.15 = (bf16[128,2048]{1,0:T(8,128)(2,1)}, bf16[128,2048]{1,0:T(8,128)(2,1)}, u32[]{:S(2)}, u32[]{:S(2)}) collective-permute-start(bf16[128,2048]{1,0:T(8,128)(2,1)} %get-tuple-element.75), channel_id=1, source_target_pairs={{0,2},{1,3},{2,0},{3,1},{4,6},{5,7},{6,4},{7,5},{8,10},{9,11},{10,... | collective-permute-start | bytes 1572872 | tf_op jit(solution)/shard_map/ppermute | solution.py:75
  296.5 14.9 %collective-permute-start.18 = (bf16[128,2048]{1,0:T(8,128)(2,1)S(1)}, bf16[128,2048]{1,0:T(8,128)(2,1)S(1)}, u32[]{:S(2)}, u32[]{:S(2)}) collective-permute-start(bf16[128,2048]{1,0:T(8,128)(2,1)S(1)} %get-tuple-element.90), channel_id=1, source_target_pairs={{0,1},{1,0},{2,3},{3,2},{4,5},{5,4},{6,7},{7,6},{8,9},{9,8},{10,11... | collective-permute-start | bytes 1572872 | tf_op jit(solution)/shard_map/ppermute | solution.py:75
  297.5 15.2 %collective-permute-start.21 = (bf16[128,2048]{1,0:T(8,128)(2,1)S(1)}, bf16[128,2048]{1,0:T(8,128)(2,1)S(1)}, u32[]{:S(2)}, u32[]{:S(2)}) collective-permute-start(bf16[128,2048]{1,0:T(8,128)(2,1)S(1)} %get-tuple-element.89), channel_id=1, source_target_pairs={{0,2},{1,3},{2,0},{3,1},{4,6},{5,7},{6,4},{7,5},{8,10},{9,11},{10,... | collective-permute-start | bytes 1572872 | tf_op jit(solution)/shard_map/ppermute | solution.py:75
  298.2 23.6 %collective-permute-start.19 = (bf16[128,2048]{1,0:T(8,128)(2,1)S(1)}, bf16[128,2048]{1,0:T(8,128)(2,1)S(1)}, u32[]{:S(2)}, u32[]{:S(2)}) collective-permute-start(bf16[128,2048]{1,0:T(8,128)(2,1)S(1)} %get-tuple-element.89), channel_id=1, source_target_pairs={{0,1},{1,0},{2,3},{3,2},{4,5},{5,4},{6,7},{7,6},{8,9},{9,8},{10,11... | collective-permute-start | bytes 1572872 | tf_op jit(solution)/shard_map/ppermute | solution.py:75
  299.9 22.5 %collective-permute-start.20 = (bf16[128,2048]{1,0:T(8,128)(2,1)S(1)}, bf16[128,2048]{1,0:T(8,128)(2,1)S(1)}, u32[]{:S(2)}, u32[]{:S(2)}) collective-permute-start(bf16[128,2048]{1,0:T(8,128)(2,1)S(1)} %get-tuple-element.90), channel_id=1, source_target_pairs={{0,2},{1,3},{2,0},{3,1},{4,6},{5,7},{6,4},{7,5},{8,10},{9,11},{10,... | collective-permute-start | bytes 1572872 | tf_op jit(solution)/shard_map/ppermute | solution.py:75
  311.4 16.5 %collective-permute-start.22 = (bf16[128,2048]{1,0:T(8,128)(2,1)S(1)}, bf16[128,2048]{1,0:T(8,128)(2,1)S(1)}, u32[]{:S(2)}, u32[]{:S(2)}) collective-permute-start(bf16[128,2048]{1,0:T(8,128)(2,1)S(1)} %collective-permute-done.18), channel_id=1, source_target_pairs={{0,2},{1,3},{2,0},{3,1},{4,6},{5,7},{6,4},{7,5},{8,10},{9,11},{10,... | collective-permute-start | bytes 1572872 | tf_op jit(solution)/shard_map/ppermute | solution.py:75
  312.7 15.3 %collective-permute-start.23 = (bf16[128,2048]{1,0:T(8,128)(2,1)S(1)}, bf16[128,2048]{1,0:T(8,128)(2,1)S(1)}, u32[]{:S(2)}, u32[]{:S(2)}) collective-permute-start(bf16[128,2048]{1,0:T(8,128)(2,1)S(1)} %collective-permute-done.21), channel_id=1, source_target_pairs={{0,1},{1,0},{2,3},{3,2},{4,5},{5,4},{6,7},{7,6},{8,9},{9,8},{10,11... | collective-permute-start | bytes 1572872 | tf_op jit(solution)/shard_map/ppermute | solution.py:75
  361.0 14.9 %collective-permute-start.28 = (bf16[128,2048]{1,0:T(8,128)(2,1)S(1)}, bf16[128,2048]{1,0:T(8,128)(2,1)S(1)}, u32[]{:S(2)}, u32[]{:S(2)}) collective-permute-start(bf16[128,2048]{1,0:T(8,128)(2,1)S(1)} %get-tuple-element.68), channel_id=1, source_target_pairs={{0,2},{1,3},{2,0},{3,1},{4,6},{5,7},{6,4},{7,5},{8,10},{9,11},{10,... | collective-permute-start | bytes 1572872 | tf_op jit(solution)/shard_map/ppermute | solution.py:75
  362.1 22.5 %collective-permute-start.27 = (bf16[128,2048]{1,0:T(8,128)(2,1)S(1)}, bf16[128,2048]{1,0:T(8,128)(2,1)S(1)}, u32[]{:S(2)}, u32[]{:S(2)}) collective-permute-start(bf16[128,2048]{1,0:T(8,128)(2,1)S(1)} %get-tuple-element.69), channel_id=1, source_target_pairs={{0,2},{1,3},{2,0},{3,1},{4,6},{5,7},{6,4},{7,5},{8,10},{9,11},{10,... | collective-permute-start | bytes 1572872 | tf_op jit(solution)/shard_map/ppermute | solution.py:75
  407.8 14.9 %collective-permute-start.30 = (bf16[128,2048]{1,0:T(8,128)(2,1)S(1)}, bf16[128,2048]{1,0:T(8,128)(2,1)S(1)}, u32[]{:S(2)}, u32[]{:S(2)}) collective-permute-start(bf16[128,2048]{1,0:T(8,128)(2,1)S(1)} %get-tuple-element.88), channel_id=1, source_target_pairs={{0,1},{1,0},{2,3},{3,2},{4,5},{5,4},{6,7},{7,6},{8,9},{9,8},{10,11... | collective-permute-start | bytes 1572872 | tf_op jit(solution)/shard_map/ppermute | solution.py:75
  410.2 19.3 %collective-permute-start.31 = (bf16[128,2048]{1,0:T(8,128)(2,1)S(1)}, bf16[128,2048]{1,0:T(8,128)(2,1)S(1)}, u32[]{:S(2)}, u32[]{:S(2)}) collective-permute-start(bf16[128,2048]{1,0:T(8,128)(2,1)S(1)} %get-tuple-element.87), channel_id=1, source_target_pairs={{0,1},{1,0},{2,3},{3,2},{4,5},{5,4},{6,7},{7,6},{8,9},{9,8},{10,11... | collective-permute-start | bytes 1572872 | tf_op jit(solution)/shard_map/ppermute | solution.py:75
  410.7 19.2 %collective-permute-start.32 = (bf16[128,2048]{1,0:T(8,128)(2,1)S(1)}, bf16[128,2048]{1,0:T(8,128)(2,1)S(1)}, u32[]{:S(2)}, u32[]{:S(2)}) collective-permute-start(bf16[128,2048]{1,0:T(8,128)(2,1)S(1)} %get-tuple-element.88), channel_id=1, source_target_pairs={{0,2},{1,3},{2,0},{3,1},{4,6},{5,7},{6,4},{7,5},{8,10},{9,11},{10,... | collective-permute-start | bytes 1572872 | tf_op jit(solution)/shard_map/ppermute | solution.py:75
  464.2 14.9 %collective-permute-start.37 = (bf16[128,2048]{1,0:T(8,128)(2,1)}, bf16[128,2048]{1,0:T(8,128)(2,1)S(1)}, u32[]{:S(2)}, u32[]{:S(2)}) collective-permute-start(bf16[128,2048]{1,0:T(8,128)(2,1)} %get-tuple-element.64), channel_id=1, source_target_pairs={{0,1},{1,0},{2,3},{3,2},{4,5},{5,4},{6,7},{7,6},{8,9},{9,8},{10,11... | collective-permute-start | bytes 1572872 | tf_op jit(solution)/shard_map/ppermute | solution.py:75
  466.8 19.2 %collective-permute-start.39 = (bf16[128,2048]{1,0:T(8,128)(2,1)}, bf16[128,2048]{1,0:T(8,128)(2,1)S(1)}, u32[]{:S(2)}, u32[]{:S(2)}) collective-permute-start(bf16[128,2048]{1,0:T(8,128)(2,1)} %get-tuple-element.63), channel_id=1, source_target_pairs={{0,2},{1,3},{2,0},{3,1},{4,6},{5,7},{6,4},{7,5},{8,10},{9,11},{10,... | collective-permute-start | bytes 1572872 | tf_op jit(solution)/shard_map/ppermute | solution.py:75
  512.5 370.0 %collective-permute-start.44 = (f32[1,4352]{1,0:T(1,128)S(1)}, f32[1,4352]{1,0:T(1,128)S(1)}, u32[]{:S(2)}, u32[]{:S(2)}) collective-permute-start(f32[1,4352]{1,0:T(1,128)S(1)} %add.247), channel_id=1, source_target_pairs={{0,4},{4,0},{8,12},{12,8},{16,20},{20,16},{24,28},{28,24},{1,5},{5... | collective-permute-start | bytes 52232 | tf_op jit(solution)/shard_map/ppermute | solution.py:88
  (62 other events, 909.9 us)
Sparse Core Ops, SparseCore 0:
  96.4 90.0 all-gather.2

commit v4 on v3

--- a/solution.py
+++ b/solution.py
@@ -115,14 +115,34 @@
 RING = 4
 
 
-def reduce_kernel(
-    n_fsdp, n_rep, units, piece_rows, piece_cols, *refs
-):
-    lefts, rights = refs[: len(units)], refs[len(units) : 2 * len(units)]
-    out = refs[2 * len(units)]
-    (lm, lo, rh, sb, kb, r1, inb, xb) = refs[2 * len(units) + 1 : 2 * len(units) + 9]
-    (tile_sem, r1s, r1r, ins, inr, xs, xr, os_, fs, fr, gs, gr, ls) = refs[2 * len(units) + 9 :]
+ROW_STEP = 32
+TILES = 8
+
+
+def norm_back(grad, raw, gain):
+    scale = lax.rsqrt(jnp.mean(raw * raw, axis=-1, keepdims=True) + EPS_NORM)
+    unit = raw * scale
+    inner = grad * gain
+    return scale * (inner - unit * jnp.mean(inner * unit, axis=-1, keepdims=True)), grad * unit
+
+
+def backward_kernel(n_fsdp, n_rep, heads_k, units, piece_rows, piece_cols, *refs):
+    (hidden, normed_mlp, gated, normed, grad_branch, grad_mlp, w_mlp, w_output, w_attn) = refs[:9]
+    (middle, grad_result, tokens, attn_raw, all_cos, all_sin, all_q, all_k, all_v) = refs[9:18]
+    (gains, head_gains, pair_ref) = refs[18:21]
+    (out, grad_attn, grad_raw, inb, xb, tokens_grad, gain_out, head_gain_out) = refs[21:29]
+    (lm, lo, rh, sb, kb, r1, c_slot, d_slot, big, wt, own, pbuf, land_a, land_b) = refs[29:43]
+    (mid, gres, tok, ga, wo, raw, cs, sn, qb, kvb, vb, gb, gg, ob) = refs[43:57]
+    (tile_sem, r1s, r1r, ins, inr, xs, xr, os_, fs, fr, gs, gr, ls) = refs[57:70]
+    (load_sem, first_sem, wt_sem, ps, pr, qs, qr, ag_s, ag_r, ag_l, block_sem) = refs[70:]
+    lefts = (hidden, normed_mlp, gated, normed)
+    rights = (grad_branch, grad_mlp, grad_attn, grad_raw)
     total = sum(unit.count for unit in units)
+    rows, width = own.shape
+    rows_all = n_fsdp * rows
+    ff = grad_mlp.shape[1] // 2
+    tile = width // TILES
+    others = range(1, n_fsdp)
     rep, mine = lax.axis_index("rep"), lax.axis_index("fsdp")
     core, place = rep % 2, rep // 2
     n_line = n_rep // 2
@@ -132,17 +152,19 @@
     inward = (place + 1 - 2 * side) * 2 + core
     outward = (place - 1 + 2 * side) * 2 + core
     sib = rep + 1 - 2 * core
-    middle = depth == half - 1
+    at_middle = depth == half - 1
 
     barrier = pltpu.get_barrier_semaphore()
 
-    def greet(device):
-        pl.semaphore_signal(barrier, inc=1, device_id=device, device_id_type=MESH)
-
-    greet({"rep": sib, "fsdp": mine})
-    greet({"rep": inward, "fsdp": mine})
-    for s in range(1, n_fsdp):
-        greet({"rep": rep, "fsdp": flipped(mine, s, n_fsdp)})
+    def greet(to_rep, to_fsdp):
+        pl.semaphore_signal(
+            barrier, inc=1, device_id={"rep": to_rep, "fsdp": to_fsdp}, device_id_type=MESH
+        )
+
+    greet(sib, mine)
+    greet(inward, mine)
+    for s in others:
+        greet(rep, flipped(mine, s, n_fsdp))
 
     @pl.when(depth == 0)
     def _():
@@ -150,58 +172,48 @@
 
     @pl.when(depth > 0)
     def _():
-        greet({"rep": outward, "fsdp": mine})
+        greet(outward, mine)
         pl.semaphore_wait(barrier, 2 + n_fsdp)
 
-    def remote(src, dst, send, recv, to_rep, to_fsdp):
-        return pltpu.make_async_remote_copy(
-            src_ref=src,
-            dst_ref=dst,
-            send_sem=send,
-            recv_sem=recv,
-            device_id={"rep": to_rep, "fsdp": to_fsdp},
-            device_id_type=MESH,
-        )
 
     def r1_copy(p):
-        return remote(sb.at[p % RING], r1.at[p], r1s.at[p], r1r.at[p], sib, mine)
+        return remote_copy(sb.at[p % RING], r1.at[p], r1s.at[p], r1r.at[p], sib, mine)
 
     def in_copy(p):
-        return remote(r1.at[p], inb.at[p], ins.at[p], inr.at[p], inward, mine)
+        return remote_copy(r1.at[p], inb.at[p], ins.at[p], inr.at[p], inward, mine)
 
     def x_copy(p):
-        return remote(r1.at[p], xb.at[p], xs.at[p], xr.at[p], inward, mine)
+        return remote_copy(r1.at[p], xb.at[p], xs.at[p], xr.at[p], inward, mine)
 
     def o_copy(p, src):
-        return remote(src.at[p], xb.at[p], os_.at[p], xr.at[p], outward, mine)
+        return remote_copy(src.at[p], xb.at[p], os_.at[p], xr.at[p], outward, mine)
+
+    def inside_of(p, unit):
+        inside = at_least(p, unit.base, total - unit.base)
+        stop = unit.base + unit.count
+        if stop < total:
+            inside = inside * (1 - at_least(p, stop, total - stop))
+        return inside
 
     def owner_of(p):
-        step, place_at, keep = 0, p, 1
-        for u, unit in enumerate(units):
+        step = 0
+        for unit in units:
             if unit.by_owner:
-                inside = at_least(p, unit.base, total - unit.base)
-                if unit.base + unit.count < total:
-                    stop = unit.base + unit.count
-                    inside = inside * (1 - at_least(p, stop, total - stop))
                 i = p - unit.base
-                step = step + inside * (n_fsdp - 1 - i // unit.col_blocks)
+                step = step + inside_of(p, unit) * (n_fsdp - 1 - i // unit.col_blocks)
         return step
 
     def spot(p, source):
         where = p
         for unit in units:
             if unit.by_owner:
-                inside = at_least(p, unit.base, total - unit.base)
-                if unit.base + unit.count < total:
-                    stop = unit.base + unit.count
-                    inside = inside * (1 - at_least(p, stop, total - stop))
                 i = p - unit.base
                 spread = unit.base + source * unit.col_blocks + i % unit.col_blocks
-                where = where + inside * (spread - p)
+                where = where + inside_of(p, unit) * (spread - p)
         return where
 
     def f_copy(p, step):
-        return remote(
+        return remote_copy(
             r1.at[p],
             out.at[spot(p, mine), core],
             fs.at[p],
@@ -211,15 +223,48 @@
         )
 
     def g_copy(p, src, where):
-        return remote(src, out.at[where, core], gs.at[p], gr.at[p], sib, mine)
+        return remote_copy(src, out.at[where, core], gs.at[p], gr.at[p], sib, mine)
 
     def l_copy(p):
         return pltpu.make_async_copy(r1.at[p], out.at[spot(p, mine), core], ls.at[p])
 
+    def c_load(p):
+        return pltpu.make_async_copy(inb.at[p], c_slot, load_sem.at[0])
+
+    def d_load(p):
+        return pltpu.make_async_copy(xb.at[p], d_slot, load_sem.at[1])
+
+    def e_load(p):
+        return pltpu.make_async_copy(xb.at[p], r1.at[p], load_sem.at[2])
+
     def add_into(p, other):
-        r1[p] = (r1[p].astype(jnp.float32) + other.astype(jnp.float32)).astype(jnp.bfloat16)
-
-    def stage_b(p):
+        r1[p] = in_bf16(in_f32(r1[p]) + in_f32(other))
+
+    def begin_c(p):
+        @pl.when(depth > 0)
+        def _():
+            in_copy(p).wait_recv()
+            c_load(p).start()
+
+    def begin_d(p):
+        @pl.when(at_middle)
+        def _():
+            x_copy(p).wait_recv()
+            d_load(p).start()
+
+    def begin_e(p):
+        @pl.when(depth < half - 1)
+        def _():
+            o_copy(p, xb).wait_recv()
+
+            @pl.when(depth > 0)
+            def _():
+                o_copy(p, xb).start()
+
+            in_copy(p).wait_send()
+            e_load(p).start()
+
+    def end_b(p):
         r1_copy(p).wait_recv()
         add_into(p, kb[p % RING])
         if half > 1:
@@ -230,41 +275,35 @@
         else:
             x_copy(p).start()
 
-    def stage_c(p):
+    def end_c(p):
         @pl.when(depth > 0)
         def _():
-            in_copy(p).wait_recv()
-            add_into(p, inb[p])
+            c_load(p).wait()
+            add_into(p, c_slot[...])
 
             @pl.when(depth < half - 1)
             def _():
                 in_copy(p).start()
 
-            @pl.when(middle)
+            @pl.when(at_middle)
             def _():
                 x_copy(p).start()
 
-    def stage_d(p):
-        @pl.when(middle)
-        def _():
-            x_copy(p).wait()
-            add_into(p, xb[p])
+    def end_d(p):
+        @pl.when(at_middle)
+        def _():
+            d_load(p).wait()
+            x_copy(p).wait_send()
+            add_into(p, d_slot[...])
 
             @pl.when(depth > 0)
             def _():
                 o_copy(p, r1).start()
 
-    def stage_e(p):
+    def end_e(p):
         @pl.when(depth < half - 1)
         def _():
-            o_copy(p, xb).wait_recv()
-
-            @pl.when(depth > 0)
-            def _():
-                o_copy(p, xb).start()
-
-            in_copy(p).wait_send()
-            r1[p] = xb[p]
+            e_load(p).wait()
 
         step = owner_of(p)
 
@@ -277,7 +316,7 @@
         def _():
             f_copy(p, step).start()
 
-    def stage_g(p):
+    def end_g(p):
         step = owner_of(p)
 
         @pl.when(step > 0)
@@ -286,11 +325,15 @@
             where = spot(p, flipped(mine, step, n_fsdp))
             g_copy(p, out.at[where, core], where).start()
 
-    stages = [(LAG_B, stage_b), (LAG_C, stage_c), (LAG_D, stage_d), (LAG_E, stage_e), (LAG_G, stage_g)]
-
-    def service(t):
+    def run(stages, t):
         for lag, stage in stages:
             pl.when((t >= lag) & (t < total + lag))(functools.partial(stage, t - lag))
+
+    def begin(t):
+        run([(LAG_C, begin_c), (LAG_D, begin_d), (LAG_E, begin_e)], t)
+
+    def end(t):
+        run([(LAG_B, end_b), (LAG_C, end_c), (LAG_D, end_d), (LAG_E, end_e), (LAG_G, end_g)], t)
 
     def tiles(u, i, slot):
         unit = units[u]
@@ -302,26 +345,244 @@
         else:
             first = core * unit.row_blocks * piece_rows + r * piece_rows
             second = (1 - core) * unit.row_blocks * piece_rows + r * piece_rows
-        first = pl.multiple_of(first, piece_rows)
-        second = pl.multiple_of(second, piece_rows)
-        cols = pl.multiple_of(j * piece_cols, piece_cols)
+        first = pl.ds(pl.multiple_of(first, piece_rows), piece_rows)
+        second = pl.ds(pl.multiple_of(second, piece_rows), piece_rows)
+        cols = pl.ds(pl.multiple_of(j * piece_cols, piece_cols), piece_cols)
         return [
-            pltpu.make_async_copy(
-                lefts[u].at[:, pl.ds(first, piece_rows)], lm.at[slot], tile_sem.at[slot, 0]
-            ),
-            pltpu.make_async_copy(
-                lefts[u].at[:, pl.ds(second, piece_rows)], lo.at[slot], tile_sem.at[slot, 1]
-            ),
-            pltpu.make_async_copy(
-                rights[u].at[:, pl.ds(cols, piece_cols)], rh.at[slot], tile_sem.at[slot, 2]
-            ),
+            pltpu.make_async_copy(lefts[u].at[:, first], lm.at[slot], tile_sem.at[slot, 0]),
+            pltpu.make_async_copy(lefts[u].at[:, second], lo.at[slot], tile_sem.at[slot, 1]),
+            pltpu.make_async_copy(rights[u].at[:, cols], rh.at[slot], tile_sem.at[slot, 2]),
         ]
 
+
+    first_pairs = (
+        (grad_mlp.at[:, pl.ds(0, ff)], big.at[pl.ds(0, rows_all)]),
+        (grad_mlp.at[:, pl.ds(ff, ff)], big.at[pl.ds(rows_all, rows_all)]),
+        (middle, mid),
+        (grad_result, gres),
+        (tokens, tok),
+        (w_output, wo),
+    )
+
+    def first_loads(which):
+        return [pltpu.make_async_copy(*first_pairs[i], first_sem.at[i]) for i in which]
+
+    def attn_load():
+        return pltpu.make_async_copy(w_attn, big.at[pl.ds(0, width)], first_sem.at[6])
+
+    def tile_of(j):
+        return pl.ds(pl.multiple_of(j * tile, tile), tile)
+
+    def wt_load(j):
+        return pltpu.make_async_copy(w_mlp.at[tile_of(j)], wt.at[j % 2], wt_sem.at[j % 2])
+
+    def p_copy(s, j):
+        return remote_copy(
+            pbuf.at[s - 1, :, tile_of(j)],
+            land_a.at[s - 1, :, tile_of(j)],
+            ps.at[s, j],
+            pr.at[s, j],
+            rep,
+            flipped(mine, s, n_fsdp),
+        )
+
+    def q_copy(s):
+        return remote_copy(
+            pbuf.at[s - 1], land_b.at[s - 1], qs.at[s], qr.at[s], rep, flipped(mine, s, n_fsdp)
+        )
+
+    gather = GatherRows(n_fsdp, rep, mine, ga, grad_attn, (ag_s, ag_r, ag_l))
+
+    def mlp_products(j):
+        @pl.when(j == 0)
+        def _():
+            for copy in first_loads((0, 1)):
+                copy.wait()
+
+        wt_load(j).wait()
+
+        @pl.when(j + 1 < TILES)
+        def _():
+            wt_load(j + 1).start()
+
+        for s in (*others, 0):
+            part = product_of(big[s * rows : (s + 1) * rows], wt[j % 2, :, :ff], 1, 1)
+            part += product_of(
+                big[rows_all + s * rows : rows_all + (s + 1) * rows], wt[j % 2, :, ff:], 1, 1
+            )
+            if s == 0:
+                own[:, tile_of(j)] = part
+            else:
+                pbuf[s - 1, :, tile_of(j)] = in_bf16(part)
+                p_copy(s, j).start()
+
+    def middle_back():
+        attn_load().start()
+        for copy in first_loads((2, 3)):
+            copy.wait()
+
+        def wait_tiles(j, carry):
+            for s in others:
+                p_copy(s, j).wait()
+            return carry
+
+        lax.fori_loop(0, TILES, wait_tiles, 0)
+        gain_out[...] = jnp.zeros_like(gain_out)
+        head_gain_out[...] = jnp.zeros_like(head_gain_out)
+
+        def some_rows(r, carry):
+            cut = pl.ds(pl.multiple_of(r * ROW_STEP, ROW_STEP), ROW_STEP)
+            grad = own[cut]
+            for s in others:
+                grad += in_f32(land_a[s - 1, cut])
+            back, gain_rows = norm_back(grad, mid[cut], gains[1:2])
+            gain_out[1:2] += jnp.sum(gain_rows, axis=0, keepdims=True)
+            back = gres[cut] + back
+            gres[cut] = back
+            ga[cut] = in_bf16(back)
+            return carry
+
+        lax.fori_loop(0, rows // ROW_STEP, some_rows, 0)
+        gather.start()
+
+    def block_loads(s):
+        cut = pl.ds(pl.multiple_of(s * rows, rows), rows)
+        pairs = (
+            (attn_raw, raw), (all_cos, cs), (all_sin, sn), (all_q, qb), (all_k, kvb), (all_v, vb)
+        )
+        copies = [
+            pltpu.make_async_copy(src.at[cut], dst, block_sem.at[i])
+            for i, (src, dst) in enumerate(pairs)
+        ]
+        return copies
+
+    def grad_load(s):
+        cut = pl.ds(pl.multiple_of(s * rows, rows), rows)
+        return pltpu.make_async_copy(grad_attn.at[cut], gb, block_sem.at[6])
+
+    def store(s):
+        cut = pl.ds(pl.multiple_of(s * rows, rows), rows)
+        return pltpu.make_async_copy(ob, grad_raw.at[cut], block_sem.at[7])
+
+    def heads_back(s, heads):
+        attend_back(
+            heads_k,
+            heads,
+            block_mask(pair_ref, rows, s),
+            cs[...],
+            sn[...],
+            head_gains[0:1],
+            head_gains[1:2],
+            raw,
+            qb,
+            kvb,
+            vb,
+            gg,
+            ob,
+            head_gain_out,
+        )
+
+    early = heads_k // 2
+
+    def block_first(s):
+        copies = block_loads(s)
+        for copy in copies:
+            copy.start()
+
+        @pl.when(s == 0)
+        def _():
+            first_loads((5,))[0].wait()
+            gb[...] = ga[...]
+
+        for k in others:
+
+            @pl.when(s == k)
+            def _(k=k):
+                gather.arrive(k)
+
+        @pl.when(s > 0)
+        def _():
+            copy = grad_load(s)
+            copy.start()
+            copy.wait()
+
+        gg[...] = product_of(gb[...], wo[...], 1, 1)
+        for copy in copies:
+            copy.wait()
+        heads_back(s, range(early))
+
+    def block_second(s):
+        heads_back(s, range(early, heads_k))
+        store(s).start()
+
+    def block_third(s):
+        store(s).wait()
+
+        @pl.when(s == 0)
+        def _():
+            attn_load().wait()
+
+        def one_tile(j, carry):
+            part = product_of(ob[...], big[tile_of(j)], 1, 1)
+
+            @pl.when(s == 0)
+            def _():
+                own[:, tile_of(j)] = part
+
+            @pl.when(s > 0)
+            def _():
+                pbuf[s - 1, :, tile_of(j)] = in_bf16(part)
+
+            return carry
+
+        lax.fori_loop(0, TILES, one_tile, 0)
+
+        @pl.when(s > 0)
+        def _():
+            q_copy(s).start()
+
+    def tokens_back():
+        first_loads((4,))[0].wait()
+        for s in others:
+            q_copy(s).wait()
+
+        def some_rows(r, carry):
+            cut = pl.ds(pl.multiple_of(r * ROW_STEP, ROW_STEP), ROW_STEP)
+            grad = own[cut]
+            for s in others:
+                grad += in_f32(land_b[s - 1, cut])
+            back, gain_rows = norm_back(grad, in_f32(tok[cut]), gains[0:1])
+            gain_out[0:1] += jnp.sum(gain_rows, axis=0, keepdims=True)
+            tokens_grad[cut] = in_bf16(gres[cut] + back)
+            return carry
+
+        lax.fori_loop(0, rows // ROW_STEP, some_rows, 0)
+
+    def tasks(u, i):
+        if u == 0:
+            pl.when(i < TILES)(lambda: mlp_products(i))
+        if u == 1:
+            pl.when(i == 2)(middle_back)
+            pl.when(i == 6)(gather.forward)
+            pl.when(i == 12)(lambda: gather.own().wait())
+            last = 12 + 3 * (n_fsdp - 1)
+            busy = ((i >= 6) & (i < 9)) | ((i >= 12) & (i < last))
+            s = at_least(i, 9, units[1].count) * ((i - 9) // 3)
+            for phase, task in enumerate((block_first, block_second, block_third)):
+                pl.when(busy & (i % 3 == phase))(functools.partial(task, s))
+        if u == 2:
+
+            @pl.when(i == 2)
+            def _():
+                gather.sent()
+                tokens_back()
+
     def product(left, right):
-        return lax.dot_general(
-            left, right, (((0,), (0,)), ((), ())), preferred_element_type=jnp.float32
-        )
-
+        return product_of(left, right, 0, 0)
+
+    for copy in first_loads(range(6)):
+        copy.start()
+    wt_load(0).start()
     for copy in tiles(0, 0, 0):
         copy.start()
     for u, unit in enumerate(units):
@@ -329,6 +590,7 @@
         def step(i, carry, u=u, unit=unit):
             t = unit.base + i
             slot = t % 2
+            begin(t)
             for copy in tiles(u, i, slot):
                 copy.wait()
 
@@ -348,16 +610,18 @@
             def _():
                 r1_copy(t - RING).wait_send()
 
-            sb[t % RING] = product(lo[slot], rh[slot]).astype(jnp.bfloat16)
+            sb[t % RING] = in_bf16(product(lo[slot], rh[slot]))
             r1_copy(t).start()
             kb[t % RING] = product(lm[slot], rh[slot])
-            service(t)
+            end(t)
+            tasks(u, i)
             return carry
 
         lax.fori_loop(0, unit.count, step, 0)
 
     def drain(t, carry):
-        service(t)
+        begin(t)
+        end(t)
         return carry
 
     lax.fori_loop(total, total + LAG_G, drain, 0)
@@ -387,37 +651,87 @@
     lax.fori_loop(0, total, finish, 0)
 
 
-def reduced(n_fsdp, n_rep, units, piece_rows, piece_cols, lefts, rights):
+def backward(n_fsdp, n_rep, heads_k, units, piece_rows, piece_cols, args):
     total = sum(unit.count for unit in units)
-    rows = lefts[0].shape[0]
-    half = n_rep // 4
+    rows_all, rows = args[0].shape[0], args[9].shape[0]
+    width, cols = args[8].shape
+    cols_q, cols_k = heads_k * (H // KV) * HD, heads_k * HD
+    two_ff = args[5].shape[1]
     dma = pltpu.SemaphoreType.DMA
     piece = (piece_rows, piece_cols)
+    low, full = jnp.bfloat16, jnp.float32
     any_spec = pl.BlockSpec(memory_space=pl.ANY)
-    flops = sum(4 * unit.count for unit in units) * rows * piece_rows * piece_cols
+    vmem = pl.BlockSpec(memory_space=pltpu.VMEM)
+    flops = sum(4 * unit.count for unit in units) * rows_all * piece_rows * piece_cols
+    outs = (
+        ((total, 2) + piece, low),
+        ((rows_all, width), low),
+        ((rows_all, cols), low),
+        ((total,) + piece, low),
+        ((total,) + piece, low),
+        ((rows, width), low),
+        ((8, width), full),
+        ((8, HD), full),
+    )
+    scratch = (
+        ((2, rows_all, piece_rows), low),
+        ((2, rows_all, piece_rows), low),
+        ((2, rows_all, piece_cols), low),
+        ((RING,) + piece, low),
+        ((RING,) + piece, full),
+        ((total,) + piece, low),
+        (piece, low),
+        (piece, low),
+        ((max(2 * rows_all, width), cols), low),
+        ((2, width // TILES, two_ff), low),
+        ((rows, width), full),
+        ((n_fsdp - 1, rows, width), low),
+        ((n_fsdp - 1, rows, width), low),
+        ((n_fsdp - 1, rows, width), low),
+        ((rows, width), full),
+        ((rows, width), full),
+        ((rows, width), low),
+        ((rows, width), low),
+        ((cols_q, width), low),
+        ((rows, cols), full),
+        ((rows, HD), full),
+        ((rows, HD), full),
+        ((rows, cols_q), low),
+        ((rows, cols_k), low),
+        ((rows, cols_k), low),
+        ((rows, width), low),
+        ((rows, cols_q), full),
+        ((rows, cols), low),
+    )
     return pl.pallas_call(
-        functools.partial(reduce_kernel, n_fsdp, n_rep, units, piece_rows, piece_cols),
-        out_shape=jax.ShapeDtypeStruct((total, 2) + piece, jnp.bfloat16),
-        in_specs=[any_spec] * (2 * len(units)),
-        out_specs=any_spec,
-        scratch_shapes=[
-            pltpu.VMEM((2, rows, piece_rows), jnp.bfloat16),
-            pltpu.VMEM((2, rows, piece_rows), jnp.bfloat16),
-            pltpu.VMEM((2, rows, piece_cols), jnp.bfloat16),
-            pltpu.VMEM((RING,) + piece, jnp.bfloat16),
-            pltpu.VMEM((RING,) + piece, jnp.float32),
-            pltpu.VMEM((total,) + piece, jnp.bfloat16),
-            pltpu.VMEM((total,) + piece, jnp.bfloat16),
-            pltpu.VMEM((total,) + piece, jnp.bfloat16),
-            dma((2, 3)),
-        ]
-        + [dma((total,)) for _ in range(12)],
+        functools.partial(
+            backward_kernel, n_fsdp, n_rep, heads_k, units, piece_rows, piece_cols
+        ),
+        out_shape=[jax.ShapeDtypeStruct(shape, kind) for shape, kind in outs],
+        in_specs=[any_spec] * 18 + [vmem] * 2 + [pl.BlockSpec(memory_space=pltpu.SMEM)],
+        out_specs=[any_spec] * 5 + [vmem] * 3,
+        scratch_shapes=[pltpu.VMEM(shape, kind) for shape, kind in scratch]
+        + [dma((2, 3))]
+        + [dma((total,)) for _ in range(12)]
+        + [
+            dma((3,)),
+            dma((7,)),
+            dma((2,)),
+            dma((n_fsdp, TILES)),
+            dma((n_fsdp, TILES)),
+            dma((n_fsdp,)),
+            dma((n_fsdp,)),
+            dma((n_fsdp, 2)),
+            dma((n_fsdp, 2)),
+            dma,
+            dma((8,)),
+        ],
         compiler_params=pltpu.CompilerParams(
-            collective_id=0, has_side_effects=True, vmem_limit_bytes=60 << 20
+            collective_id=0, has_side_effects=True, vmem_limit_bytes=62 << 20
         ),
-        cost_estimate=pl.CostEstimate(flops=flops, bytes_accessed=1 << 30, transcendentals=0),
-        name="reduce_weight_gradients",
-    )(*lefts, *rights)
+        cost_estimate=pl.CostEstimate(flops=2 * flops, bytes_accessed=1 << 30, transcendentals=0),
+        name="backward",
+    )(*args)
 
 
 def widen_kernel(in_ref, out_ref):
@@ -463,8 +777,7 @@
     )(pieces, pieces, pieces)
 
 
-def block_mask(pair_ref, rows):
-    block = pl.program_id(0)
+def block_mask(pair_ref, rows, block):
     head_len = pair_ref[block, 0]
     both_len = head_len + pair_ref[block, 1]
     query_row = lax.broadcasted_iota(jnp.int32, (rows, rows), 0)
@@ -512,7 +825,7 @@
 ):
     group = H // KV
     cols_q, cols_k = heads_k * group * HD, heads_k * HD
-    allowed = block_mask(pair_ref, raw_ref.shape[0])
+    allowed = block_mask(pair_ref, raw_ref.shape[0], pl.program_id(0))
     angle_cos, angle_sin = cos_ref[...], sin_ref[...]
     for j in range(heads_k):
         own = slice(j * HD, (j + 1) * HD)
@@ -536,14 +849,15 @@
             gated_ref[:, cut] = in_bf16(context * jax.nn.sigmoid(gate))
 
 
-def attend_back_kernel(
+def attend_back(
     heads_k,
-    pair_ref,
+    heads,
+    allowed,
+    angle_cos,
+    angle_sin,
+    query_gain,
+    key_gain,
     raw_ref,
-    cos_ref,
-    sin_ref,
-    qg_ref,
-    kg_ref,
     q_ref,
     k_ref,
     v_ref,
@@ -553,14 +867,7 @@
 ):
     group = H // KV
     cols_q, cols_k = heads_k * group * HD, heads_k * HD
-    allowed = block_mask(pair_ref, raw_ref.shape[0])
-    angle_cos, angle_sin = cos_ref[...], sin_ref[...]
-
-    @pl.when(pl.program_id(0) == 0)
-    def _():
-        gain_ref[...] = jnp.zeros_like(gain_ref)
-
-    for j in range(heads_k):
+    for j in heads:
         own = slice(j * HD, (j + 1) * HD)
         keys, values = k_ref[:, own], v_ref[:, own]
         grad_keys, grad_values = 0.0, 0.0
@@ -582,7 +889,7 @@
             grad_keys += product_of(grad_scores, queries, 0, 0)
             grad_queries = product_of(grad_scores, keys, 1, 0) * HD ** (-0.5)
             grad_raw, gain_rows = head_backward(
-                grad_queries, raw_ref[:, cut], qg_ref[...], angle_cos, angle_sin
+                grad_queries, raw_ref[:, cut], query_gain, angle_cos, angle_sin
             )
             out_ref[:, cut] = in_bf16(grad_raw)
             gain_ref[0:1, :] += jnp.sum(gain_rows, axis=0, keepdims=True)
@@ -590,7 +897,7 @@
         grad_raw, gain_rows = head_backward(
             grad_keys * HD ** (-0.5),
             raw_ref[:, key_start : key_start + HD],
-            kg_ref[...],
+            key_gain,
             angle_cos,
             angle_sin,
         )
@@ -635,41 +942,6 @@
     )(pair_len, raw, angle_cos, angle_sin, query_gain, key_gain)
 
 
-def attend_back(
-    heads_k, rows, pair_len, raw, angle_cos, angle_sin, query_gain, key_gain, q, k, v, grad_gated
-):
-    rows_all, cols = raw.shape
-    cols_q, cols_k = heads_k * (H // KV) * HD, heads_k * HD
-    return pl.pallas_call(
-        functools.partial(attend_back_kernel, heads_k),
-        grid=(rows_all // rows,),
-        in_specs=[
-            pl.BlockSpec(memory_space=pltpu.SMEM),
-            rows_spec(rows, cols),
-            rows_spec(rows, HD),
-            rows_spec(rows, HD),
-            whole_spec((1, HD)),
-            whole_spec((1, HD)),
-            rows_spec(rows, cols_q),
-            rows_spec(rows, cols_k),
-            rows_spec(rows, cols_k),
-            rows_spec(rows, cols_q),
-        ],
-        out_shape=[
-            jax.ShapeDtypeStruct((rows_all, cols), jnp.bfloat16),
-            jax.ShapeDtypeStruct((8, HD), jnp.float32),
-        ],
-        out_specs=[rows_spec(rows, cols), whole_spec((8, HD))],
-        cost_estimate=pl.CostEstimate(
-            flops=14 * rows_all * rows * cols_q,
-            bytes_accessed=10 * rows_all * cols,
-            transcendentals=rows_all * rows * heads_k * 2,
-        ),
-        compiler_params=pltpu.CompilerParams(vmem_limit_bytes=32 << 20),
-        name="attend_back",
-    )(pair_len, raw, angle_cos, angle_sin, query_gain, key_gain, q, k, v, grad_gated)
-
-
 def after(values, *others):
     return lax.optimization_barrier((values, *others))[0]
 
@@ -699,14 +971,17 @@
         self.n_fsdp, self.rep, self.mine = n_fsdp, rep, mine
         self.source, self.target = source, target
         self.send, self.recv, self.local = sems
-        self.half = source.shape[0] // 2
+        self.rows = source.shape[0]
+        self.half = self.rows // 2
+        self.relay = ((1, 0), (2, 1)) if n_fsdp == 4 else ()
 
     def copy(self, s, h, to=None, src=None):
-        rows = pl.ds(h * self.half, self.half)
         to = s if to is None else to
         return remote_copy(
-            self.source.at[rows] if src is None else self.target.at[src, rows],
-            self.target.at[s, rows],
+            self.source.at[pl.ds(h * self.half, self.half)]
+            if src is None
+            else self.target.at[pl.ds(src * self.rows + h * self.half, self.half)],
+            self.target.at[pl.ds(s * self.rows + h * self.half, self.half)],
             self.send.at[s, h],
             self.recv.at[s, h],
             self.rep,
@@ -714,7 +989,9 @@
         )
 
     def own(self):
-        return pltpu.make_async_copy(self.source, self.target.at[0], self.local)
+        return pltpu.make_async_copy(
+            self.source, self.target.at[pl.ds(0, self.rows)], self.local
+        )
 
     def start(self):
         for s, h in ((1, 0), (2, 1), (1, 1), (2, 0)):
@@ -733,14 +1010,20 @@
             self.copy(2, 1).wait_recv()
             self.copy(3, 1, to=1, src=2).start()
 
+    def arrive(self, s):
+        for h in range(2):
+            if (s, h) not in self.relay:
+                self.copy(s, h).wait_recv()
+
+    def sent(self):
+        for s in range(1, self.n_fsdp):
+            for h in range(2):
+                self.copy(s, h).wait_send()
+
     def finish(self):
         for s in range(1, self.n_fsdp):
-            for h in range(2):
-                copy = self.copy(s, h)
-                if self.n_fsdp == 4 and (s, h) in ((1, 0), (2, 1)):
-                    copy.wait_send()
-                else:
-                    copy.wait()
+            self.arrive(s)
+        self.sent()
         self.own().wait()
 
 
@@ -853,7 +1136,7 @@
     dma = pltpu.SemaphoreType.DMA
     any_spec = pl.BlockSpec(memory_space=pl.ANY)
     shapes = (
-        (n_fsdp, rows, width),
+        (n_fsdp * rows, width),
         (n_fsdp,) + gains.shape,
         (n_fsdp * deep, sum(widths)),
         (n_fsdp - 1, deep // n_rep, 2 * ff),
@@ -973,7 +1256,6 @@
         w_gate,
         w_up,
     )
-    tokens_all = tokens_all.reshape(rows_all, width)
     gains = in_f32(gains.reshape(n_fsdp, 16 * HD))
     attention_gain_f = gains[:, :deep].reshape(-1)
     mlp_gain_f = gains[:, deep : 2 * deep].reshape(-1)
@@ -1010,7 +1292,7 @@
         return scatter_rows(own, [parts[i * rows : (i + 1) * rows] for i in range(n_fsdp - 1)])
 
     middle = tokens_f + summed(gated_b, w_output, times)
-    normed_mlp, mlp_norm_back = jax.vjp(rms_scale, middle, mlp_gain_f)
+    normed_mlp = rms_scale(middle, mlp_gain_f)
     normed_mlp_all = jnp.concatenate(gather_rows(in_bf16(normed_mlp)))
     gate_pre = times(normed_mlp_all, w_mlp[:, :ff])
     up_pre = times(normed_mlp_all, w_mlp[:, ff:])
@@ -1031,23 +1313,6 @@
     grad_gate_b = in_bf16(grad_gate_pre)
     grad_up_b = in_bf16(grad_up_pre)
     grad_mlp_b = jnp.concatenate([grad_gate_b, grad_up_b], axis=1)
-    grad_normed_mlp = summed(grad_mlp_b, w_mlp, times_trans)
-    grad_middle_norm, grad_mlp_gain = mlp_norm_back(grad_normed_mlp)
-    grad_middle = grad_result + grad_middle_norm
-
-    grad_attn_all = jnp.concatenate(gather_rows(in_bf16(grad_middle)))
-    grad_gated = times_trans(grad_attn_all, w_output)
-    grad_raw_b, head_gains = attend_back(*head_args, queries_b, keys_b, values_b, grad_gated)
-    grad_query_gain, grad_key_gain = head_gains[0], head_gains[1]
-    grad_normed = summed(grad_raw_b, w_attn, times_trans)
-    _, norm_back = jax.vjp(rms_scale, tokens_f, attention_gain_f)
-    grad_tokens_norm, grad_attention_gain = norm_back(grad_normed)
-    tokens_grad = in_bf16(grad_middle + grad_tokens_norm)
-
-    dgains = sum_everywhere(
-        jnp.concatenate([grad_attention_gain, grad_mlp_gain, grad_query_gain, grad_key_gain])[None]
-    )[0]
-
     piece_rows, piece_cols = deep // 2, width // n_fsdp
     units, base = [], 0
     for by_owner, row_blocks, cols in (
@@ -1058,15 +1323,46 @@
     ):
         units.append(Unit(base, by_owner, row_blocks, cols // piece_cols))
         base += units[-1].count
-    pieces = reduced(
+    gain_rows = jnp.concatenate(
+        [attention_gain_f[None], mlp_gain_f[None], jnp.zeros((6, width), jnp.float32)]
+    )
+    head_gains = jnp.concatenate(
+        [query_gain_f[None], key_gain_f[None], jnp.zeros((6, HD), jnp.float32)]
+    )
+    pieces, _, _, _, _, tokens_grad, gain_parts, head_gain_parts = backward(
         n_fsdp,
         n_rep,
+        heads_k,
         units,
         piece_rows,
         piece_cols,
-        (hidden_b, normed_mlp_all, gated_b, normed_all),
-        (grad_branch_all, grad_mlp_b, grad_attn_all, grad_raw_b),
-    )
+        (
+            hidden_b,
+            normed_mlp_all,
+            gated_b,
+            normed_all,
+            grad_branch_all,
+            grad_mlp_b,
+            w_mlp,
+            w_output,
+            w_attn,
+            middle,
+            grad_result,
+            tokens,
+            attn_raw,
+            angle_cos,
+            angle_sin,
+            queries_b,
+            keys_b,
+            values_b,
+            gain_rows,
+            head_gains,
+            pair_len,
+        ),
+    )
+    dgains = sum_everywhere(
+        jnp.concatenate([gain_parts[:2].reshape(1, -1), head_gain_parts[:2].reshape(1, -1)], axis=1)
+    )[0]
     down, mlp, outp, attn = units
 
     def by_rows(unit, weight):

time: 909 us -> 795 us (0.87)
  waiting for transfers between devices: 161 us -> 97.4 us
  matrix products: 103 us -> 62.9 us
  Pallas kernels: 484 us -> 512 us
  starting transfers between devices: 49.1 us -> 29.3 us
  other arithmetic: 37.8 us -> 25 us
    ppermute x42 -> x24, waiting for transfers between devices: 155 us -> 86.9 us  [shift(): return lax.ppermute(values, 'fsdp', [(i, i ^ step) for i in range(n_fsdp)])]
    dot_general x6 -> x1, matrix products: 56.2 us -> 15 us  [times_trans(): lax.dot_general(left_side, right_side, (((1,), (1,)), ((), ())), preferre...]
    pallas_call x2 -> x1, Pallas kernels: 348 us -> 376 us  [backward(): pl.pallas_call(functools.partial(backward_kernel, n_fsdp, n_rep, heads_k,...]
    ppermute x42 -> x24, starting transfers between devices: 44.9 us -> 24.9 us  [shift(): return lax.ppermute(values, 'fsdp', [(i, i ^ step) for i in range(n_fsdp)])]
    convert_element_type x6 -> x3, other arithmetic: 12.6 us -> 2.81 us  [in_bf16(): return values.astype(jnp.bfloat16)]
  transfers between devices with their start and end apart: 48 -> 30, of which waited for: 33 -> 19; matrix products, arithmetic and copies ran while one was open for 7% -> 6% of each run, Pallas kernels for 42% -> 6%
where the time goes in v4:
time: 795 us; the launch traced here: 786 us
  Pallas kernels  512 us (64%)
  waiting for transfers between devices  97.4 us (12%)
  matrix products  62.9 us (8%)
  local copies, waits for them, and re-layouts  43.5 us (5%)
  starting transfers between devices  29.3 us (4%)
  other arithmetic  25 us (3%)
  between operations  15.5 us (2%)
    pallas_call x1, Pallas kernels, backward(): pl.pallas_call(functools.partial(backward_kernel, n_fsdp, n_rep, heads_k,...  376 us
    ppermute x24, waiting for transfers between devices, shift(): return lax.ppermute(values, 'fsdp', [(i, i ^ step) for i in range(n_fsdp)])  86.9 us
    pallas_call x1, Pallas kernels, fetched(): pl.pallas_call(functools.partial(fetch_kernel, n_fsdp, n_rep, widths, ff)...  85.5 us
    dot_general x7, matrix products, times(): jnp.dot(left_side, right_side, preferred_element_type=jnp.float32)  48 us
    pallas_call x4, Pallas kernels, widened(): pl.pallas_call(widen_kernel, grid=grid, out_shape=jax.ShapeDtypeStruct(sh...  29.2 us
    ppermute x24, starting transfers between devices, shift(): return lax.ppermute(values, 'fsdp', [(i, i ^ step) for i in range(n_fsdp)])  24.9 us
  transfers between devices with their start and end apart: 30, of which 19 were waited for; matrix products, arithmetic and copies ran while one was open for 6% of the time, Pallas kernels for 6%

profile of v4, /device:TPU:0, one launch (start us, length us, event | category | flops | bytes accessed | tf_op | source)
XLA Modules:
  0.0 785.7 jit_solution(2377153275007861306)
XLA Ops:
  10.6 85.5 %fetch.1 = (bf16[1024,2048]{1,0:T(8,128)(2,1)}, bf16[4,16,128]{2,1,0:T(8,128)(2,1)}, bf16[2048,1536]{1,0:T(8,128)(2,1)}, bf16[3,64,3072]{2,1,0:T(8,128)(2,1)}) custom-call(bf16[256,2048]{1,0:T(8,128)(2,1)} %refs_11_.1, bf16[16,128]{1,0:T(8,128)(2,1)} %pad_bitcast_fusion.refs_1_, bf16[512,2048]{1,0:T(8,128)(2,1)} %refs_2_.1, bf16[512,2048]{1,0:T(8,128)(2,1)} %refs_3_.1, ...), custom_call_target="tpu_custom_call" | custom-call | tf_op jit(solution)/shard_map/fetch/pallas_call | solution.py:1146
  107.1 6.7 fusion.38.raw_ref.refs_12_
  113.8 12.5 %attend.1 = (bf16[1024,512]{1,0:T(8,128)(2,1)S(1)}, bf16[1024,256]{1,0:T(8,128)(2,1)S(1)}, bf16[1024,256]{1,0:T(8,128)(2,1)S(1)}, bf16[1024,512]{1,0:T(8,128)(2,1)S(1)}) custom-call(s32[4,2]{1,0:T(4,128)S(1)} %reshape.194.pair_ref.refs_20_, f32[1024,1536]{1,0:T(8,128)S(1)} %fusion.38.raw_ref.refs_12_, f32[1024,128]{1,0:T(8,128)S(1)} %pad_maximum_fusion.1.cos_ref.refs_13_, ...), custom_call_target="tpu_custom_call" | custom-call | flops 536870912 | bytes 12582912 | tf_op jit(solution)/shard_map/attend/pallas_call | solution.py:922
  131.9 10.8 %collective-permute-done.4 = bf16[128,2048]{1,0:T(8,128)(2,1)S(1)} collective-permute-done((bf16[128,2048]{1,0:T(8,128)(2,1)S(1)}, bf16[128,2048]{1,0:T(8,128)(2,1)S(1)}, u32[]{:S(2)}, u32[]{:S(2)}) %collective-permute-start.4) | collective-permute-done | bytes 524320 | tf_op jit(solution)/shard_map/ppermute | solution.py:75
  148.7 7.3 collective-permute-done
  161.4 5.5 collective-permute-done.3
  176.9 6.4 broadcast_in_dim.60
  190.4 10.8 %collective-permute-done.6 = bf16[128,2048]{1,0:T(8,128)(2,1)S(1)} collective-permute-done((bf16[128,2048]{1,0:T(8,128)(2,1)}, bf16[128,2048]{1,0:T(8,128)(2,1)S(1)}, u32[]{:S(2)}, u32[]{:S(2)}) %collective-permute-start.6) | collective-permute-done | bytes 524320 | tf_op jit(solution)/shard_map/ppermute | solution.py:75
  212.0 4.2 fusion.32
  223.3 10.6 %fusion.8 = f32[1024,1536]{1,0:T(8,128)} fusion(bf16[1024,2048]{1,0:T(8,128)(2,1)S(1)} %copy-done.15, bf16[2048,3072]{1,0:T(8,128)(2,1)} %constant_dynamic-update-slice_fusion.14.refs_6_), kind=kOutput, calls=%fused_computation.11 | convolution fusion | flops 6442450944 | bytes 16777216 | tf_op jit(solution)/shard_map/dot_general | solution.py:46
  233.9 10.8 %multiply_convert_fusion.1 = (bf16[1024,1536]{1,0:T(8,128)(2,1)S(1)}, f32[1024,1536]{1,0:T(8,128)}) fusion(f32[1024,1536]{1,0:T(8,128)} %fusion.8, bf16[1024,2048]{1,0:T(8,128)(2,1)S(1)} %copy-done.15, bf16[2048,3072]{1,0:T(8,128)(2,1)S(1)} %copy-done.9), kind=kOutput, calls=%fused_computation.15 | convolution fusion | flops 6451888128 | bytes 26214400 | tf_op jit(solution)/shard_map/dot_general | solution.py:46
  244.7 9.1 %convolution_convert_fusion.1 = bf16[768,2048]{1,0:T(8,128)(2,1)S(1)} fusion(bf16[1536,2048]{1,0:T(8,128)(2,1)} %param.31, bf16[1024,1536]{1,0:T(8,128)(2,1)S(1)} %get-tuple-element.91.refs_0_), kind=kOutput, calls=%fused_computation.19 | convolution fusion | flops 4833411072 | bytes 11796480 | tf_op jit(solution)/shard_map/dot_general | solution.py:46
  257.6 10.9 %collective-permute-done.16 = bf16[128,2048]{1,0:T(8,128)(2,1)S(1)} collective-permute-done((bf16[128,2048]{1,0:T(8,128)(2,1)S(1)}, bf16[128,2048]{1,0:T(8,128)(2,1)S(1)}, u32[]{:S(2)}, u32[]{:S(2)}) %collective-permute-start.16) | collective-permute-done | bytes 524320 | tf_op jit(solution)/shard_map/ppermute | solution.py:75
  282.7 4.3 collective-permute-done.15
  288.3 6.3 multiply_reduce_fusion
  302.0 6.6 collective-permute-done.21
  310.9 6.3 collective-permute-done.18
  317.9 8.5 %collective-permute-done.22 = bf16[128,2048]{1,0:T(8,128)(2,1)S(1)} collective-permute-done((bf16[128,2048]{1,0:T(8,128)(2,1)S(1)}, bf16[128,2048]{1,0:T(8,128)(2,1)S(1)}, u32[]{:S(2)}, u32[]{:S(2)}) %collective-permute-start.22) | collective-permute-done | bytes 524320 | tf_op jit(solution)/shard_map/ppermute | solution.py:75
  326.5 15.0 %fusion.5 = (bf16[1024,1536]{1,0:T(8,128)(2,1)S(1)}, bf16[1024,1536]{1,0:T(8,128)(2,1)S(1)}) fusion(f32[1024,1536]{1,0:T(8,128)} %fusion.8, f32[1024,1536]{1,0:T(8,128)} %get-tuple-element.92, bf16[1024,2048]{1,0:T(8,128)(2,1)S(1)} %constant_dynamic-update-slice_fusion.7.refs_4_, bf16[1536,2048]{1,0:T(8,128)(2,1)} %param.31), kind=kOutput, calls=%fused_computation.8 | convolution fusion | flops 6464471040 | bytes 29360128 | tf_op jit(solution)/shard_map/dot_general | solution.py:50
  345.1 376.2 %backward.1 = (bf16[52,2,256,512]{3,2,1,0:T(8,128)(2,1)}, bf16[1024,2048]{1,0:T(8,128)(2,1)}, bf16[1024,1536]{1,0:T(8,128)(2,1)}, bf16[52,256,512]{2,1,0:T(8,128...) custom-call(bf16[1024,1536]{1,0:T(8,128)(2,1)} %copy-done.19, ...), custom_call_target="tpu_custom_call" | custom-call | flops 55834574848 | bytes 1073741824 | tf_op jit(solution)/shard_map/backward/pallas_call | solution.py:706
  741.9 8.2 %widen.7 = f32[1536,2048]{1,0:T(8,128)} custom-call(bf16[52,2,256,512]{3,2,1,0:T(8,128)(2,1)} %get-tuple-element.42.query_in.gate_in.pair_in.in_ref), custom_call_target="tpu_custom_call" | custom-call | tf_op jit(solution)/shard_map/widen/pallas_call | solution.py:745
  750.1 8.8 %widen.6 = f32[512,6144]{1,0:T(8,128)} custom-call(bf16[52,2,256,512]{3,2,1,0:T(8,128)(2,1)} %get-tuple-element.42.query_in.gate_in.pair_in.in_ref), custom_call_target="tpu_custom_call" | custom-call | tf_op jit(solution)/shard_map/widen/pallas_call | solution.py:745
  758.9 8.8 %widen.5 = f32[512,6144]{1,0:T(8,128)} custom-call(bf16[52,2,256,512]{3,2,1,0:T(8,128)(2,1)} %get-tuple-element.42.query_in.gate_in.pair_in.in_ref), custom_call_target="tpu_custom_call" | custom-call | tf_op jit(solution)/shard_map/widen/pallas_call | solution.py:745
  767.8 8.7 %widen_heads.1 = (f32[512,2048]{1,0:T(8,128)}, f32[512,2048]{1,0:T(8,128)}, f32[512,1024]{1,0:T(8,128)}, f32[512,1024]{1,0:T(8,128)}) custom-call(bf16[52,2,256,512]{3,2,1,0:T(8,128)(2,1)} %get-tuple-element.42.query_in.gate_in.pair_in.in_ref, bf16[52,2,256,512]{3,2,1,0:T(8,128)(2,1)} %get-tuple-element.42.query_in.gate_in.pair_in.in_ref, ...), custom_call_target="tpu_custom_call" | custom-call | tf_op jit(solution)/shard_map/widen_heads/pallas_call | solution.py:770
  (184 shorter events, 121.7 us)
Async XLA Ops:
  7.2 204.8 %all-gather.3.cloned.1.call-start = ((), (), s32[]{:S(2)}) async-start(), calls=%async_computation | async-start | bytes 10616832 | tf_op jit(solution)/shard_map/all_gather | solution.py:1265
  129.3 13.3 %collective-permute-start.4 = (bf16[128,2048]{1,0:T(8,128)(2,1)S(1)}, bf16[128,2048]{1,0:T(8,128)(2,1)S(1)}, u32[]{:S(2)}, u32[]{:S(2)}) collective-permute-start(bf16[128,2048]{1,0:T(8,128)(2,1)S(1)} %get-tuple-element.66), channel_id=1, source_target_pairs={{0,2},{1,3},{2,0},{3,1},{4,6},{5,7},{6,4},{7,5},{8,10},{9,11},{10,... | collective-permute-start | bytes 1572872 | tf_op jit(solution)/shard_map/ppermute | solution.py:75
  129.9 14.9 %collective-permute-start.1 = (bf16[128,2048]{1,0:T(8,128)(2,1)S(1)}, bf16[128,2048]{1,0:T(8,128)(2,1)S(1)}, u32[]{:S(2)}, u32[]{:S(2)}) collective-permute-start(bf16[128,2048]{1,0:T(8,128)(2,1)S(1)} %get-tuple-element.68), channel_id=1, source_target_pairs={{0,1},{1,0},{2,3},{3,2},{4,5},{5,4},{6,7},{7,6},{8,9},{9,8},{10,11... | collective-permute-start | bytes 1572872 | tf_op jit(solution)/shard_map/ppermute | solution.py:75
  131.4 24.6 %collective-permute-start = (bf16[128,2048]{1,0:T(8,128)(2,1)}, bf16[128,2048]{1,0:T(8,128)(2,1)S(1)}, u32[]{:S(2)}, u32[]{:S(2)}) collective-permute-start(bf16[128,2048]{1,0:T(8,128)(2,1)} %get-tuple-element.65), channel_id=1, source_target_pairs={{0,1},{1,0},{2,3},{3,2},{4,5},{5,4},{6,7},{7,6},{8,9},{9,8},{10,11... | collective-permute-start | bytes 1572872 | tf_op jit(solution)/shard_map/ppermute | solution.py:75
  145.1 15.0 %collective-permute-start.2 = (bf16[128,2048]{1,0:T(8,128)(2,1)S(1)}, bf16[128,2048]{1,0:T(8,128)(2,1)}, u32[]{:S(2)}, u32[]{:S(2)}) collective-permute-start(bf16[128,2048]{1,0:T(8,128)(2,1)S(1)} %get-tuple-element.69), channel_id=1, source_target_pairs={{0,2},{1,3},{2,0},{3,1},{4,6},{5,7},{6,4},{7,5},{8,10},{9,11},{10,... | collective-permute-start | bytes 1572872 | tf_op jit(solution)/shard_map/ppermute | solution.py:75
  146.7 20.2 %collective-permute-start.3 = (bf16[128,2048]{1,0:T(8,128)(2,1)}, bf16[128,2048]{1,0:T(8,128)(2,1)S(1)}, u32[]{:S(2)}, u32[]{:S(2)}) collective-permute-start(bf16[128,2048]{1,0:T(8,128)(2,1)} %get-tuple-element.67), channel_id=1, source_target_pairs={{0,2},{1,3},{2,0},{3,1},{4,6},{5,7},{6,4},{7,5},{8,10},{9,11},{10,... | collective-permute-start | bytes 1572872 | tf_op jit(solution)/shard_map/ppermute | solution.py:75
  147.2 19.7 %collective-permute-start.5 = (bf16[128,2048]{1,0:T(8,128)(2,1)S(1)}, bf16[128,2048]{1,0:T(8,128)(2,1)}, u32[]{:S(2)}, u32[]{:S(2)}) collective-permute-start(bf16[128,2048]{1,0:T(8,128)(2,1)S(1)} %get-tuple-element.70), channel_id=1, source_target_pairs={{0,1},{1,0},{2,3},{3,2},{4,5},{5,4},{6,7},{7,6},{8,9},{9,8},{10,11... | collective-permute-start | bytes 1572872 | tf_op jit(solution)/shard_map/ppermute | solution.py:75
  173.4 15.7 %collective-permute-start.9 = (bf16[128,2048]{1,0:T(8,128)(2,1)}, bf16[128,2048]{1,0:T(8,128)(2,1)S(1)}, u32[]{:S(2)}, u32[]{:S(2)}) collective-permute-start(bf16[128,2048]{1,0:T(8,128)(2,1)} %get-tuple-element.75), channel_id=1, source_target_pairs={{0,2},{1,3},{2,0},{3,1},{4,6},{5,7},{6,4},{7,5},{8,10},{9,11},{10,... | collective-permute-start | bytes 1572872 | tf_op jit(solution)/shard_map/ppermute | solution.py:75
  174.9 27.7 %collective-permute-start.7 = (bf16[128,2048]{1,0:T(8,128)(2,1)}, bf16[128,2048]{1,0:T(8,128)(2,1)}, u32[]{:S(2)}, u32[]{:S(2)}) collective-permute-start(bf16[128,2048]{1,0:T(8,128)(2,1)} %get-tuple-element.75), channel_id=1, source_target_pairs={{0,1},{1,0},{2,3},{3,2},{4,5},{5,4},{6,7},{7,6},{8,9},{9,8},{10,11... | collective-permute-start | bytes 1572872 | tf_op jit(solution)/shard_map/ppermute | solution.py:75
  175.2 25.9 %collective-permute-start.6 = (bf16[128,2048]{1,0:T(8,128)(2,1)}, bf16[128,2048]{1,0:T(8,128)(2,1)S(1)}, u32[]{:S(2)}, u32[]{:S(2)}) collective-permute-start(bf16[128,2048]{1,0:T(8,128)(2,1)} %get-tuple-element.76), channel_id=1, source_target_pairs={{0,1},{1,0},{2,3},{3,2},{4,5},{5,4},{6,7},{7,6},{8,9},{9,8},{10,11... | collective-permute-start | bytes 1572872 | tf_op jit(solution)/shard_map/ppermute | solution.py:75
  185.9 18.5 %collective-permute-start.8 = (bf16[128,2048]{1,0:T(8,128)(2,1)}, bf16[128,2048]{1,0:T(8,128)(2,1)}, u32[]{:S(2)}, u32[]{:S(2)}) collective-permute-start(bf16[128,2048]{1,0:T(8,128)(2,1)} %get-tuple-element.76), channel_id=1, source_target_pairs={{0,2},{1,3},{2,0},{3,1},{4,6},{5,7},{6,4},{7,5},{8,10},{9,11},{10,... | collective-permute-start | bytes 1572872 | tf_op jit(solution)/shard_map/ppermute | solution.py:75
  189.1 22.1 %collective-permute-start.11 = (bf16[128,2048]{1,0:T(8,128)(2,1)S(1)}, bf16[128,2048]{1,0:T(8,128)(2,1)S(1)}, u32[]{:S(2)}, u32[]{:S(2)}) collective-permute-start(bf16[128,2048]{1,0:T(8,128)(2,1)S(1)} %collective-permute-done.9), channel_id=1, source_target_pairs={{0,1},{1,0},{2,3},{3,2},{4,5},{5,4},{6,7},{7,6},{8,9},{9,8},{10,11... | collective-permute-start | bytes 1572872 | tf_op jit(solution)/shard_map/ppermute | solution.py:75
  255.0 13.5 %collective-permute-start.16 = (bf16[128,2048]{1,0:T(8,128)(2,1)S(1)}, bf16[128,2048]{1,0:T(8,128)(2,1)S(1)}, u32[]{:S(2)}, u32[]{:S(2)}) collective-permute-start(bf16[128,2048]{1,0:T(8,128)(2,1)S(1)} %get-tuple-element.60), channel_id=1, source_target_pairs={{0,2},{1,3},{2,0},{3,1},{4,6},{5,7},{6,4},{7,5},{8,10},{9,11},{10,... | collective-permute-start | bytes 1572872 | tf_op jit(solution)/shard_map/ppermute | solution.py:75
  255.6 14.9 %collective-permute-start.13 = (bf16[128,2048]{1,0:T(8,128)(2,1)S(1)}, bf16[128,2048]{1,0:T(8,128)(2,1)S(1)}, u32[]{:S(2)}, u32[]{:S(2)}) collective-permute-start(bf16[128,2048]{1,0:T(8,128)(2,1)S(1)} %get-tuple-element.62), channel_id=1, source_target_pairs={{0,1},{1,0},{2,3},{3,2},{4,5},{5,4},{6,7},{7,6},{8,9},{9,8},{10,11... | collective-permute-start | bytes 1572872 | tf_op jit(solution)/shard_map/ppermute | solution.py:75
  256.8 21.6 %collective-permute-start.12 = (bf16[128,2048]{1,0:T(8,128)(2,1)}, bf16[128,2048]{1,0:T(8,128)(2,1)}, u32[]{:S(2)}, u32[]{:S(2)}) collective-permute-start(bf16[128,2048]{1,0:T(8,128)(2,1)} %get-tuple-element.59), channel_id=1, source_target_pairs={{0,1},{1,0},{2,3},{3,2},{4,5},{5,4},{6,7},{7,6},{8,9},{9,8},{10,11... | collective-permute-start | bytes 1572872 | tf_op jit(solution)/shard_map/ppermute | solution.py:75
  271.8 9.5 %collective-permute-start.14 = (bf16[128,2048]{1,0:T(8,128)(2,1)}, bf16[128,2048]{1,0:T(8,128)(2,1)}, u32[]{:S(2)}, u32[]{:S(2)}) collective-permute-start(bf16[128,2048]{1,0:T(8,128)(2,1)} %get-tuple-element.63), channel_id=1, source_target_pairs={{0,2},{1,3},{2,0},{3,1},{4,6},{5,7},{6,4},{7,5},{8,10},{9,11},{10,... | collective-permute-start | bytes 1572872 | tf_op jit(solution)/shard_map/ppermute | solution.py:75
  273.3 13.6 %collective-permute-start.15 = (bf16[128,2048]{1,0:T(8,128)(2,1)}, bf16[128,2048]{1,0:T(8,128)(2,1)}, u32[]{:S(2)}, u32[]{:S(2)}) collective-permute-start(bf16[128,2048]{1,0:T(8,128)(2,1)} %get-tuple-element.61), channel_id=1, source_target_pairs={{0,2},{1,3},{2,0},{3,1},{4,6},{5,7},{6,4},{7,5},{8,10},{9,11},{10,... | collective-permute-start | bytes 1572872 | tf_op jit(solution)/shard_map/ppermute | solution.py:75
  274.0 13.0 %collective-permute-start.17 = (bf16[128,2048]{1,0:T(8,128)(2,1)}, bf16[128,2048]{1,0:T(8,128)(2,1)}, u32[]{:S(2)}, u32[]{:S(2)}) collective-permute-start(bf16[128,2048]{1,0:T(8,128)(2,1)} %get-tuple-element.64), channel_id=1, source_target_pairs={{0,1},{1,0},{2,3},{3,2},{4,5},{5,4},{6,7},{7,6},{8,9},{9,8},{10,11... | collective-permute-start | bytes 1572872 | tf_op jit(solution)/shard_map/ppermute | solution.py:75
  296.5 12.1 %collective-permute-start.21 = (bf16[128,2048]{1,0:T(8,128)(2,1)S(1)}, bf16[128,2048]{1,0:T(8,128)(2,1)S(1)}, u32[]{:S(2)}, u32[]{:S(2)}) collective-permute-start(bf16[128,2048]{1,0:T(8,128)(2,1)S(1)} %get-tuple-element.73), channel_id=1, source_target_pairs={{0,2},{1,3},{2,0},{3,1},{4,6},{5,7},{6,4},{7,5},{8,10},{9,11},{10,... | collective-permute-start | bytes 1572872 | tf_op jit(solution)/shard_map/ppermute | solution.py:75
  298.1 19.7 %collective-permute-start.19 = (bf16[128,2048]{1,0:T(8,128)(2,1)S(1)}, bf16[128,2048]{1,0:T(8,128)(2,1)S(1)}, u32[]{:S(2)}, u32[]{:S(2)}) collective-permute-start(bf16[128,2048]{1,0:T(8,128)(2,1)S(1)} %get-tuple-element.73), channel_id=1, source_target_pairs={{0,1},{1,0},{2,3},{3,2},{4,5},{5,4},{6,7},{7,6},{8,9},{9,8},{10,11... | collective-permute-start | bytes 1572872 | tf_op jit(solution)/shard_map/ppermute | solution.py:75
  298.4 18.8 %collective-permute-start.18 = (bf16[128,2048]{1,0:T(8,128)(2,1)S(1)}, bf16[128,2048]{1,0:T(8,128)(2,1)S(1)}, u32[]{:S(2)}, u32[]{:S(2)}) collective-permute-start(bf16[128,2048]{1,0:T(8,128)(2,1)S(1)} %get-tuple-element.74), channel_id=1, source_target_pairs={{0,1},{1,0},{2,3},{3,2},{4,5},{5,4},{6,7},{7,6},{8,9},{9,8},{10,11... | collective-permute-start | bytes 1572872 | tf_op jit(solution)/shard_map/ppermute | solution.py:75
  300.8 17.0 %collective-permute-start.20 = (bf16[128,2048]{1,0:T(8,128)(2,1)S(1)}, bf16[128,2048]{1,0:T(8,128)(2,1)S(1)}, u32[]{:S(2)}, u32[]{:S(2)}) collective-permute-start(bf16[128,2048]{1,0:T(8,128)(2,1)S(1)} %get-tuple-element.74), channel_id=1, source_target_pairs={{0,2},{1,3},{2,0},{3,1},{4,6},{5,7},{6,4},{7,5},{8,10},{9,11},{10,... | collective-permute-start | bytes 1572872 | tf_op jit(solution)/shard_map/ppermute | solution.py:75
  308.6 17.8 %collective-permute-start.23 = (bf16[128,2048]{1,0:T(8,128)(2,1)S(1)}, bf16[128,2048]{1,0:T(8,128)(2,1)S(1)}, u32[]{:S(2)}, u32[]{:S(2)}) collective-permute-start(bf16[128,2048]{1,0:T(8,128)(2,1)S(1)} %collective-permute-done.21), channel_id=1, source_target_pairs={{0,1},{1,0},{2,3},{3,2},{4,5},{5,4},{6,7},{7,6},{8,9},{9,8},{10,11... | collective-permute-start | bytes 1572872 | tf_op jit(solution)/shard_map/ppermute | solution.py:75
  735.7 40.8 %collective-permute-start.28 = (f32[1,4352]{1,0:T(1,128)S(1)}, f32[1,4352]{1,0:T(1,128)S(1)}, u32[]{:S(2)}, u32[]{:S(2)}) collective-permute-start(f32[1,4352]{1,0:T(1,128)S(1)} %add.191), channel_id=1, source_target_pairs={{0,16},{4,20},{8,24},{12,28},{16,0},{20,4},{24,8},{28,12},{1,17},{... | collective-permute-start | bytes 52232 | tf_op jit(solution)/shard_map/ppermute | solution.py:88
  (28 other events, 537.3 us)
Sparse Core Ops, SparseCore 0:
  96.2 90.0 all-gather.2

commit v5 on v4

--- a/solution.py
+++ b/solution.py
@@ -17,12 +17,6 @@
 EPS_NORM = 1e-06
 ROPE_BASE = 1000000.0
 NEG_FILL = -1e30
-
-
-def rms_scale(values, gain_vec):
-    return (
-        values * lax.rsqrt(jnp.mean(values * values, axis=-1, keepdims=True) + EPS_NORM) * gain_vec
-    )
 
 
 def row_layout(pair_len, row_count, head_dim):
@@ -36,58 +30,17 @@
     angles = position[..., None] * inv_freq
     angle_cos, angle_sin = jnp.cos(angles), jnp.sin(angles)
     return (
-        segment,
         jnp.concatenate([angle_cos, angle_cos], axis=-1),
         jnp.concatenate([angle_sin, angle_sin], axis=-1),
     )
 
 
-def times(left_side, right_side, out=jnp.float32):
-    return jnp.dot(left_side, right_side, preferred_element_type=jnp.float32).astype(out)
-
-
-def times_trans(left_side, right_side, out=jnp.float32):
-    return lax.dot_general(
-        left_side, right_side, (((1,), (1,)), ((), ())), preferred_element_type=jnp.float32
-    ).astype(out)
-
-
-def trans_times(left_side, right_side, out=jnp.float32):
-    return lax.dot_general(
-        left_side, right_side, (((0,), (0,)), ((), ())), preferred_element_type=jnp.float32
-    ).astype(out)
-
-
-def swiglu(gate_pre, up_pre):
-    return jax.nn.silu(gate_pre) * up_pre
-
-
 def in_f32(values):
     return values.astype(jnp.float32)
 
 
 def in_bf16(values):
     return values.astype(jnp.bfloat16)
-
-
-def shift(values, step):
-    n_fsdp = lax.axis_size("fsdp")
-    return lax.ppermute(values, "fsdp", [(i, i ^ step) for i in range(n_fsdp)])
-
-
-def sibling(values):
-    n_rep = lax.axis_size("rep")
-    return lax.ppermute(values, "rep", [(i, i ^ 1) for i in range(n_rep)])
-
-
-def sum_everywhere(values):
-    for axis in ("fsdp", "rep"):
-        n = lax.axis_size(axis)
-        step = 1
-        while step < n:
-            values = values + lax.ppermute(values, axis, [(i, i ^ step) for i in range(n)])
-            step *= 2
-    return values
 
 
 def flipped(index, step, n):
@@ -130,11 +83,13 @@
     (hidden, normed_mlp, gated, normed, grad_branch, grad_mlp, w_mlp, w_output, w_attn) = refs[:9]
     (middle, grad_result, tokens, attn_raw, all_cos, all_sin, all_q, all_k, all_v) = refs[9:18]
     (gains, head_gains, pair_ref) = refs[18:21]
-    (out, grad_attn, grad_raw, inb, xb, tokens_grad, gain_out, head_gain_out) = refs[21:29]
-    (lm, lo, rh, sb, kb, r1, c_slot, d_slot, big, wt, own, pbuf, land_a, land_b) = refs[29:43]
-    (mid, gres, tok, ga, wo, raw, cs, sn, qb, kvb, vb, gb, gg, ob) = refs[43:57]
-    (tile_sem, r1s, r1r, ins, inr, xs, xr, os_, fs, fr, gs, gr, ls) = refs[57:70]
-    (load_sem, first_sem, wt_sem, ps, pr, qs, qr, ag_s, ag_r, ag_l, block_sem) = refs[70:]
+    (out, grad_attn, grad_raw, inb, xb, tokens_grad, gain_out) = refs[21:28]
+    (lm, lo, rh, sb, kb, r1, c_slot, d_slot, big, wt, own, pbuf, land_a, land_b) = refs[28:42]
+    (mid, gres, tok, ga, wo, raw, cs, sn, qb, kvb, vb, gb, gg, ob) = refs[42:56]
+    (tile_sem, r1s, r1r, ins, inr, xs, xr, os_, fs, fr, gs, gr, ls) = refs[56:69]
+    (load_sem, first_sem, wt_sem, ps, pr, qs, qr, ag_s, ag_r, ag_l, block_sem) = refs[69:80]
+    (near_land, pair_land, in_land, far_land, near_s, near_r, line_s, line_r) = refs[80:]
+    head_gain_out = gain_out.at[:, pl.ds(own.shape[1], HD)]
     lefts = (hidden, normed_mlp, gated, normed)
     rights = (grad_branch, grad_mlp, grad_attn, grad_raw)
     total = sum(unit.count for unit in units)
@@ -416,19 +371,11 @@
                 pbuf[s - 1, :, tile_of(j)] = in_bf16(part)
                 p_copy(s, j).start()
 
-    def middle_back():
-        attn_load().start()
-        for copy in first_loads((2, 3)):
-            copy.wait()
-
-        def wait_tiles(j, carry):
-            for s in others:
-                p_copy(s, j).wait()
-            return carry
-
-        lax.fori_loop(0, TILES, wait_tiles, 0)
-        gain_out[...] = jnp.zeros_like(gain_out)
-        head_gain_out[...] = jnp.zeros_like(head_gain_out)
+    row_steps = rows // ROW_STEP
+
+    def middle_back(part):
+        if part == 0:
+            middle_sums()
 
         def some_rows(r, carry):
             cut = pl.ds(pl.multiple_of(r * ROW_STEP, ROW_STEP), ROW_STEP)
@@ -436,14 +383,30 @@
             for s in others:
                 grad += in_f32(land_a[s - 1, cut])
             back, gain_rows = norm_back(grad, mid[cut], gains[1:2])
-            gain_out[1:2] += jnp.sum(gain_rows, axis=0, keepdims=True)
+            gain_out[1:2, :width] += jnp.sum(gain_rows, axis=0, keepdims=True)
             back = gres[cut] + back
             gres[cut] = back
             ga[cut] = in_bf16(back)
             return carry
 
-        lax.fori_loop(0, rows // ROW_STEP, some_rows, 0)
-        gather.start()
+        lax.fori_loop(part * row_steps // 2, (part + 1) * row_steps // 2, some_rows, 0)
+        if part == 1:
+            gather.start()
+            for copy in block_loads(0):
+                copy.start()
+
+    def middle_sums():
+        attn_load().start()
+        for copy in first_loads((2, 3)):
+            copy.wait()
+
+        def wait_tiles(j, carry):
+            for s in others:
+                p_copy(s, j).wait()
+            return carry
+
+        lax.fori_loop(0, TILES, wait_tiles, 0)
+        gain_out[...] = jnp.zeros_like(gain_out)
 
     def block_loads(s):
         cut = pl.ds(pl.multiple_of(s * rows, rows), rows)
@@ -485,10 +448,6 @@
     early = heads_k // 2
 
     def block_first(s):
-        copies = block_loads(s)
-        for copy in copies:
-            copy.start()
-
         @pl.when(s == 0)
         def _():
             first_loads((5,))[0].wait()
@@ -507,7 +466,7 @@
             copy.wait()
 
         gg[...] = product_of(gb[...], wo[...], 1, 1)
-        for copy in copies:
+        for copy in block_loads(s):
             copy.wait()
         heads_back(s, range(early))
 
@@ -515,6 +474,11 @@
         heads_back(s, range(early, heads_k))
         store(s).start()
 
+        @pl.when(s + 1 < n_fsdp)
+        def _():
+            for copy in block_loads(s + 1):
+                copy.start()
+
     def block_third(s):
         store(s).wait()
 
@@ -541,10 +505,12 @@
         def _():
             q_copy(s).start()
 
-    def tokens_back():
-        first_loads((4,))[0].wait()
-        for s in others:
-            q_copy(s).wait()
+    def tokens_back(part):
+        if part == 0:
+            gather.sent()
+            first_loads((4,))[0].wait()
+            for s in others:
+                q_copy(s).wait()
 
         def some_rows(r, carry):
             cut = pl.ds(pl.multiple_of(r * ROW_STEP, ROW_STEP), ROW_STEP)
@@ -552,30 +518,101 @@
             for s in others:
                 grad += in_f32(land_b[s - 1, cut])
             back, gain_rows = norm_back(grad, in_f32(tok[cut]), gains[0:1])
-            gain_out[0:1] += jnp.sum(gain_rows, axis=0, keepdims=True)
+            gain_out[0:1, :width] += jnp.sum(gain_rows, axis=0, keepdims=True)
             tokens_grad[cut] = in_bf16(gres[cut] + back)
             return carry
 
-        lax.fori_loop(0, rows // ROW_STEP, some_rows, 0)
+        lax.fori_loop(part * row_steps // 2, (part + 1) * row_steps // 2, some_rows, 0)
+        if part == 1:
+            near_land[mine] = gain_out[...]
+            for s in others:
+                near_copy(s).start()
+
+
+    def near_copy(s):
+        return remote_copy(
+            gain_out,
+            near_land.at[mine],
+            near_s.at[s],
+            near_r.at[s],
+            rep,
+            flipped(mine, s, n_fsdp),
+        )
+
+    def line_copy(k, target, to_rep):
+        return remote_copy(gain_out, target, line_s.at[k], line_r.at[k], to_rep, mine)
+
+    def pair_copy():
+        return line_copy(0, pair_land, sib)
+
+    def gain_in():
+        return line_copy(1, in_land, inward)
+
+    def gain_across():
+        return line_copy(2, far_land, inward)
+
+    def gain_back():
+        return line_copy(3, far_land, outward)
+
+    def gains_near():
+        for s in others:
+            near_copy(s).wait()
+        summed = near_land[0]
+        for k in others:
+            summed += near_land[k]
+        gain_out[...] = summed
+        pair_copy().start()
+
+    def gains_pair():
+        pair_copy().wait()
+        gain_out[...] += pair_land[...]
+
+        @pl.when(depth == 0)
+        def _():
+            (gain_in if half > 1 else gain_across)().start()
+
+    def gains_in(k):
+        @pl.when(depth == k)
+        def _():
+            gain_in().wait_recv()
+            gain_out[...] += in_land[...]
+            (gain_in if k < half - 1 else gain_across)().start()
+
+    def gains_across():
+        @pl.when(at_middle)
+        def _():
+            gain_across().wait()
+            gain_out[...] += far_land[...]
+            if half > 1:
+                gain_back().start()
+
+    def gains_back(k):
+        @pl.when(depth == k)
+        def _():
+            gain_back().wait_recv()
+            gain_in().wait_send()
+            gain_out[...] = far_land[...]
+            if k > 0:
+                gain_back().start()
 
     def tasks(u, i):
         if u == 0:
-            pl.when(i < TILES)(lambda: mlp_products(i))
+            pl.when((i >= 4) & (i < 4 + TILES))(lambda: mlp_products(i - 4))
         if u == 1:
-            pl.when(i == 2)(middle_back)
-            pl.when(i == 6)(gather.forward)
-            pl.when(i == 12)(lambda: gather.own().wait())
-            last = 12 + 3 * (n_fsdp - 1)
-            busy = ((i >= 6) & (i < 9)) | ((i >= 12) & (i < last))
-            s = at_least(i, 9, units[1].count) * ((i - 9) // 3)
+            for part in range(2):
+                pl.when(i == 7 + part)(functools.partial(middle_back, part))
+            pl.when(i == 12)(gather.forward)
+            pl.when(i == 15)(lambda: gather.own().wait())
+            last = 15 + 3 * (n_fsdp - 1)
+            busy = ((i >= 9) & (i < 12)) | ((i >= 15) & (i < last))
+            s = at_least(i, 12, units[1].count) * ((i - 12) // 3)
             for phase, task in enumerate((block_first, block_second, block_third)):
                 pl.when(busy & (i % 3 == phase))(functools.partial(task, s))
-        if u == 2:
-
-            @pl.when(i == 2)
-            def _():
-                gather.sent()
-                tokens_back()
+        if u == 3:
+            for part in range(2):
+                pl.when(i == 2 + part)(functools.partial(tokens_back, part))
+            pl.when(i == 6)(gains_near)
+            pl.when(i == 8)(gains_pair)
 
     def product(left, right):
         return product_of(left, right, 0, 0)
@@ -649,6 +686,16 @@
         return carry
 
     lax.fori_loop(0, total, finish, 0)
+    for k in range(1, half):
+        gains_in(k)
+    gains_across()
+    for k in range(half - 2, -1, -1):
+        gains_back(k)
+    if half > 1:
+
+        @pl.when(depth > 0)
+        def _():
+            gain_back().wait_send()
 
 
 def backward(n_fsdp, n_rep, heads_k, units, piece_rows, piece_cols, args):
@@ -670,8 +717,7 @@
         ((total,) + piece, low),
         ((total,) + piece, low),
         ((rows, width), low),
-        ((8, width), full),
-        ((8, HD), full),
+        ((8, width + HD), full),
     )
     scratch = (
         ((2, rows_all, piece_rows), low),
@@ -709,7 +755,7 @@
         ),
         out_shape=[jax.ShapeDtypeStruct(shape, kind) for shape, kind in outs],
         in_specs=[any_spec] * 18 + [vmem] * 2 + [pl.BlockSpec(memory_space=pltpu.SMEM)],
-        out_specs=[any_spec] * 5 + [vmem] * 3,
+        out_specs=[any_spec] * 5 + [vmem] * 2,
         scratch_shapes=[pltpu.VMEM(shape, kind) for shape, kind in scratch]
         + [dma((2, 3))]
         + [dma((total,)) for _ in range(12)]
@@ -725,6 +771,14 @@
             dma((n_fsdp, 2)),
             dma,
             dma((8,)),
+            pltpu.VMEM((n_fsdp, 8, width + HD), full),
+            pltpu.VMEM((8, width + HD), full),
+            pltpu.VMEM((8, width + HD), full),
+            pltpu.VMEM((8, width + HD), full),
+            dma((n_fsdp,)),
+            dma((n_fsdp,)),
+            dma((4,)),
+            dma((4,)),
         ],
         compiler_params=pltpu.CompilerParams(
             collective_id=0, has_side_effects=True, vmem_limit_bytes=62 << 20
@@ -820,18 +874,26 @@
     return exponent / jnp.sum(exponent, axis=-1, keepdims=True)
 
 
-def attend_kernel(
-    heads_k, pair_ref, raw_ref, cos_ref, sin_ref, qg_ref, kg_ref, q_ref, k_ref, v_ref, gated_ref
+def attend(
+    heads_k,
+    allowed,
+    angle_cos,
+    angle_sin,
+    query_gain,
+    key_gain,
+    raw_ref,
+    q_ref,
+    k_ref,
+    v_ref,
+    gated_ref,
 ):
     group = H // KV
     cols_q, cols_k = heads_k * group * HD, heads_k * HD
-    allowed = block_mask(pair_ref, raw_ref.shape[0], pl.program_id(0))
-    angle_cos, angle_sin = cos_ref[...], sin_ref[...]
     for j in range(heads_k):
         own = slice(j * HD, (j + 1) * HD)
         keys = head_forward(
             raw_ref[:, 2 * cols_q + j * HD : 2 * cols_q + (j + 1) * HD],
-            kg_ref[...],
+            key_gain,
             angle_cos,
             angle_sin,
         )
@@ -841,7 +903,7 @@
         v_ref[:, own] = values
         for h in range(j * group, (j + 1) * group):
             cut = slice(h * HD, (h + 1) * HD)
-            queries = head_forward(raw_ref[:, cut], qg_ref[...], angle_cos, angle_sin)
+            queries = head_forward(raw_ref[:, cut], query_gain, angle_cos, angle_sin)
             q_ref[:, cut] = queries
             probs = in_bf16(softmax_of(queries, keys, allowed))
             context = product_of(probs, values, 1, 0)
@@ -907,45 +969,6 @@
         out_ref[:, value_start : value_start + HD] = in_bf16(grad_values)
 
 
-def rows_spec(rows, cols):
-    return pl.BlockSpec((rows, cols), lambda s: (s, 0))
-
-
-def whole_spec(shape):
-    return pl.BlockSpec(shape, lambda s: (0, 0))
-
-
-def attend(heads_k, rows, pair_len, raw, angle_cos, angle_sin, query_gain, key_gain):
-    rows_all, cols = raw.shape
-    cols_q, cols_k = heads_k * (H // KV) * HD, heads_k * HD
-    outs = (cols_q, cols_k, cols_k, cols_q)
-    return pl.pallas_call(
-        functools.partial(attend_kernel, heads_k),
-        grid=(rows_all // rows,),
-        in_specs=[
-            pl.BlockSpec(memory_space=pltpu.SMEM),
-            rows_spec(rows, cols),
-            rows_spec(rows, HD),
-            rows_spec(rows, HD),
-            whole_spec((1, HD)),
-            whole_spec((1, HD)),
-        ],
-        out_shape=[jax.ShapeDtypeStruct((rows_all, c), jnp.bfloat16) for c in outs],
-        out_specs=[rows_spec(rows, c) for c in outs],
-        cost_estimate=pl.CostEstimate(
-            flops=4 * rows_all * rows * cols_q,
-            bytes_accessed=8 * rows_all * cols,
-            transcendentals=rows_all * rows * heads_k * 2,
-        ),
-        compiler_params=pltpu.CompilerParams(vmem_limit_bytes=32 << 20),
-        name="attend",
-    )(pair_len, raw, angle_cos, angle_sin, query_gain, key_gain)
-
-
-def after(values, *others):
-    return lax.optimization_barrier((values, *others))[0]
-
-
 def remote_copy(src, dst, send, recv, to_rep, to_fsdp):
     return pltpu.make_async_remote_copy(
         src_ref=src,
@@ -1027,34 +1050,120 @@
         self.own().wait()
 
 
-def fetch_kernel(n_fsdp, n_rep, widths, ff, *refs):
-    (tokens, gains, wq, wg, wk, wv, w_gate, w_up) = refs[:8]
-    (tokens_all, gains_all, w_attn, mlp_part) = refs[8:12]
-    (ts, tr, tl, gs, gr, ws, wr, zs, zr, cs, cr, ms, mr, ls) = refs[12:]
+def forward_kernel(n_fsdp, n_rep, heads_k, *refs):
+    (tokens, gains, wq, wg, wk, wv, w_gate, w_up, w_output, w_down, teacher) = refs[:11]
+    (all_cos, all_sin, pair_ref, factor_ref) = refs[11:15]
+    (normed_all, raw_all, q_all, k_all, v_all, gated_all, w_attn, w_mlp) = refs[15:23]
+    (middle_out, nmlp_all, hidden_all, gbranch_all, gmlp_all, gres_out, block_out) = refs[23:30]
+    (gu_all, gain_out, head_gain_out, loss_out) = refs[30:34]
+    (tok, gl, wa, wo, wd, wm, nb, raw, cs, sn, qb, kvb, vb, gb, own, pbuf, land) = refs[34:51]
+    (mid, nm, te, gu, hb, gm) = refs[51:57]
+    (ts, tr, tl, us, ur, ul, bs, br, bl, gain_s, gain_r, ws, wr, zs, zr, cps, cpr) = refs[57:74]
+    (ms, mr, hs, hr, ss, sr, ps, pr, qs, qr, load, keep, mine_sem) = refs[74:]
+    rows, width = own.shape
+    cols, ff = raw.shape[1], hb.shape[1]
+    deep = wq.shape[0]
+    widths = tuple(w.shape[1] // n_fsdp for w in (wq, wg, wk, wv))
+    starts = [sum(widths[:i]) for i in range(4)]
+    others = range(1, n_fsdp)
+    n_line = n_rep // 2
     rep, mine = lax.axis_index("rep"), lax.axis_index("fsdp")
     core, place = rep % 2, rep // 2
     sib = rep + 1 - 2 * core
     partner = (place + 1 - 2 * (place % 2)) * 2 + core
-    deep = wq.shape[0]
-    block, part_rows = deep // 4, deep // n_rep
-    others = range(1, n_fsdp)
-    greet_all([(sib, mine), (partner, mine)] + [(rep, flipped(mine, s, n_fsdp)) for s in others])
-
-    weights = (wq, wg, wk, wv)
-    starts = [sum(widths[:i]) for i in range(4)]
+    block, part = deep // 4, deep // n_rep
     band = (place % 2) * 2 + core
     other_band = (1 - place % 2) * 2 + core
-
-    def gain_copy(s):
+    hops = range(1, n_line)
+    row_steps = rows // ROW_STEP
+    near = sorted({1, n_line - 1})
+    greet_all(
+        [(sib, mine)]
+        + [(((place + k) % n_line) * 2 + core, mine) for k in near]
+        + [(rep, flipped(mine, s, n_fsdp)) for s in others]
+    )
+
+
+    def columns(peer, wide):
+        return pl.ds(pl.multiple_of(peer * wide, wide), wide)
+
+    def mlp_copy(s, i):
+        peer = flipped(mine, s, n_fsdp)
         return remote_copy(
-            gains, gains_all.at[mine], gs.at[s], gr.at[s], rep, flipped(mine, s, n_fsdp)
-        )
+            (w_gate, w_up)[i].at[pl.ds(rep * part, part), columns(peer, ff)],
+            w_mlp.at[pl.ds(mine * deep + rep * part, part), pl.ds(i * ff, ff)],
+            ms.at[s, i],
+            mr.at[s, i],
+            rep,
+            peer,
+        )
+
+    def part_at(s, of_rep):
+        return w_mlp.at[pl.ds(flipped(mine, s, n_fsdp) * deep + of_rep * part, part)]
+
+    def line_copy(s, k, up):
+        step = 1 if up else -1
+        src = part_at(s, ((place - step * (k - 1) + n_line) % n_line) * 2 + core)
+        to_rep = ((place + step + n_line) % n_line) * 2 + core
+        way = 0 if up else 1
+        return remote_copy(src, src, hs.at[way, s, k], hr.at[way, s, k], to_rep, mine)
+
+    def line_sends(k):
+        for up in (True, False):
+            first, last = (k - 1, n_line - 2) if up else (1, n_line - k)
+
+            @pl.when((place >= first) & (place <= last))
+            def _(up=up):
+                for s in others:
+                    line_copy(s, k, up).start()
+
+    def line_arrivals(k):
+        for up in (True, False):
+            first, last = (k, n_line - 1) if up else (0, n_line - 1 - k)
+
+            @pl.when((place >= first) & (place <= last))
+            def _(up=up):
+                for s in others:
+                    line_copy(s, k, up).wait_recv()
+                    share_copy(s, k, up).start()
+
+        if k + 1 < n_line:
+            line_sends(k + 1)
+
+    def share_copy(s, k, up):
+        step = 1 if up else -1
+        src = part_at(s, ((place - step * k + n_line) % n_line) * 2 + core)
+        way = 0 if up else 1
+        return remote_copy(src, src, ss.at[way, s, k], sr.at[way, s, k], sib, mine)
+
+    def shares(action):
+        for s in others:
+            action(share_copy(s, 0, True))
+        for k in hops:
+            for up in (True, False):
+                first, last = (k, n_line - 1) if up else (0, n_line - 1 - k)
+
+                @pl.when((place >= first) & (place <= last))
+                def _(k=k, up=up):
+                    for s in others:
+                        action(share_copy(s, k, up))
+
+    def lines_sent():
+        for k in hops:
+            for up in (True, False):
+                first, last = (k - 1, n_line - 2) if up else (1, n_line - k)
+
+                @pl.when((place >= first) & (place <= last))
+                def _(k=k, up=up):
+                    for s in others:
+                        line_copy(s, k, up).wait_send()
+
+    weights = (wq, wg, wk, wv)
 
     def weight_copy(s, i):
         peer = flipped(mine, s, n_fsdp)
-        cols = pl.ds(pl.multiple_of(peer * widths[i], widths[i]), widths[i])
         return remote_copy(
-            weights[i].at[pl.ds(band * block, block), cols],
+            weights[i].at[pl.ds(band * block, block), columns(peer, widths[i])],
             w_attn.at[pl.ds(mine * deep + band * block, block), pl.ds(starts[i], widths[i])],
             ws.at[s, i],
             wr.at[s, i],
@@ -1071,125 +1180,479 @@
     def sibling_copy(s, k):
         which = band if k == 0 else other_band
         return remote_copy(
-            band_at(s, which), band_at(s, which), cs.at[s, k], cr.at[s, k], sib, mine
-        )
-
-    def mlp_copy(s, i):
-        peer = flipped(mine, s, n_fsdp)
-        cols = pl.ds(pl.multiple_of(peer * ff, ff), ff)
+            band_at(s, which), band_at(s, which), cps.at[s, k], cpr.at[s, k], sib, mine
+        )
+
+    def gain_copy(s):
         return remote_copy(
-            (w_gate, w_up)[i].at[pl.ds(rep * part_rows, part_rows), cols],
-            mlp_part.at[s - 1, :, pl.ds(i * ff, ff)],
-            ms.at[s, i],
-            mr.at[s, i],
-            rep,
-            peer,
-        )
-
-    def own_copy(i):
-        cols = pl.ds(pl.multiple_of(mine * widths[i], widths[i]), widths[i])
-        return pltpu.make_async_copy(
-            weights[i].at[:, cols],
-            w_attn.at[pl.ds(mine * deep, deep), pl.ds(starts[i], widths[i])],
-            ls.at[i],
-        )
-
-    own_gain = pltpu.make_async_copy(gains, gains_all.at[mine], ls.at[4])
-    rows = GatherRows(n_fsdp, rep, mine, tokens, tokens_all, (ts, tr, tl))
+            gains, gl.at[mine], gain_s.at[s], gain_r.at[s], rep, flipped(mine, s, n_fsdp)
+        )
+
+    mine_rows = pl.ds(mine * deep, deep)
+    mine_pairs = [
+        (weights[i].at[:, columns(mine, widths[i])], w_attn.at[mine_rows, pl.ds(starts[i], widths[i])])
+        for i in range(4)
+    ]
+    mine_pairs += [
+        (w.at[:, columns(mine, ff)], w_mlp.at[mine_rows, pl.ds(i * ff, ff)])
+        for i, w in enumerate((w_gate, w_up))
+    ]
+    mine_pairs += [(gains, gl.at[mine]), (w_output, wo), (w_down, wd), (teacher, te)]
+
+    def local(which):
+        return [pltpu.make_async_copy(*mine_pairs[i], mine_sem.at[i]) for i in which]
+
+    def attn_load():
+        return pltpu.make_async_copy(w_attn, wa, load.at[0])
+
+    def mlp_load():
+        return pltpu.make_async_copy(w_mlp, wm, load.at[1])
+
+    token_rows = GatherRows(n_fsdp, rep, mine, tokens, tok, (ts, tr, tl))
+    up_rows = GatherRows(n_fsdp, rep, mine, nm, nmlp_all, (us, ur, ul))
+    back_rows = GatherRows(n_fsdp, rep, mine, nm, gbranch_all, (bs, br, bl))
+
     for s in others:
         gain_copy(s).start()
         for i in range(4):
             weight_copy(s, i).start()
-    rows.start()
-    own_gain.start()
-    for i in range(4):
-        own_copy(i).start()
+    token_rows.start()
+    for copy in local(range(10)):
+        copy.start()
     for s in others:
         for i in range(4):
             weight_copy(s, i).wait_recv()
         partner_copy(s).start()
         sibling_copy(s, 0).start()
-    rows.forward()
     for s in others:
         for i in range(2):
             mlp_copy(s, i).start()
+    token_rows.forward()
+    local((6,))[0].wait()
+    gain_out[...] = jnp.zeros_like(gain_out)
+    head_gain_out[...] = jnp.zeros_like(head_gain_out)
+    for s in others:
+        gain_copy(s).wait()
+    lines = deep // HD
+    for f in range(n_fsdp):
+        piece = in_f32(gl[f])
+        for kind in range(2):
+            for r in range(lines):
+                at = f * deep + r * HD
+                gain_out[kind : kind + 1, at : at + HD] = piece[
+                    kind * lines + r : kind * lines + r + 1
+                ]
+            head_gain_out[kind : kind + 1] += piece[2 * lines + kind : 2 * lines + kind + 1]
     for s in others:
         partner_copy(s).wait_recv()
         sibling_copy(s, 1).start()
-    rows.finish()
     for s in others:
-        gain_copy(s).wait()
+        for k in range(2):
+            sibling_copy(s, k).wait_recv()
+    for copy in local((0, 1, 2, 3)):
+        copy.wait()
+    attn_load().start()
+    for s in others:
+        for i in range(2):
+            mlp_copy(s, i).wait_recv()
+        share_copy(s, 0, True).start()
+    line_sends(1)
+    for copy in local((7, 8, 9)):
+        copy.wait()
+
+    def block_rows(s):
+        return pl.ds(pl.multiple_of(s * rows, rows), rows)
+
+    def some_rows(base, r):
+        return pl.ds(pl.multiple_of(base + r * ROW_STEP, ROW_STEP), ROW_STEP)
+
+    def tiled(count, wide, body):
+        def one(j, carry):
+            body(pl.ds(pl.multiple_of(j * wide, wide), wide))
+            return carry
+
+        lax.fori_loop(0, count, one, 0)
+
+    def by_rows(body):
+        def one(r, carry):
+            body(r)
+            return carry
+
+        lax.fori_loop(0, row_steps, one, 0)
+
+    tile = width // 4
+
+    def leave(s, left, right):
+        def one(cut):
+            product = product_of(left[...], right[:, cut], 1, 0)
+
+            @pl.when(s == 0)
+            def _():
+                own[:, cut] = product
+
+            @pl.when(s > 0)
+            def _():
+                pbuf[s - 1, :, cut] = in_bf16(product)
+
+        tiled(4, tile, one)
+
+    def out_copy(s, sends, recvs):
+        return remote_copy(
+            pbuf.at[s - 1],
+            land.at[s - 1],
+            sends.at[s],
+            recvs.at[s],
+            rep,
+            flipped(mine, s, n_fsdp),
+        )
+
+    def summed(cut):
+        total = own[cut]
+        for s in others:
+            total += in_f32(land[s - 1, cut])
+        return total
+
+    def scaled(values, gain):
+        scale = lax.rsqrt(jnp.mean(values * values, axis=-1, keepdims=True) + EPS_NORM)
+        return in_bf16(values * scale * gain)
+
+
+    def attention_stores(s):
+        cut = block_rows(s)
+        pairs = (
+            (nb, normed_all), (raw, raw_all), (qb, q_all), (kvb, k_all), (vb, v_all), (gb, gated_all)
+        )
+        return [
+            pltpu.make_async_copy(src, dst.at[cut], keep.at[i])
+            for i, (src, dst) in enumerate(pairs)
+        ]
+
+    def angle_loads(s):
+        cut = block_rows(s)
+        return [
+            pltpu.make_async_copy(all_cos.at[cut], cs, load.at[2]),
+            pltpu.make_async_copy(all_sin.at[cut], sn, load.at[3]),
+        ]
+
+    def attention(i, carry):
+        s = (i + 1) % n_fsdp
+        for copy in angle_loads(s):
+            copy.start()
+        for k in range(n_fsdp):
+
+            @pl.when(s == k)
+            def _(k=k):
+                if k == 0:
+                    token_rows.own().wait()
+                else:
+                    token_rows.arrive(k)
+
+        @pl.when(i > 0)
+        def _():
+            for copy in attention_stores(s):
+                copy.wait()
+
+        def normed_rows(r):
+            values = in_f32(tok[some_rows(s * rows, r)])
+            nb[some_rows(0, r)] = scaled(values, gain_out[0:1])
+
+        by_rows(normed_rows)
+
+        @pl.when(i == 0)
+        def _():
+            attn_load().wait()
+
+        def raw_tile(cut):
+            raw[:, cut] = product_of(nb[...], wa[:, cut], 1, 0)
+
+        tiled(3, cols // 3, raw_tile)
+        for copy in angle_loads(s):
+            copy.wait()
+        attend(
+            heads_k,
+            block_mask(pair_ref, rows, s),
+            cs[...],
+            sn[...],
+            head_gain_out[0:1],
+            head_gain_out[1:2],
+            raw,
+            qb,
+            kvb,
+            vb,
+            gb,
+        )
+        for copy in attention_stores(s):
+            copy.start()
+        leave(s, gb, wo)
+
+        @pl.when(s > 0)
+        def _():
+            out_copy(s, ps, pr).start()
+
+        return carry
+
+    lax.fori_loop(0, n_fsdp, attention, 0)
+    for k in range(1, n_line // 2):
+        line_arrivals(k)
+    for s in others:
+        out_copy(s, ps, pr).wait()
+
+    def middle_rows(r):
+        cut = some_rows(0, r)
+        values = in_f32(tok[cut]) + summed(cut)
+        mid[cut] = values
+        nm[cut] = scaled(values, gain_out[1:2])
+
+    by_rows(middle_rows)
+    up_rows.start()
+
+    def middle_store():
+        return pltpu.make_async_copy(mid, middle_out, load.at[4])
+
+    middle_store().start()
+    for copy in attention_stores(0):
+        copy.wait()
+
+
+    for k in range(n_line // 2, n_line - 1):
+        line_arrivals(k)
+    up_rows.forward()
+    line_arrivals(n_line - 1)
+    shares(lambda copy: copy.wait_recv())
+    for copy in local((4, 5)):
+        copy.wait()
+    mlp_load().start()
+    mlp_load().wait()
+
+    def block_load(source, s):
+        return pltpu.make_async_copy(source.at[block_rows(s)], nb, load.at[2])
+
+    def ff_stores(s):
+        cut = block_rows(s)
+        return [
+            pltpu.make_async_copy(hb, hidden_all.at[cut], keep.at[0]),
+            pltpu.make_async_copy(gu, gu_all.at[cut], keep.at[1]),
+        ]
+
+    def into_nb(gather, source, s):
+        @pl.when(s == 0)
+        def _():
+            nb[...] = nm[...]
+
+        for k in others:
+
+            @pl.when(s == k)
+            def _(k=k):
+                gather.arrive(k)
+
+        @pl.when(s > 0)
+        def _():
+            copy = block_load(source, s)
+            copy.start()
+            copy.wait()
+
+    def feed_forward(i, carry):
+        s = (i + 1) % n_fsdp
+        into_nb(up_rows, nmlp_all, s)
+
+        @pl.when(i > 0)
+        def _():
+            for copy in ff_stores(s):
+                copy.wait()
+
+        def pre_tile(cut):
+            gu[:, cut] = product_of(nb[...], wm[:, cut], 1, 0)
+
+        tiled(6, ff // 3, pre_tile)
+
+        def hidden_rows(r):
+            cut = some_rows(0, r)
+            gate_pre = gu[cut, :ff]
+            hb[cut] = in_bf16(gate_pre * jax.nn.sigmoid(gate_pre) * gu[cut, ff:])
+
+        by_rows(hidden_rows)
+        for copy in ff_stores(s):
+            copy.start()
+        leave(s, hb, wd)
+
+        @pl.when(s > 0)
+        def _():
+            out_copy(s, qs, qr).start()
+
+        return carry
+
+    lax.fori_loop(0, n_fsdp, feed_forward, 0)
+    up_rows.sent()
+    up_rows.own().wait()
+    middle_store().wait()
+    for copy in ff_stores(0):
+        copy.wait()
+
+
+    def gu_load(s):
+        return pltpu.make_async_copy(gu_all.at[block_rows(s)], gu, load.at[5])
+
+    gu_load(0).start()
+    for s in others:
+        out_copy(s, qs, qr).wait()
+    head_len = pair_ref[0, 0]
+    both_len = head_len + pair_ref[0, 1]
+    loss_out[...] = jnp.zeros_like(loss_out)
+
+    def error_rows(r):
+        cut = some_rows(0, r)
+        index = r * ROW_STEP + lax.broadcasted_iota(jnp.int32, (ROW_STEP, 1), 0)
+        valid = (index < both_len).astype(jnp.float32)
+        result = mid[cut] + summed(cut)
+        error = (result - in_f32(te[cut])) * valid
+        square = jnp.sum(error * error, axis=-1, keepdims=True)
+        first = jnp.where(index < head_len, square, 0.0)
+        loss_out[0:1] += jnp.sum(first, axis=0, keepdims=True)
+        loss_out[1:2] += jnp.sum(square - first, axis=0, keepdims=True)
+        te[cut] = in_bf16(result * valid)
+        grad = error * factor_ref[0, 0]
+        mid[cut] = grad
+        nm[cut] = in_bf16(grad)
+
+    by_rows(error_rows)
+    back_rows.start()
+    last_stores = [
+        pltpu.make_async_copy(te, block_out, load.at[3]),
+        pltpu.make_async_copy(mid, gres_out, load.at[4]),
+    ]
+    for copy in last_stores:
+        copy.start()
+
+    def grad_store(s):
+        return pltpu.make_async_copy(gm, gmlp_all.at[block_rows(s)], keep.at[2])
+
+    def feed_back(s, carry):
+        @pl.when(s == 1)
+        def _():
+            back_rows.forward()
+
+        into_nb(back_rows, gbranch_all, s)
+
+        def hidden_tile(cut):
+            raw[:, cut] = product_of(nb[...], wd[cut], 1, 1)
+
+        tiled(3, ff // 3, hidden_tile)
+        gu_load(s).wait()
+
+        @pl.when(s > 0)
+        def _():
+            grad_store(s).wait()
+
+        def grad_rows(r):
+            cut = some_rows(0, r)
+            gate_pre, grad = gu[cut, :ff], raw[cut]
+            gate = jax.nn.sigmoid(gate_pre)
+            silu = gate_pre * gate
+            gm[cut, :ff] = in_bf16(grad * gu[cut, ff:] * (gate + silu * (1.0 - gate)))
+            gm[cut, ff:] = in_bf16(grad * silu)
+
+        by_rows(grad_rows)
+        grad_store(s).start()
+
+        @pl.when(s + 1 < n_fsdp)
+        def _():
+            gu_load(s + 1).start()
+
+        return carry
+
+    lax.fori_loop(0, n_fsdp, feed_back, 0)
+
+    grad_store(0).wait()
+    for copy in last_stores:
+        copy.wait()
+    back_rows.sent()
+    back_rows.own().wait()
+    token_rows.sent()
+    for s in others:
         partner_copy(s).wait_send()
         for i in range(4):
             weight_copy(s, i).wait_send()
         for i in range(2):
-            sibling_copy(s, i).wait()
-            mlp_copy(s, i).wait()
-    own_gain.wait()
-    for i in range(4):
-        own_copy(i).wait()
-
-
-def fetched(n_fsdp, n_rep, widths, ff, tokens, gains, *weights):
-    deep = weights[0].shape[0]
-    rows, width = tokens.shape
+            sibling_copy(s, i).wait_send()
+            mlp_copy(s, i).wait_send()
+    lines_sent()
+    shares(lambda copy: copy.wait_send())
+
+
+def forward(n_fsdp, n_rep, heads_k, args):
+    rows, width = args[0].shape
+    rows_all = n_fsdp * rows
+    cols_q, cols_k = heads_k * (H // KV) * HD, heads_k * HD
+    cols = 2 * cols_q + 2 * cols_k
+    ff = args[9].shape[0]
+    n_line = n_rep // 2
+    low, full = jnp.bfloat16, jnp.float32
     dma = pltpu.SemaphoreType.DMA
     any_spec = pl.BlockSpec(memory_space=pl.ANY)
-    shapes = (
-        (n_fsdp * rows, width),
-        (n_fsdp,) + gains.shape,
-        (n_fsdp * deep, sum(widths)),
-        (n_fsdp - 1, deep // n_rep, 2 * ff),
+    vmem, smem = pl.BlockSpec(memory_space=pltpu.VMEM), pl.BlockSpec(memory_space=pltpu.SMEM)
+    outs = (
+        ((rows_all, width), low),
+        ((rows_all, cols), full),
+        ((rows_all, cols_q), low),
+        ((rows_all, cols_k), low),
+        ((rows_all, cols_k), low),
+        ((rows_all, cols_q), low),
+        ((width, cols), low),
+        ((width, 2 * ff), low),
+        ((rows, width), full),
+        ((rows_all, width), low),
+        ((rows_all, ff), low),
+        ((rows_all, width), low),
+        ((rows_all, 2 * ff), low),
+        ((rows, width), full),
+        ((rows, width), low),
+        ((rows_all, 2 * ff), full),
+        ((8, width), full),
+        ((8, HD), full),
+        ((8, HD), full),
     )
-    pair, four = dma((n_fsdp, 2)), dma((n_fsdp, 4))
-    one = dma((n_fsdp,))
+    scratch = (
+        ((rows_all, width), low),
+        ((n_fsdp, 16, HD), low),
+        ((width, cols), low),
+        ((cols_q, width), low),
+        ((ff, width), low),
+        ((width, 2 * ff), low),
+        ((rows, width), low),
+        ((rows, cols), full),
+        ((rows, HD), full),
+        ((rows, HD), full),
+        ((rows, cols_q), low),
+        ((rows, cols_k), low),
+        ((rows, cols_k), low),
+        ((rows, cols_q), low),
+        ((rows, width), full),
+        ((n_fsdp - 1, rows, width), low),
+        ((n_fsdp - 1, rows, width), low),
+        ((rows, width), full),
+        ((rows, width), low),
+        ((rows, width), low),
+        ((rows, 2 * ff), full),
+        ((rows, ff), low),
+        ((rows, 2 * ff), low),
+    )
+    one, pair, four = dma((n_fsdp,)), dma((n_fsdp, 2)), dma((n_fsdp, 4))
+    line = dma((2, n_fsdp, n_line))
     return pl.pallas_call(
-        functools.partial(fetch_kernel, n_fsdp, n_rep, widths, ff),
-        out_shape=[jax.ShapeDtypeStruct(shape, jnp.bfloat16) for shape in shapes],
-        in_specs=[any_spec] * 8,
-        out_specs=[any_spec] * 4,
-        scratch_shapes=[
-            pair, pair, dma, one, one, four, four, one, one, pair, pair, pair, pair, dma((5,))
-        ],
-        compiler_params=pltpu.CompilerParams(collective_id=1, has_side_effects=True),
-        name="fetch",
-    )(tokens, gains, *weights)
-
-
-def gather_rows(block):
-    n_fsdp = lax.axis_size("fsdp")
-    if n_fsdp != 4:
-        return [block] + [shift(block, s) for s in range(1, n_fsdp)]
-    half = block.shape[0] // 2
-    top, low = block[:half], block[half:]
-    x_top, y_low = shift(top, 1), shift(low, 2)
-    x_low, y_top = shift(low, 1), shift(top, 2)
-    d_top, d_low = shift(x_top, 2), shift(y_low, 1)
-    return [
-        block,
-        jnp.concatenate([x_top, x_low]),
-        jnp.concatenate([y_top, y_low]),
-        jnp.concatenate([d_top, d_low]),
-    ]
-
-
-def scatter_rows(own, parts):
-    n_fsdp = lax.axis_size("fsdp")
-    if n_fsdp != 4:
-        for s in range(1, n_fsdp):
-            own = own + in_f32(shift(parts[s - 1], s))
-        return own
-    half = own.shape[0] // 2
-    p_x, p_y, p_d = parts
-    r_y = shift(p_d[:half], 1)
-    r_x = shift(p_d[half:], 2)
-    x_top = shift(p_x[:half], 1)
-    y_low = shift(p_y[half:], 2)
-    y_top = shift(in_bf16(in_f32(p_y[:half]) + in_f32(r_y)), 2)
-    x_low = shift(in_bf16(in_f32(p_x[half:]) + in_f32(r_x)), 1)
-    return own + jnp.concatenate(
-        [in_f32(x_top) + in_f32(y_top), in_f32(y_low) + in_f32(x_low)]
-    )
+        functools.partial(forward_kernel, n_fsdp, n_rep, heads_k),
+        out_shape=[jax.ShapeDtypeStruct(shape, kind) for shape, kind in outs],
+        in_specs=[any_spec] * 13 + [smem] * 2,
+        out_specs=[any_spec] * 16 + [vmem] * 3,
+        scratch_shapes=[pltpu.VMEM(shape, kind) for shape, kind in scratch]
+        + [pair, pair, dma] * 3
+        + [one, one, four, four, one, one, pair, pair]
+        + [pair, pair, line, line, line, line, one, one, one, one]
+        + [dma((6,)), dma((6,)), dma((10,))],
+        compiler_params=pltpu.CompilerParams(
+            collective_id=1, has_side_effects=True, vmem_limit_bytes=62 << 20
+        ),
+        name="forward",
+    )(*args)
 
 
 def shards(
@@ -1234,85 +1697,68 @@
     ).reshape(n_fsdp, 2)
     token_count = jnp.sum(lengths).astype(jnp.float32)
     factor = rows * n_rep * n_fsdp / (2.0 * token_count)
-    segments, angle_cos, angle_sin = row_layout(pair_len, rows, HD)
+    angle_cos, angle_sin = row_layout(pair_len, rows, HD)
     angle_cos, angle_sin = angle_cos.reshape(rows_all, HD), angle_sin.reshape(rows_all, HD)
-    segment = segments[0]
-    valid_row = (segment < 2).astype(jnp.float32)
 
     small = query_gain.shape[0]
-    gains_own = jnp.concatenate([attention_gain, mlp_gain, query_gain, key_gain])
-    gains_own = jnp.pad(gains_own, (0, 16 * HD - gains_own.shape[0])).reshape(16, HD)
-    tokens_all, gains, w_attn, mlp_part = fetched(
+
+    def spread(gain):
+        return lax.dynamic_update_slice(
+            jnp.zeros((1, HD), jnp.bfloat16), gain[None], (0, mine * small)
+        )
+
+    gain_block = jnp.concatenate(
+        [
+            attention_gain.reshape(-1, HD),
+            mlp_gain.reshape(-1, HD),
+            spread(query_gain),
+            spread(key_gain),
+            jnp.zeros((14 - 2 * deep // HD, HD), jnp.bfloat16),
+        ]
+    )
+    (
+        normed_all,
+        attn_raw,
+        queries_b,
+        keys_b,
+        values_b,
+        gated_b,
+        w_attn,
+        w_mlp,
+        middle,
+        normed_mlp_all,
+        hidden_b,
+        grad_branch_all,
+        grad_mlp_b,
+        grad_result,
+        block_out,
+        _,
+        gain_rows,
+        head_gains,
+        losses,
+    ) = forward(
         n_fsdp,
         n_rep,
-        (cols_q, cols_q, cols_k, cols_k),
-        ff,
-        tokens,
-        gains_own,
-        w_query,
-        w_outgate,
-        w_key,
-        w_value,
-        w_gate,
-        w_up,
+        heads_k,
+        (
+            tokens,
+            gain_block,
+            w_query,
+            w_outgate,
+            w_key,
+            w_value,
+            w_gate,
+            w_up,
+            w_output,
+            w_down,
+            teacher,
+            angle_cos,
+            angle_sin,
+            pair_len,
+            (2.0 * factor).reshape(1, 1),
+        ),
     )
-    gains = in_f32(gains.reshape(n_fsdp, 16 * HD))
-    attention_gain_f = gains[:, :deep].reshape(-1)
-    mlp_gain_f = gains[:, deep : 2 * deep].reshape(-1)
-    query_gain_f = gains[:, 2 * deep : 2 * deep + small].reshape(-1)
-    key_gain_f = gains[:, 2 * deep + small : 2 * deep + 2 * small].reshape(-1)
-
-    mlp_parts = lax.all_gather(mlp_part, "rep", axis=0)
-    w_mlp = jnp.zeros((n_fsdp * deep, 2 * ff), jnp.bfloat16)
-    for i, weight in enumerate((w_gate, w_up)):
-        own = lax.dynamic_slice(weight, (0, mine * ff), (deep, ff))
-        w_mlp = lax.dynamic_update_slice(w_mlp, own, (mine * deep, i * ff))
-    for s in others:
-        rows_of = mlp_parts[:, s - 1].reshape(deep, 2 * ff)
-        w_mlp = lax.dynamic_update_slice(w_mlp, rows_of, ((mine ^ s) * deep, 0))
-
-    tokens_f = in_f32(tokens)
-    normed_all = in_bf16(rms_scale(in_f32(tokens_all), attention_gain_f))
-    attn_raw = times(normed_all, w_attn)
-    head_args = (
-        heads_k,
-        rows,
-        pair_len,
-        attn_raw,
-        angle_cos,
-        angle_sin,
-        query_gain_f[None],
-        key_gain_f[None],
-    )
-    queries_b, keys_b, values_b, gated_b = attend(*head_args)
-
-    def summed(left, right, product):
-        own = product(left[:rows], right, jnp.float32)
-        parts = product(left[rows:], right, jnp.bfloat16)
-        return scatter_rows(own, [parts[i * rows : (i + 1) * rows] for i in range(n_fsdp - 1)])
-
-    middle = tokens_f + summed(gated_b, w_output, times)
-    normed_mlp = rms_scale(middle, mlp_gain_f)
-    normed_mlp_all = jnp.concatenate(gather_rows(in_bf16(normed_mlp)))
-    gate_pre = times(normed_mlp_all, w_mlp[:, :ff])
-    up_pre = times(normed_mlp_all, w_mlp[:, ff:])
-    hidden, swiglu_back = jax.vjp(swiglu, gate_pre, up_pre)
-    hidden_b = in_bf16(hidden)
-    result = middle + summed(hidden_b, w_down, times)
-
-    error_rows = (result - in_f32(teacher)) * valid_row[:, None]
-    row_sq = jnp.sum(error_rows * error_rows, axis=-1)
-    slot_mask = (segment[:, None] == jnp.arange(2, dtype=jnp.int32)[None, :]).astype(jnp.float32)
-    seq_loss = jnp.sum(row_sq[:, None] * slot_mask, axis=0) / (2.0 * token_count)
-    block_out = in_bf16(result * valid_row[:, None])
-    grad_result = 2.0 * factor * error_rows
-
-    grad_branch_all = jnp.concatenate(gather_rows(in_bf16(grad_result)))
-    grad_hidden = times_trans(grad_branch_all, w_down)
-    grad_gate_pre, grad_up_pre = swiglu_back(grad_hidden)
-    grad_gate_b = in_bf16(grad_gate_pre)
-    grad_up_b = in_bf16(grad_up_pre)
-    grad_mlp_b = jnp.concatenate([grad_gate_b, grad_up_b], axis=1)
+    seq_loss = losses[:2, 0] / (2.0 * token_count)
     piece_rows, piece_cols = deep // 2, width // n_fsdp
     units, base = [], 0
     for by_owner, row_blocks, cols in (
@@ -1323,13 +1769,7 @@
     ):
         units.append(Unit(base, by_owner, row_blocks, cols // piece_cols))
         base += units[-1].count
-    gain_rows = jnp.concatenate(
-        [attention_gain_f[None], mlp_gain_f[None], jnp.zeros((6, width), jnp.float32)]
-    )
-    head_gains = jnp.concatenate(
-        [query_gain_f[None], key_gain_f[None], jnp.zeros((6, HD), jnp.float32)]
-    )
-    pieces, _, _, _, _, tokens_grad, gain_parts, head_gain_parts = backward(
+    pieces, _, _, _, _, tokens_grad, gain_sums = backward(
         n_fsdp,
         n_rep,
         heads_k,
@@ -1360,9 +1800,6 @@
             pair_len,
         ),
     )
-    dgains = sum_everywhere(
-        jnp.concatenate([gain_parts[:2].reshape(1, -1), head_gain_parts[:2].reshape(1, -1)], axis=1)
-    )[0]
     down, mlp, outp, attn = units
 
     def by_rows(unit, weight):
@@ -1398,22 +1835,22 @@
         (w_query.shape, w_outgate.shape, w_key.shape, w_value.shape),
     )
 
-    def own_part(start, cols):
-        return lax.dynamic_slice(dgains, (start + mine * cols,), (cols,))
+    def own_part(row, start, cols):
+        return lax.dynamic_slice(gain_sums, (row, start + mine * cols), (1, cols))[0]
 
     return (
         block_out,
         seq_loss,
         tokens_grad,
-        own_part(0, deep),
-        own_part(2 * width, small),
-        own_part(2 * width + HD, small),
+        own_part(0, 0, deep),
+        own_part(0, width, small),
+        own_part(1, width, small),
         dw_query,
         dw_key,
         dw_value,
         dw_outgate,
         dw_output,
-        own_part(width, deep),
+        own_part(1, 0, deep),
         dw_gate,
         dw_up,
         dw_down,

time: 795 us -> 706 us (0.89)
  Pallas kernels: 512 us -> 685 us
  waiting for transfers between devices: 97.4 us -> 0 us
  matrix products: 62.9 us -> 0 us
  local copies, waits for them, and re-layouts: 43.5 us -> 8.45 us
  starting transfers between devices: 29.3 us -> 0 us
  other arithmetic: 25 us -> 8.45 us
  between operations: 15.5 us -> 1.41 us
    pallas_call x2 -> x1, Pallas kernels: 97.9 us -> 266 us  [forward(): pl.pallas_call(functools.partial(forward_kernel, n_fsdp, n_rep, heads_k),...]
    ppermute x29 -> x0, waiting for transfers between devices: 97.4 us -> none  [the longest x24 86.9 us: shift(): return lax.ppermute(values, 'fsdp', [(i, i ^ step) for i in range(n_fsdp)])]
    dot_general x8 -> x0, matrix products: 62.9 us -> none  [the longest x7 48 us: times(): jnp.dot(left_side, right_side, preferred_element_type=jnp.float32)]
    ppermute x29 -> x0, starting transfers between devices: 29.3 us -> none  [the longest x24 24.9 us: shift(): return lax.ppermute(values, 'fsdp', [(i, i ^ step) for i in range(n_fsdp)])]
    unnamed x68 -> x13, local copies, waits for them, and re-layouts: 11.9 us -> 2.04 us
    dynamic_update_slice x5 -> x2, local copies, waits for them, and re-layouts: 10.9 us -> 1.55 us  [spread(): lax.dynamic_update_slice(jnp.zeros((1, HD), jnp.bfloat16), gain[None], (0...]
    slice x7 -> x0, local copies, waits for them, and re-layouts: 8.42 us -> none  [the longest x1 4.21 us: shards(): rows_of = mlp_parts[:, s - 1].reshape(deep, 2 * ff)]
  transfers between devices with their start and end apart: 30 -> 0, of which waited for: 19 -> 0; matrix products, arithmetic and copies ran while one was open for 6% -> 0% of each run, Pallas kernels for 6% -> 0%
where the time goes in v5:
time: 706 us; the launch traced here: 703 us
  Pallas kernels  685 us (97%)
  other arithmetic  8.45 us (1%)
  local copies, waits for them, and re-layouts  8.45 us (1%)
    pallas_call x1, Pallas kernels, backward(): pl.pallas_call(functools.partial(backward_kernel, n_fsdp, n_rep, heads_k,...  382 us
    pallas_call x1, Pallas kernels, forward(): pl.pallas_call(functools.partial(forward_kernel, n_fsdp, n_rep, heads_k),...  266 us
    pallas_call x4, Pallas kernels, widened(): pl.pallas_call(widen_kernel, grid=grid, out_shape=jax.ShapeDtypeStruct(sh...  29.2 us

profile of v5, /device:TPU:0, one launch (start us, length us, event | category | flops | bytes accessed | tf_op | source)
XLA Modules:
  0.0 703.4 jit_solution(5652754200087085853)
XLA Ops:
  0.7 1.3 reduce_sum.29
  2.7 0.8 dynamic_update_slice.6
  3.4 0.8 dynamic_update_slice.7
  4.3 0.1 add.64
  4.4 0.8 select_reduce_fusion.1
  5.2 0.8 select_reduce_fusion
  6.1 0.1 reshape.165.refs_13_.refs_20_
  6.2 0.2 add_reduce_fusion
  6.3 1.9 concatenate.11.refs_1_
  8.3 1.9 multiply_sine_fusion
  10.2 1.0 pad_maximum_fusion.1.refs_12_.refs_14_
  11.2 1.0 pad_maximum_fusion.refs_11_.refs_13_
  12.2 265.6 %forward.1 = (bf16[1024,2048]{1,0:T(8,128)(2,1)}, f32[1024,1536]{1,0:T(8,128)}, bf16[1024,512]{1,0:T(8,128)(2,1)}, bf16[1024,256]{1,0:T(8,128)(2,1)}, bf16[1024,...) custom-call(bf16[256,2048]{1,0:T(8,128)(2,1)} %refs_11_.1, ...), custom_call_target="tpu_custom_call" | custom-call | tf_op jit(solution)/shard_map/forward/pallas_call | solution.py:1641
  277.8 1.3 fusion.2
  279.1 381.5 %backward.1 = (bf16[52,2,256,512]{3,2,1,0:T(8,128)(2,1)}, bf16[1024,2048]{1,0:T(8,128)(2,1)}, bf16[1024,1536]{1,0:T(8,128)(2,1)}, bf16[52,256,512]{2,1,0:T(8,128...) custom-call(bf16[1024,1536]{1,0:T(8,128)(2,1)} %get-tuple-element.42.refs_0_, ...), custom_call_target="tpu_custom_call" | custom-call | flops 55834574848 | bytes 1073741824 | tf_op jit(solution)/shard_map/backward/pallas_call | solution.py:752
  660.6 1.4 dynamic-slice_bitcast_fusion
  662.0 1.4 constant_dynamic-slice_fusion
  663.4 3.4 widen.4
  666.8 8.2 %widen.7 = f32[1536,2048]{1,0:T(8,128)} custom-call(bf16[52,2,256,512]{3,2,1,0:T(8,128)(2,1)} %get-tuple-element.60.query_in.gate_in.pair_in.in_ref), custom_call_target="tpu_custom_call" | custom-call | tf_op jit(solution)/shard_map/widen/pallas_call | solution.py:799
  675.0 8.8 %widen.6 = f32[512,6144]{1,0:T(8,128)} custom-call(bf16[52,2,256,512]{3,2,1,0:T(8,128)(2,1)} %get-tuple-element.60.query_in.gate_in.pair_in.in_ref), custom_call_target="tpu_custom_call" | custom-call | tf_op jit(solution)/shard_map/widen/pallas_call | solution.py:799
  683.8 8.8 %widen.5 = f32[512,6144]{1,0:T(8,128)} custom-call(bf16[52,2,256,512]{3,2,1,0:T(8,128)(2,1)} %get-tuple-element.60.query_in.gate_in.pair_in.in_ref), custom_call_target="tpu_custom_call" | custom-call | tf_op jit(solution)/shard_map/widen/pallas_call | solution.py:799
  692.7 8.8 %widen_heads.1 = (f32[512,2048]{1,0:T(8,128)}, f32[512,2048]{1,0:T(8,128)}, f32[512,1024]{1,0:T(8,128)}, f32[512,1024]{1,0:T(8,128)}) custom-call(bf16[52,2,256,512]{3,2,1,0:T(8,128)(2,1)} %get-tuple-element.60.query_in.gate_in.pair_in.in_ref, bf16[52,2,256,512]{3,2,1,0:T(8,128)(2,1)} %get-tuple-element.60.query_in.gate_in.pair_in.in_ref, ...), custom_call_target="tpu_custom_call" | custom-call | tf_op jit(solution)/shard_map/widen_heads/pallas_call | solution.py:824
  701.5 1.0 copy.38
  702.4 1.0 copy.39
  (18 shorter events, 0.2 us)
Async XLA Ops:
  6.2 6.1 copy-start.2
  692.6 8.8 %copy-start = (bf16[256,2048]{1,0:T(8,128)(2,1)S(1)}, bf16[256,2048]{1,0:T(8,128)(2,1)}, u32[]{:S(2)}) copy-start(bf16[256,2048]{1,0:T(8,128)(2,1)} %get-tuple-element.90) | copy-start | bytes 3145732
  692.7 9.8 %copy-start.1 = (bf16[256,2048]{1,0:T(8,128)(2,1)S(1)}, bf16[256,2048]{1,0:T(8,128)(2,1)}, u32[]{:S(2)}) copy-start(bf16[256,2048]{1,0:T(8,128)(2,1)} %get-tuple-element.92) | copy-start | bytes 3145732

commit v6 on v5

--- a/solution.py
+++ b/solution.py
@@ -2,6 +2,7 @@
 
 import jax
 import jax.numpy as jnp
+import numpy as np
 from jax import lax
 from jax.experimental import pallas as pl
 from jax.experimental.pallas import tpu as pltpu
@@ -17,22 +18,6 @@
 EPS_NORM = 1e-06
 ROPE_BASE = 1000000.0
 NEG_FILL = -1e30
-
-
-def row_layout(pair_len, row_count, head_dim):
-    row_index = jnp.arange(row_count, dtype=jnp.int32)[None, :]
-    head_len = pair_len[:, :1]
-    both_len = pair_len[:, :1] + pair_len[:, 1:]
-    segment = (row_index >= head_len).astype(jnp.int32) + (row_index >= both_len).astype(jnp.int32)
-    start_row = jnp.where(segment == 0, 0, jnp.where(segment == 1, head_len, both_len))
-    position = (row_index - start_row).astype(jnp.float32)
-    inv_freq = jnp.power(ROPE_BASE, -jnp.arange(0, head_dim, 2, dtype=jnp.float32) / head_dim)
-    angles = position[..., None] * inv_freq
-    angle_cos, angle_sin = jnp.cos(angles), jnp.sin(angles)
-    return (
-        jnp.concatenate([angle_cos, angle_cos], axis=-1),
-        jnp.concatenate([angle_sin, angle_sin], axis=-1),
-    )
 
 
 def in_f32(values):
@@ -64,7 +49,7 @@
         self.count = row_blocks * col_blocks
 
 
-LAG_B, LAG_C, LAG_D, LAG_E, LAG_G = 2, 4, 6, 8, 11
+LAG_B, LAG_C, LAG_D, LAG_E, LAG_G = 2, 4, 6, 8, 14
 RING = 4
 
 
@@ -82,13 +67,13 @@
 def backward_kernel(n_fsdp, n_rep, heads_k, units, piece_rows, piece_cols, *refs):
     (hidden, normed_mlp, gated, normed, grad_branch, grad_mlp, w_mlp, w_output, w_attn) = refs[:9]
     (middle, grad_result, tokens, attn_raw, all_cos, all_sin, all_q, all_k, all_v) = refs[9:18]
-    (gains, head_gains, pair_ref) = refs[18:21]
-    (out, grad_attn, grad_raw, inb, xb, tokens_grad, gain_out) = refs[21:28]
-    (lm, lo, rh, sb, kb, r1, c_slot, d_slot, big, wt, own, pbuf, land_a, land_b) = refs[28:42]
-    (mid, gres, tok, ga, wo, raw, cs, sn, qb, kvb, vb, gb, gg, ob) = refs[42:56]
-    (tile_sem, r1s, r1r, ins, inr, xs, xr, os_, fs, fr, gs, gr, ls) = refs[56:69]
-    (load_sem, first_sem, wt_sem, ps, pr, qs, qr, ag_s, ag_r, ag_l, block_sem) = refs[69:80]
-    (near_land, pair_land, in_land, far_land, near_s, near_r, line_s, line_r) = refs[80:]
+    (gains, head_gains, lengths_ref, deal_ref) = refs[18:22]
+    (out, grad_attn, grad_raw, inb, xb, tokens_grad, gain_out) = refs[22:29]
+    (lm, lo, rh, sb, kb, r1, c_slot, d_slot, big, wt, own, pbuf, land_a, land_b) = refs[29:43]
+    (mid, gres, tok, ga, wo, raw, cs, sn, qb, kvb, vb, gb, gg, ob) = refs[43:57]
+    (tile_sem, r1s, r1r, ins, inr, xs, xr, os_, fs, fr, gs, gr, ls) = refs[57:70]
+    (load_sem, first_sem, wt_sem, ps, pr, qs, qr, ag_s, ag_r, ag_l, block_sem) = refs[70:81]
+    (near_land, pair_land, in_land, far_land, near_s, near_r, line_s, line_r) = refs[81:]
     head_gain_out = gain_out.at[:, pl.ds(own.shape[1], HD)]
     lefts = (hidden, normed_mlp, gated, normed)
     rights = (grad_branch, grad_mlp, grad_attn, grad_raw)
@@ -141,7 +126,7 @@
         return remote_copy(r1.at[p], xb.at[p], xs.at[p], xr.at[p], inward, mine)
 
     def o_copy(p, src):
-        return remote_copy(src.at[p], xb.at[p], os_.at[p], xr.at[p], outward, mine)
+        return remote_copy(src.at[p], xb.at[p], os_, xr.at[p], outward, mine)
 
     def inside_of(p, unit):
         inside = at_least(p, unit.base, total - unit.base)
@@ -171,17 +156,17 @@
         return remote_copy(
             r1.at[p],
             out.at[spot(p, mine), core],
-            fs.at[p],
+            fs,
             fr.at[p],
             rep,
             flipped(mine, step, n_fsdp),
         )
 
-    def g_copy(p, src, where):
-        return remote_copy(src, out.at[where, core], gs.at[p], gr.at[p], sib, mine)
+    def g_copy(src, where):
+        return remote_copy(src, out.at[where, core], gs, gr, sib, mine)
 
     def l_copy(p):
-        return pltpu.make_async_copy(r1.at[p], out.at[spot(p, mine), core], ls.at[p])
+        return pltpu.make_async_copy(r1.at[p], out.at[spot(p, mine), core], ls)
 
     def c_load(p):
         return pltpu.make_async_copy(inb.at[p], c_slot, load_sem.at[0])
@@ -265,7 +250,7 @@
         @pl.when(step == 0)
         def _():
             l_copy(p).start()
-            g_copy(p, r1.at[p], spot(p, mine)).start()
+            g_copy(r1.at[p], spot(p, mine)).start()
 
         @pl.when(step > 0)
         def _():
@@ -278,7 +263,7 @@
         def _():
             f_copy(p, step).wait_recv()
             where = spot(p, flipped(mine, step, n_fsdp))
-            g_copy(p, out.at[where, core], where).start()
+            g_copy(out.at[where, core], where).start()
 
     def run(stages, t):
         for lag, stage in stages:
@@ -431,7 +416,9 @@
         attend_back(
             heads_k,
             heads,
-            block_mask(pair_ref, rows, s),
+            block_mask(
+                block_lengths(lengths_ref, deal_ref, rep * n_fsdp + flipped(mine, s, n_fsdp)), rows
+            ),
             cs[...],
             sn[...],
             head_gains[0:1],
@@ -597,6 +584,18 @@
 
     def tasks(u, i):
         if u == 0:
+
+            @pl.when(i == 1)
+            def _():
+                wt_load(0).start()
+                for copy in first_loads((0, 1)):
+                    copy.start()
+
+            @pl.when(i == 6)
+            def _():
+                for copy in first_loads((2, 3, 4, 5)):
+                    copy.start()
+
             pl.when((i >= 4) & (i < 4 + TILES))(lambda: mlp_products(i - 4))
         if u == 1:
             for part in range(2):
@@ -617,9 +616,6 @@
     def product(left, right):
         return product_of(left, right, 0, 0)
 
-    for copy in first_loads(range(6)):
-        copy.start()
-    wt_load(0).start()
     for copy in tiles(0, 0, 0):
         copy.start()
     for u, unit in enumerate(units):
@@ -663,29 +659,19 @@
 
     lax.fori_loop(total, total + LAG_G, drain, 0)
 
-    def finish(p, carry):
-        @pl.when(p >= total - RING)
-        def _():
-            r1_copy(p).wait_send()
-
-        @pl.when(depth > 0)
-        def _():
-            o_copy(p, r1).wait_send()
-
-        step = owner_of(p)
-
-        @pl.when(step == 0)
-        def _():
-            l_copy(p).wait()
-
-        @pl.when(step > 0)
-        def _():
-            f_copy(p, step).wait_send()
-
-        g_copy(p, r1.at[p], p).wait()
-        return carry
-
-    lax.fori_loop(0, total, finish, 0)
+    for p in range(total - RING, total):
+        r1_copy(p).wait_send()
+    kept = sum(u.col_blocks if u.by_owner else u.count for u in units)
+    some, rest = pl.ds(0, kept), pl.ds(0, total - kept)
+    every = remote_copy(r1, out.at[:, core], gs, gr, sib, mine)
+    every.wait()
+    pltpu.make_async_copy(r1.at[some], out.at[some, core], ls).wait()
+    remote_copy(r1.at[rest], out.at[rest, core], fs, fr.at[0], sib, mine).wait_send()
+
+    @pl.when(depth > 0)
+    def _():
+        remote_copy(r1, xb, os_, xr.at[0], outward, mine).wait_send()
+
     for k in range(1, half):
         gains_in(k)
     gains_across()
@@ -754,11 +740,12 @@
             backward_kernel, n_fsdp, n_rep, heads_k, units, piece_rows, piece_cols
         ),
         out_shape=[jax.ShapeDtypeStruct(shape, kind) for shape, kind in outs],
-        in_specs=[any_spec] * 18 + [vmem] * 2 + [pl.BlockSpec(memory_space=pltpu.SMEM)],
+        in_specs=[any_spec] * 18 + [vmem] * 2 + [pl.BlockSpec(memory_space=pltpu.SMEM)] * 2,
         out_specs=[any_spec] * 5 + [vmem] * 2,
         scratch_shapes=[pltpu.VMEM(shape, kind) for shape, kind in scratch]
         + [dma((2, 3))]
-        + [dma((total,)) for _ in range(12)]
+        + [dma((total,)) for _ in range(6)]
+        + [dma, dma, dma((total,)), dma, dma, dma]
         + [
             dma((3,)),
             dma((7,)),
@@ -806,6 +793,28 @@
     )(pieces)
 
 
+def widen_both_kernel(in_ref, first_ref, second_ref):
+    cols, count = in_ref.shape[-1], in_ref.shape[0] // 2
+    for i in range(count):
+        first_ref[:, i * cols : (i + 1) * cols] = in_f32(in_ref[i, 0])
+        second_ref[:, i * cols : (i + 1) * cols] = in_f32(in_ref[count + i, 0])
+
+
+def widened_both(pieces, base, together, n_fsdp, shape):
+    rows, cols = pieces.shape[2:]
+    return pl.pallas_call(
+        widen_both_kernel,
+        grid=(2, n_fsdp),
+        out_shape=[jax.ShapeDtypeStruct(shape, jnp.float32)] * 2,
+        in_specs=[
+            pl.BlockSpec((together, 1, rows, cols), lambda c, f: (base // together + f, c, 0, 0))
+        ],
+        out_specs=[pl.BlockSpec((rows, together // 2 * cols), lambda c, f: (c, f))] * 2,
+        compiler_params=pltpu.CompilerParams(vmem_limit_bytes=32 << 20),
+        name="widen_both",
+    )(pieces)
+
+
 def widen_heads_kernel(query_in, gate_in, pair_in, query_out, gate_out, key_out, value_out):
     half = key_out.shape[1]
     query_out[...] = query_in[0, 0].astype(jnp.float32)
@@ -831,9 +840,13 @@
     )(pieces, pieces, pieces)
 
 
-def block_mask(pair_ref, rows, block):
-    head_len = pair_ref[block, 0]
-    both_len = head_len + pair_ref[block, 1]
+def block_lengths(lengths_ref, deal_ref, device):
+    head_len = lengths_ref[deal_ref[2 * device]]
+    return head_len, head_len + lengths_ref[deal_ref[2 * device + 1]]
+
+
+def block_mask(block, rows):
+    head_len, both_len = block
     query_row = lax.broadcasted_iota(jnp.int32, (rows, rows), 0)
     key_row = lax.broadcasted_iota(jnp.int32, (rows, rows), 1)
 
@@ -1052,15 +1065,16 @@
 
 def forward_kernel(n_fsdp, n_rep, heads_k, *refs):
     (tokens, gains, wq, wg, wk, wv, w_gate, w_up, w_output, w_down, teacher) = refs[:11]
-    (all_cos, all_sin, pair_ref, factor_ref) = refs[11:15]
+    (lengths_ref, deal_ref, lengths_row, freq_ref) = refs[11:15]
     (normed_all, raw_all, q_all, k_all, v_all, gated_all, w_attn, w_mlp) = refs[15:23]
     (middle_out, nmlp_all, hidden_all, gbranch_all, gmlp_all, gres_out, block_out) = refs[23:30]
-    (gu_all, gain_out, head_gain_out, loss_out) = refs[30:34]
-    (tok, gl, wa, wo, wd, wm, nb, raw, cs, sn, qb, kvb, vb, gb, own, pbuf, land) = refs[34:51]
-    (mid, nm, te, gu, hb, gm) = refs[51:57]
-    (ts, tr, tl, us, ur, ul, bs, br, bl, gain_s, gain_r, ws, wr, zs, zr, cps, cpr) = refs[57:74]
-    (ms, mr, hs, hr, ss, sr, ps, pr, qs, qr, load, keep, mine_sem) = refs[74:]
+    (gu_all, all_cos, all_sin, gain_out, head_gain_out, loss_out) = refs[30:36]
+    (tok, gl, wa, wo, wd, wm, nb, raw, cs, sn, qb, kvb, vb, gb, own, pbuf, land) = refs[36:53]
+    (mid, nm, te, gu, hb, gm) = refs[53:59]
+    (ts, tr, tl, us, ur, ul, bs, br, bl, gain_s, gain_r, ws, wr, zs, zr, cps, cpr) = refs[59:76]
+    (ms, mr, hs, hr, ss, sr, ps, pr, qs, qr, load, keep, mine_sem) = refs[76:]
     rows, width = own.shape
+    rows_all = n_fsdp * rows
     cols, ff = raw.shape[1], hb.shape[1]
     deep = wq.shape[0]
     widths = tuple(w.shape[1] // n_fsdp for w in (wq, wg, wk, wv))
@@ -1216,7 +1230,6 @@
         gain_copy(s).start()
         for i in range(4):
             weight_copy(s, i).start()
-    token_rows.start()
     for copy in local(range(10)):
         copy.start()
     for s in others:
@@ -1227,7 +1240,30 @@
     for s in others:
         for i in range(2):
             mlp_copy(s, i).start()
-    token_rows.forward()
+
+    def block_rows(s):
+        return pl.ds(pl.multiple_of(s * rows, rows), rows)
+
+    def lengths_of(s):
+        return block_lengths(lengths_ref, deal_ref, rep * n_fsdp + flipped(mine, s, n_fsdp))
+
+    def angles(s, carry):
+        head_len, both_len = lengths_of(s)
+        index = lax.broadcasted_iota(jnp.int32, (rows, HD), 0)
+        start = jnp.where(index < head_len, 0, jnp.where(index < both_len, head_len, both_len))
+        angle = (index - start).astype(jnp.float32) * freq_ref[...]
+        cs[block_rows(s)] = jnp.cos(angle)
+        sn[block_rows(s)] = jnp.sin(angle)
+        return carry
+
+    lax.fori_loop(0, n_fsdp, angles, 0)
+    angle_stores = [
+        pltpu.make_async_copy(cs, all_cos, load.at[2]),
+        pltpu.make_async_copy(sn, all_sin, load.at[3]),
+    ]
+    for copy in angle_stores:
+        copy.start()
+    token_count = jnp.sum(in_f32(lengths_row[...]), axis=1, keepdims=True)
     local((6,))[0].wait()
     gain_out[...] = jnp.zeros_like(gain_out)
     head_gain_out[...] = jnp.zeros_like(head_gain_out)
@@ -1244,24 +1280,22 @@
                 ]
             head_gain_out[kind : kind + 1] += piece[2 * lines + kind : 2 * lines + kind + 1]
     for s in others:
+        for i in range(2):
+            mlp_copy(s, i).wait_recv()
+        share_copy(s, 0, True).start()
+    token_rows.start()
+    for s in others:
         partner_copy(s).wait_recv()
         sibling_copy(s, 1).start()
+    line_sends(1)
     for s in others:
         for k in range(2):
             sibling_copy(s, k).wait_recv()
     for copy in local((0, 1, 2, 3)):
         copy.wait()
     attn_load().start()
-    for s in others:
-        for i in range(2):
-            mlp_copy(s, i).wait_recv()
-        share_copy(s, 0, True).start()
-    line_sends(1)
     for copy in local((7, 8, 9)):
         copy.wait()
-
-    def block_rows(s):
-        return pl.ds(pl.multiple_of(s * rows, rows), rows)
 
     def some_rows(base, r):
         return pl.ds(pl.multiple_of(base + r * ROW_STEP, ROW_STEP), ROW_STEP)
@@ -1327,17 +1361,8 @@
             for i, (src, dst) in enumerate(pairs)
         ]
 
-    def angle_loads(s):
-        cut = block_rows(s)
-        return [
-            pltpu.make_async_copy(all_cos.at[cut], cs, load.at[2]),
-            pltpu.make_async_copy(all_sin.at[cut], sn, load.at[3]),
-        ]
-
-    def attention(i, carry):
-        s = (i + 1) % n_fsdp
-        for copy in angle_loads(s):
-            copy.start()
+    def attention(s, carry):
+        pl.when(s == 1)(token_rows.forward)
         for k in range(n_fsdp):
 
             @pl.when(s == k)
@@ -1347,7 +1372,7 @@
                 else:
                     token_rows.arrive(k)
 
-        @pl.when(i > 0)
+        @pl.when(s > 0)
         def _():
             for copy in attention_stores(s):
                 copy.wait()
@@ -1358,7 +1383,7 @@
 
         by_rows(normed_rows)
 
-        @pl.when(i == 0)
+        @pl.when(s == 0)
         def _():
             attn_load().wait()
 
@@ -1366,13 +1391,11 @@
             raw[:, cut] = product_of(nb[...], wa[:, cut], 1, 0)
 
         tiled(3, cols // 3, raw_tile)
-        for copy in angle_loads(s):
-            copy.wait()
         attend(
             heads_k,
-            block_mask(pair_ref, rows, s),
-            cs[...],
-            sn[...],
+            block_mask(lengths_of(s), rows),
+            cs[block_rows(s)],
+            sn[block_rows(s)],
             head_gain_out[0:1],
             head_gain_out[1:2],
             raw,
@@ -1389,10 +1412,14 @@
         def _():
             out_copy(s, ps, pr).start()
 
+        if n_line > 2:
+            pl.when(s == n_fsdp - 2)(lambda: line_arrivals(1))
         return carry
 
     lax.fori_loop(0, n_fsdp, attention, 0)
-    for k in range(1, n_line // 2):
+    for copy in angle_stores:
+        copy.wait()
+    for k in range(2, n_line - 1):
         line_arrivals(k)
     for s in others:
         out_copy(s, ps, pr).wait()
@@ -1414,9 +1441,6 @@
         copy.wait()
 
 
-    for k in range(n_line // 2, n_line - 1):
-        line_arrivals(k)
-    up_rows.forward()
     line_arrivals(n_line - 1)
     shares(lambda copy: copy.wait_recv())
     for copy in local((4, 5)):
@@ -1453,6 +1477,7 @@
 
     def feed_forward(i, carry):
         s = (i + 1) % n_fsdp
+        pl.when(i == 0)(up_rows.forward)
         into_nb(up_rows, nmlp_all, s)
 
         @pl.when(i > 0)
@@ -1495,8 +1520,8 @@
     gu_load(0).start()
     for s in others:
         out_copy(s, qs, qr).wait()
-    head_len = pair_ref[0, 0]
-    both_len = head_len + pair_ref[0, 1]
+    head_len, both_len = lengths_of(0)
+    factor = (n_rep * rows_all) / token_count
     loss_out[...] = jnp.zeros_like(loss_out)
 
     def error_rows(r):
@@ -1510,11 +1535,12 @@
         loss_out[0:1] += jnp.sum(first, axis=0, keepdims=True)
         loss_out[1:2] += jnp.sum(square - first, axis=0, keepdims=True)
         te[cut] = in_bf16(result * valid)
-        grad = error * factor_ref[0, 0]
+        grad = error * factor
         mid[cut] = grad
         nm[cut] = in_bf16(grad)
 
     by_rows(error_rows)
+    loss_out[...] = loss_out[...] / (2.0 * token_count)
     back_rows.start()
     last_stores = [
         pltpu.make_async_copy(te, block_out, load.at[3]),
@@ -1527,10 +1553,7 @@
         return pltpu.make_async_copy(gm, gmlp_all.at[block_rows(s)], keep.at[2])
 
     def feed_back(s, carry):
-        @pl.when(s == 1)
-        def _():
-            back_rows.forward()
-
+        pl.when(s == 1)(back_rows.forward)
         into_nb(back_rows, gbranch_all, s)
 
         def hidden_tile(cut):
@@ -1607,6 +1630,8 @@
         ((rows, width), full),
         ((rows, width), low),
         ((rows_all, 2 * ff), full),
+        ((rows_all, HD), full),
+        ((rows_all, HD), full),
         ((8, width), full),
         ((8, HD), full),
         ((8, HD), full),
@@ -1620,8 +1645,8 @@
         ((width, 2 * ff), low),
         ((rows, width), low),
         ((rows, cols), full),
-        ((rows, HD), full),
-        ((rows, HD), full),
+        ((rows_all, HD), full),
+        ((rows_all, HD), full),
         ((rows, cols_q), low),
         ((rows, cols_k), low),
         ((rows, cols_k), low),
@@ -1641,8 +1666,8 @@
     return pl.pallas_call(
         functools.partial(forward_kernel, n_fsdp, n_rep, heads_k),
         out_shape=[jax.ShapeDtypeStruct(shape, kind) for shape, kind in outs],
-        in_specs=[any_spec] * 13 + [smem] * 2,
-        out_specs=[any_spec] * 16 + [vmem] * 3,
+        in_specs=[any_spec] * 11 + [smem] * 2 + [vmem] * 2,
+        out_specs=[any_spec] * 18 + [vmem] * 3,
         scratch_shapes=[pltpu.VMEM(shape, kind) for shape, kind in scratch]
         + [pair, pair, dma] * 3
         + [one, one, four, four, one, one, pair, pair]
@@ -1685,27 +1710,13 @@
     ff = w_down.shape[0]
     rows_all = rows * n_fsdp
 
-    peers = mine ^ jnp.arange(n_fsdp, dtype=jnp.int32)
-    devices = lax.axis_index("rep") * n_fsdp + peers
-    slot_ids = (devices[:, None] * 2 + jnp.arange(2, dtype=jnp.int32)[None, :]).reshape(-1)
-    seq_ids = jnp.arange(lengths.shape[0], dtype=jnp.int32)
-    slot_seq = jnp.sum(
-        jnp.where(seq_ids[None, :] == slot_ids[:, None], deal_order[None, :], 0), axis=1
-    )
-    pair_len = jnp.sum(
-        jnp.where(seq_ids[None, :] == slot_seq[:, None], lengths[None, :], 0), axis=1
-    ).reshape(n_fsdp, 2)
-    token_count = jnp.sum(lengths).astype(jnp.float32)
-    factor = rows * n_rep * n_fsdp / (2.0 * token_count)
-    angle_cos, angle_sin = row_layout(pair_len, rows, HD)
-    angle_cos, angle_sin = angle_cos.reshape(rows_all, HD), angle_sin.reshape(rows_all, HD)
-
+    freq = np.power(np.float32(ROPE_BASE), -np.arange(0, HD, 2, dtype=np.float32) / HD)
+    freq = jnp.asarray(np.concatenate([freq, freq])[None])
     small = query_gain.shape[0]
 
     def spread(gain):
-        return lax.dynamic_update_slice(
-            jnp.zeros((1, HD), jnp.bfloat16), gain[None], (0, mine * small)
-        )
+        lane = jnp.arange(HD, dtype=jnp.int32)
+        return jnp.where(lane // small == mine, jnp.tile(gain, n_fsdp), 0)[None]
 
     gain_block = jnp.concatenate(
         [
@@ -1733,6 +1744,8 @@
         grad_result,
         block_out,
         _,
+        angle_cos,
+        angle_sin,
         gain_rows,
         head_gains,
         losses,
@@ -1752,13 +1765,13 @@
             w_output,
             w_down,
             teacher,
-            angle_cos,
-            angle_sin,
-            pair_len,
-            (2.0 * factor).reshape(1, 1),
+            lengths,
+            deal_order,
+            lengths[None],
+            freq,
         ),
     )
-    seq_loss = losses[:2, 0] / (2.0 * token_count)
+    seq_loss = losses[:2, 0]
     piece_rows, piece_cols = deep // 2, width // n_fsdp
     units, base = [], 0
     for by_owner, row_blocks, cols in (
@@ -1797,7 +1810,8 @@
             values_b,
             gain_rows,
             head_gains,
-            pair_len,
+            lengths,
+            deal_order,
         ),
     )
     down, mlp, outp, attn = units
@@ -1813,21 +1827,9 @@
             lambda c, r: (c * blocks + r, 0),
         )
 
-    def by_owners(unit, weight, which):
-        together = unit.col_blocks // 2
-        return widened(
-            pieces,
-            (2, n_fsdp),
-            together,
-            lambda c, f: (unit.base // together + 2 * f + which, c, 0, 0),
-            weight.shape,
-            lambda c, f: (c, f),
-        )
-
     dw_down = by_rows(down, w_down)
     dw_output = by_rows(outp, w_output)
-    dw_gate = by_owners(mlp, w_gate, 0)
-    dw_up = by_owners(mlp, w_up, 1)
+    dw_gate, dw_up = widened_both(pieces, mlp.base, mlp.col_blocks, n_fsdp, w_gate.shape)
     dw_query, dw_outgate, dw_key, dw_value = widened_heads(
         pieces,
         attn.base,

time: 706 us -> 662 us (0.938)
  Pallas kernels: 685 us -> 650 us
  other arithmetic: 8.45 us -> 0.01 us
    pallas_call x1, Pallas kernels: 382 us -> 350 us  [backward(): pl.pallas_call(functools.partial(backward_kernel, n_fsdp, n_rep, heads_k,...]
    pallas_call x4 -> x2, Pallas kernels: 29.2 us -> 11.7 us  [widened(): pl.pallas_call(widen_kernel, grid=grid, out_shape=jax.ShapeDtypeStruct(sh...]
    pallas_call x0 -> x1, Pallas kernels: none -> 13.9 us  [widened_both(): pl.pallas_call(widen_both_kernel, grid=(2, n_fsdp), out_shape=[jax.ShapeD...]
where the time goes in v6:
time: 662 us; the launch traced here: 660 us
  Pallas kernels  650 us (98%)
  local copies, waits for them, and re-layouts  9.43 us (1%)
    pallas_call x1, Pallas kernels, backward(): pl.pallas_call(functools.partial(backward_kernel, n_fsdp, n_rep, heads_k,...  350 us
    pallas_call x1, Pallas kernels, forward(): pl.pallas_call(functools.partial(forward_kernel, n_fsdp, n_rep, heads_k),...  265 us
    pallas_call x1, Pallas kernels, widened_both(): pl.pallas_call(widen_both_kernel, grid=(2, n_fsdp), out_shape=[jax.ShapeD...  13.9 us

profile of v6, /device:TPU:0, one launch (start us, length us, event | category | flops | bytes accessed | tf_op | source)
XLA Modules:
  0.0 659.8 jit_solution(1227315599575794981)
XLA Ops:
  0.6 0.7 tile.20
  1.3 0.1 tile.21
  1.4 0.7 tile.8
  2.0 0.1 tile.9
  2.2 1.9 concatenate.3.refs_1_
  4.1 264.9 %forward.1 = (bf16[1024,2048]{1,0:T(8,128)(2,1)}, f32[1024,1536]{1,0:T(8,128)}, bf16[1024,512]{1,0:T(8,128)(2,1)}, bf16[1024,256]{1,0:T(8,128)(2,1)}, bf16[1024,...) custom-call(bf16[256,2048]{1,0:T(8,128)(2,1)} %refs_11_.3, ...), custom_call_target="tpu_custom_call" | custom-call | tf_op jit(solution)/shard_map/forward/pallas_call | solution.py:1666
  269.0 1.3 slice_reduce_fusion
  270.3 350.5 %backward.1 = (bf16[52,2,256,512]{3,2,1,0:T(8,128)(2,1)}, bf16[1024,2048]{1,0:T(8,128)(2,1)}, bf16[1024,1536]{1,0:T(8,128)(2,1)}, bf16[52,256,512]{2,1,0:T(8,128...) custom-call(bf16[1024,1536]{1,0:T(8,128)(2,1)} %get-tuple-element.46.refs_0_, ...), custom_call_target="tpu_custom_call" | custom-call | flops 55834574848 | bytes 1073741824 | tf_op jit(solution)/shard_map/backward/pallas_call | solution.py:738
  620.8 1.4 constant_dynamic-slice_fusion.1
  622.2 1.3 dynamic-slice_bitcast_fusion
  623.5 8.7 %widen_heads.1 = (f32[512,2048]{1,0:T(8,128)}, f32[512,2048]{1,0:T(8,128)}, f32[512,1024]{1,0:T(8,128)}, f32[512,1024]{1,0:T(8,128)}) custom-call(bf16[52,2,256,512]{3,2,1,0:T(8,128)(2,1)} %get-tuple-element.66.query_in.gate_in.pair_in.in_ref, bf16[52,2,256,512]{3,2,1,0:T(8,128)(2,1)} %get-tuple-element.66.query_in.gate_in.pair_in.in_ref, ...), custom_call_target="tpu_custom_call" | custom-call | tf_op jit(solution)/shard_map/widen_heads/pallas_call | solution.py:833
  632.2 3.4 widen.2
  635.6 13.9 %widen_both.1 = (f32[512,6144]{1,0:T(8,128)}, f32[512,6144]{1,0:T(8,128)}) custom-call(bf16[52,2,256,512]{3,2,1,0:T(8,128)(2,1)} %get-tuple-element.66.query_in.gate_in.pair_in.in_ref), custom_call_target="tpu_custom_call" | custom-call | tf_op jit(solution)/shard_map/widen_both/pallas_call | solution.py:805
  649.5 0.0 copy-start
  649.5 0.0 copy-start.1
  649.5 8.3 %widen.3 = f32[1536,2048]{1,0:T(8,128)} custom-call(bf16[52,2,256,512]{3,2,1,0:T(8,128)(2,1)} %get-tuple-element.66.query_in.gate_in.pair_in.in_ref), custom_call_target="tpu_custom_call" | custom-call | tf_op jit(solution)/shard_map/widen/pallas_call | solution.py:786
  657.8 0.0 copy-done
  657.8 1.0 copy.34
  658.8 0.0 copy-done.1
  658.8 1.0 copy.35
  (2 shorter events, 0.0 us)
Async XLA Ops:
  649.5 8.3 %copy-start = (bf16[256,2048]{1,0:T(8,128)(2,1)S(1)}, bf16[256,2048]{1,0:T(8,128)(2,1)}, u32[]{:S(2)}) copy-start(bf16[256,2048]{1,0:T(8,128)(2,1)} %get-tuple-element.94) | copy-start | bytes 3145732
  649.5 9.3 %copy-start.1 = (bf16[256,2048]{1,0:T(8,128)(2,1)S(1)}, bf16[256,2048]{1,0:T(8,128)(2,1)}, u32[]{:S(2)}) copy-start(bf16[256,2048]{1,0:T(8,128)(2,1)} %get-tuple-element.96) | copy-start | bytes 3145732

commit v7 on v6

--- a/solution.py
+++ b/solution.py
@@ -1330,19 +1330,52 @@
 
         tiled(4, tile, one)
 
-    def out_copy(s, sends, recvs):
+
+    relayed = n_fsdp == 4
+
+    def half_rows(h):
+        return pl.ds(h * (rows // 2), rows // 2)
+
+    def out_copy(s, h, sends, recvs):
+        to, at = s, s - 1
+        if relayed and s == 3:
+            to, at = h + 1, 2
         return remote_copy(
-            pbuf.at[s - 1],
-            land.at[s - 1],
-            sends.at[s],
-            recvs.at[s],
+            pbuf.at[s - 1, half_rows(h)],
+            land.at[at, half_rows(h)],
+            sends.at[s, h],
+            recvs.at[s, h],
             rep,
-            flipped(mine, s, n_fsdp),
+            flipped(mine, to, n_fsdp),
         )
+
+    def send_block(s, sends, recvs):
+        for k in others:
+
+            @pl.when(s == k)
+            def _(k=k):
+                for h in range(2):
+                    if not relayed or (k, h) not in ((1, 1), (2, 0)):
+                        out_copy(k, h, sends, recvs).start()
+
+    def relay(sends, recvs):
+        if relayed:
+            for h, near in ((0, 2), (1, 1)):
+                out_copy(3, h, sends, recvs).wait_recv()
+                cut = half_rows(h)
+                pbuf[near - 1, cut] = in_bf16(in_f32(pbuf[near - 1, cut]) + in_f32(land[2, cut]))
+                out_copy(near, h, sends, recvs).start()
+
+    def arrived(sends, recvs):
+        for s in others:
+            for h in range(2):
+                if not (relayed and s == 3):
+                    out_copy(s, h, sends, recvs).wait_recv()
+                out_copy(s, h, sends, recvs).wait_send()
 
     def summed(cut):
         total = own[cut]
-        for s in others:
+        for s in range(1, 3 if relayed else n_fsdp):
             total += in_f32(land[s - 1, cut])
         return total
 
@@ -1408,10 +1441,7 @@
             copy.start()
         leave(s, gb, wo)
 
-        @pl.when(s > 0)
-        def _():
-            out_copy(s, ps, pr).start()
-
+        send_block(s, ps, pr)
         if n_line > 2:
             pl.when(s == n_fsdp - 2)(lambda: line_arrivals(1))
         return carry
@@ -1419,10 +1449,10 @@
     lax.fori_loop(0, n_fsdp, attention, 0)
     for copy in angle_stores:
         copy.wait()
+    relay(ps, pr)
     for k in range(2, n_line - 1):
         line_arrivals(k)
-    for s in others:
-        out_copy(s, ps, pr).wait()
+    arrived(ps, pr)
 
     def middle_rows(r):
         cut = some_rows(0, r)
@@ -1500,13 +1530,11 @@
             copy.start()
         leave(s, hb, wd)
 
-        @pl.when(s > 0)
-        def _():
-            out_copy(s, qs, qr).start()
-
+        send_block(s, qs, qr)
         return carry
 
     lax.fori_loop(0, n_fsdp, feed_forward, 0)
+    relay(qs, qr)
     up_rows.sent()
     up_rows.own().wait()
     middle_store().wait()
@@ -1518,8 +1546,7 @@
         return pltpu.make_async_copy(gu_all.at[block_rows(s)], gu, load.at[5])
 
     gu_load(0).start()
-    for s in others:
-        out_copy(s, qs, qr).wait()
+    arrived(qs, qr)
     head_len, both_len = lengths_of(0)
     factor = (n_rep * rows_all) / token_count
     loss_out[...] = jnp.zeros_like(loss_out)
@@ -1671,7 +1698,7 @@
         scratch_shapes=[pltpu.VMEM(shape, kind) for shape, kind in scratch]
         + [pair, pair, dma] * 3
         + [one, one, four, four, one, one, pair, pair]
-        + [pair, pair, line, line, line, line, one, one, one, one]
+        + [pair, pair, line, line, line, line, pair, pair, pair, pair]
         + [dma((6,)), dma((6,)), dma((10,))],
         compiler_params=pltpu.CompilerParams(
             collective_id=1, has_side_effects=True, vmem_limit_bytes=62 << 20

time: 662 us -> 650 us (0.982)
  Pallas kernels: 650 us -> 638 us
    pallas_call x1, Pallas kernels: 265 us -> 254 us  [forward(): pl.pallas_call(functools.partial(forward_kernel, n_fsdp, n_rep, heads_k),...]
where the time goes in v7:
time: 650 us; the launch traced here: 648 us
  Pallas kernels  638 us (98%)
  local copies, waits for them, and re-layouts  9.43 us (1%)
    pallas_call x1, Pallas kernels, backward(): pl.pallas_call(functools.partial(backward_kernel, n_fsdp, n_rep, heads_k,...  349 us
    pallas_call x1, Pallas kernels, forward(): pl.pallas_call(functools.partial(forward_kernel, n_fsdp, n_rep, heads_k),...  254 us
    pallas_call x1, Pallas kernels, widened_both(): pl.pallas_call(widen_both_kernel, grid=(2, n_fsdp), out_shape=[jax.ShapeD...  13.9 us

profile of v7, /device:TPU:0, one launch (start us, length us, event | category | flops | bytes accessed | tf_op | source)
XLA Modules:
  0.0 648.0 jit_solution(2435397186313070447)
XLA Ops:
  0.6 0.7 tile.20
  1.3 0.1 tile.21
  1.4 0.7 tile.8
  2.0 0.1 tile.9
  2.2 1.9 concatenate.3.refs_1_
  4.1 254.2 %forward.1 = (bf16[1024,2048]{1,0:T(8,128)(2,1)}, f32[1024,1536]{1,0:T(8,128)}, bf16[1024,512]{1,0:T(8,128)(2,1)}, bf16[1024,256]{1,0:T(8,128)(2,1)}, bf16[1024,...) custom-call(bf16[256,2048]{1,0:T(8,128)(2,1)} %refs_11_.3, ...), custom_call_target="tpu_custom_call" | custom-call | tf_op jit(solution)/shard_map/forward/pallas_call | solution.py:1693
  258.2 1.3 slice_reduce_fusion
  259.5 349.5 %backward.1 = (bf16[52,2,256,512]{3,2,1,0:T(8,128)(2,1)}, bf16[1024,2048]{1,0:T(8,128)(2,1)}, bf16[1024,1536]{1,0:T(8,128)(2,1)}, bf16[52,256,512]{2,1,0:T(8,128...) custom-call(bf16[1024,1536]{1,0:T(8,128)(2,1)} %get-tuple-element.46.refs_0_, ...), custom_call_target="tpu_custom_call" | custom-call | flops 55834574848 | bytes 1073741824 | tf_op jit(solution)/shard_map/backward/pallas_call | solution.py:738
  609.0 1.4 constant_dynamic-slice_fusion.1
  610.5 1.3 dynamic-slice_bitcast_fusion
  611.8 8.7 %widen_heads.1 = (f32[512,2048]{1,0:T(8,128)}, f32[512,2048]{1,0:T(8,128)}, f32[512,1024]{1,0:T(8,128)}, f32[512,1024]{1,0:T(8,128)}) custom-call(bf16[52,2,256,512]{3,2,1,0:T(8,128)(2,1)} %get-tuple-element.66.query_in.gate_in.pair_in.in_ref, bf16[52,2,256,512]{3,2,1,0:T(8,128)(2,1)} %get-tuple-element.66.query_in.gate_in.pair_in.in_ref, ...), custom_call_target="tpu_custom_call" | custom-call | tf_op jit(solution)/shard_map/widen_heads/pallas_call | solution.py:833
  620.5 3.4 widen.2
  623.8 13.9 %widen_both.1 = (f32[512,6144]{1,0:T(8,128)}, f32[512,6144]{1,0:T(8,128)}) custom-call(bf16[52,2,256,512]{3,2,1,0:T(8,128)(2,1)} %get-tuple-element.66.query_in.gate_in.pair_in.in_ref), custom_call_target="tpu_custom_call" | custom-call | tf_op jit(solution)/shard_map/widen_both/pallas_call | solution.py:805
  637.7 0.0 copy-start
  637.7 0.0 copy-start.1
  637.7 8.3 %widen.3 = f32[1536,2048]{1,0:T(8,128)} custom-call(bf16[52,2,256,512]{3,2,1,0:T(8,128)(2,1)} %get-tuple-element.66.query_in.gate_in.pair_in.in_ref), custom_call_target="tpu_custom_call" | custom-call | tf_op jit(solution)/shard_map/widen/pallas_call | solution.py:786
  646.1 0.0 copy-done
  646.1 1.0 copy.34
  647.1 0.0 copy-done.1
  647.1 1.0 copy.35
  (2 shorter events, 0.0 us)
Async XLA Ops:
  637.7 8.3 %copy-start = (bf16[256,2048]{1,0:T(8,128)(2,1)S(1)}, bf16[256,2048]{1,0:T(8,128)(2,1)}, u32[]{:S(2)}) copy-start(bf16[256,2048]{1,0:T(8,128)(2,1)} %get-tuple-element.94) | copy-start | bytes 3145732
  637.7 9.3 %copy-start.1 = (bf16[256,2048]{1,0:T(8,128)(2,1)S(1)}, bf16[256,2048]{1,0:T(8,128)(2,1)}, u32[]{:S(2)}) copy-start(bf16[256,2048]{1,0:T(8,128)(2,1)} %get-tuple-element.96) | copy-start | bytes 3145732

commit v8 on v7

--- a/solution.py
+++ b/solution.py
@@ -49,7 +49,7 @@
         self.count = row_blocks * col_blocks
 
 
-LAG_B, LAG_C, LAG_D, LAG_E, LAG_G = 2, 4, 6, 8, 14
+LAG_B, LAG_C, LAG_D, LAG_E, LAG_G = 1, 3, 5, 7, 13
 RING = 4
 
 
@@ -106,15 +106,6 @@
     for s in others:
         greet(rep, flipped(mine, s, n_fsdp))
 
-    @pl.when(depth == 0)
-    def _():
-        pl.semaphore_wait(barrier, 1 + n_fsdp)
-
-    @pl.when(depth > 0)
-    def _():
-        greet(outward, mine)
-        pl.semaphore_wait(barrier, 2 + n_fsdp)
-
 
     def r1_copy(p):
         return remote_copy(sb.at[p % RING], r1.at[p], r1s.at[p], r1r.at[p], sib, mine)
@@ -618,6 +609,16 @@
 
     for copy in tiles(0, 0, 0):
         copy.start()
+
+    @pl.when(depth == 0)
+    def _():
+        pl.semaphore_wait(barrier, 1 + n_fsdp)
+
+    @pl.when(depth > 0)
+    def _():
+        greet(outward, mine)
+        pl.semaphore_wait(barrier, 2 + n_fsdp)
+
     for u, unit in enumerate(units):
 
         def step(i, carry, u=u, unit=unit):

time: 650 us -> 644 us (level)
  no operation moved by 1% of the time
where the time goes in v8:
time: 644 us; the launch traced here: 642 us
  Pallas kernels  632 us (98%)
  local copies, waits for them, and re-layouts  9.43 us (1%)
    pallas_call x1, Pallas kernels, backward(): pl.pallas_call(functools.partial(backward_kernel, n_fsdp, n_rep, heads_k,...  343 us
    pallas_call x1, Pallas kernels, forward(): pl.pallas_call(functools.partial(forward_kernel, n_fsdp, n_rep, heads_k),...  254 us
    pallas_call x1, Pallas kernels, widened_both(): pl.pallas_call(widen_both_kernel, grid=(2, n_fsdp), out_shape=[jax.ShapeD...  13.9 us

profile of v8, /device:TPU:0, one launch (start us, length us, event | category | flops | bytes accessed | tf_op | source)
XLA Modules:
  0.0 641.8 jit_solution(3918225177746500755)
XLA Ops:
  0.6 0.7 tile.20
  1.3 0.1 tile.21
  1.4 0.7 tile.8
  2.0 0.1 tile.9
  2.2 1.9 concatenate.3.refs_1_
  4.1 254.2 %forward.1 = (bf16[1024,2048]{1,0:T(8,128)(2,1)}, f32[1024,1536]{1,0:T(8,128)}, bf16[1024,512]{1,0:T(8,128)(2,1)}, bf16[1024,256]{1,0:T(8,128)(2,1)}, bf16[1024,...) custom-call(bf16[256,2048]{1,0:T(8,128)(2,1)} %refs_11_.3, ...), custom_call_target="tpu_custom_call" | custom-call | tf_op jit(solution)/shard_map/forward/pallas_call | solution.py:1694
  258.2 1.3 slice_reduce_fusion
  259.5 343.2 %backward.1 = (bf16[52,2,256,512]{3,2,1,0:T(8,128)(2,1)}, bf16[1024,2048]{1,0:T(8,128)(2,1)}, bf16[1024,1536]{1,0:T(8,128)(2,1)}, bf16[52,256,512]{2,1,0:T(8,128...) custom-call(bf16[1024,1536]{1,0:T(8,128)(2,1)} %get-tuple-element.46.refs_0_, ...), custom_call_target="tpu_custom_call" | custom-call | flops 55834574848 | bytes 1073741824 | tf_op jit(solution)/shard_map/backward/pallas_call | solution.py:739
  602.8 1.4 constant_dynamic-slice_fusion.1
  604.2 1.3 dynamic-slice_bitcast_fusion
  605.5 8.7 %widen_heads.1 = (f32[512,2048]{1,0:T(8,128)}, f32[512,2048]{1,0:T(8,128)}, f32[512,1024]{1,0:T(8,128)}, f32[512,1024]{1,0:T(8,128)}) custom-call(bf16[52,2,256,512]{3,2,1,0:T(8,128)(2,1)} %get-tuple-element.66.query_in.gate_in.pair_in.in_ref, bf16[52,2,256,512]{3,2,1,0:T(8,128)(2,1)} %get-tuple-element.66.query_in.gate_in.pair_in.in_ref, ...), custom_call_target="tpu_custom_call" | custom-call | tf_op jit(solution)/shard_map/widen_heads/pallas_call | solution.py:834
  614.2 3.4 widen.2
  617.6 13.9 %widen_both.1 = (f32[512,6144]{1,0:T(8,128)}, f32[512,6144]{1,0:T(8,128)}) custom-call(bf16[52,2,256,512]{3,2,1,0:T(8,128)(2,1)} %get-tuple-element.66.query_in.gate_in.pair_in.in_ref), custom_call_target="tpu_custom_call" | custom-call | tf_op jit(solution)/shard_map/widen_both/pallas_call | solution.py:806
  631.5 0.0 copy-start
  631.5 0.0 copy-start.1
  631.5 8.3 %widen.3 = f32[1536,2048]{1,0:T(8,128)} custom-call(bf16[52,2,256,512]{3,2,1,0:T(8,128)(2,1)} %get-tuple-element.66.query_in.gate_in.pair_in.in_ref), custom_call_target="tpu_custom_call" | custom-call | tf_op jit(solution)/shard_map/widen/pallas_call | solution.py:787
  639.8 0.0 copy-done
  639.8 1.0 copy.34
  640.8 0.0 copy-done.1
  640.8 1.0 copy.35
  (2 shorter events, 0.0 us)
Async XLA Ops:
  631.5 8.3 %copy-start = (bf16[256,2048]{1,0:T(8,128)(2,1)S(1)}, bf16[256,2048]{1,0:T(8,128)(2,1)}, u32[]{:S(2)}) copy-start(bf16[256,2048]{1,0:T(8,128)(2,1)} %get-tuple-element.94) | copy-start | bytes 3145732
  631.5 9.3 %copy-start.1 = (bf16[256,2048]{1,0:T(8,128)(2,1)S(1)}, bf16[256,2048]{1,0:T(8,128)(2,1)}, u32[]{:S(2)}) copy-start(bf16[256,2048]{1,0:T(8,128)(2,1)} %get-tuple-element.96) | copy-start | bytes 3145732

commit v9 on v8

--- a/solution.py
+++ b/solution.py
@@ -53,7 +53,7 @@
 RING = 4
 
 
-ROW_STEP = 32
+ROW_STEP = 64
 TILES = 8
 
 

time: 644 us -> 643 us (level)
  no operation moved by 1% of the time
where the time goes in v9:
time: 643 us; the launch traced here: 641 us
  Pallas kernels  631 us (98%)
  local copies, waits for them, and re-layouts  9.43 us (1%)
    pallas_call x1, Pallas kernels, backward(): pl.pallas_call(functools.partial(backward_kernel, n_fsdp, n_rep, heads_k,...  343 us
    pallas_call x1, Pallas kernels, forward(): pl.pallas_call(functools.partial(forward_kernel, n_fsdp, n_rep, heads_k),...  254 us
    pallas_call x1, Pallas kernels, widened_both(): pl.pallas_call(widen_both_kernel, grid=(2, n_fsdp), out_shape=[jax.ShapeD...  13.9 us

profile of v9, /device:TPU:0, one launch (start us, length us, event | category | flops | bytes accessed | tf_op | source)
XLA Modules:
  0.0 641.4 jit_solution(14415340808042278767)
XLA Ops:
  0.6 0.7 tile.20
  1.3 0.1 tile.21
  1.4 0.7 tile.8
  2.0 0.1 tile.9
  2.2 1.9 concatenate.3.refs_1_
  4.1 253.8 %forward.1 = (bf16[1024,2048]{1,0:T(8,128)(2,1)}, f32[1024,1536]{1,0:T(8,128)}, bf16[1024,512]{1,0:T(8,128)(2,1)}, bf16[1024,256]{1,0:T(8,128)(2,1)}, bf16[1024,...) custom-call(bf16[256,2048]{1,0:T(8,128)(2,1)} %refs_11_.3, ...), custom_call_target="tpu_custom_call" | custom-call | tf_op jit(solution)/shard_map/forward/pallas_call | solution.py:1694
  257.8 1.3 slice_reduce_fusion
  259.2 343.2 %backward.1 = (bf16[52,2,256,512]{3,2,1,0:T(8,128)(2,1)}, bf16[1024,2048]{1,0:T(8,128)(2,1)}, bf16[1024,1536]{1,0:T(8,128)(2,1)}, bf16[52,256,512]{2,1,0:T(8,128...) custom-call(bf16[1024,1536]{1,0:T(8,128)(2,1)} %get-tuple-element.46.refs_0_, ...), custom_call_target="tpu_custom_call" | custom-call | flops 55834574848 | bytes 1073741824 | tf_op jit(solution)/shard_map/backward/pallas_call | solution.py:739
  602.3 1.4 constant_dynamic-slice_fusion.1
  603.8 1.3 dynamic-slice_bitcast_fusion
  605.1 8.7 %widen_heads.1 = (f32[512,2048]{1,0:T(8,128)}, f32[512,2048]{1,0:T(8,128)}, f32[512,1024]{1,0:T(8,128)}, f32[512,1024]{1,0:T(8,128)}) custom-call(bf16[52,2,256,512]{3,2,1,0:T(8,128)(2,1)} %get-tuple-element.66.query_in.gate_in.pair_in.in_ref, bf16[52,2,256,512]{3,2,1,0:T(8,128)(2,1)} %get-tuple-element.66.query_in.gate_in.pair_in.in_ref, ...), custom_call_target="tpu_custom_call" | custom-call | tf_op jit(solution)/shard_map/widen_heads/pallas_call | solution.py:834
  613.8 3.4 widen.2
  617.1 13.9 %widen_both.1 = (f32[512,6144]{1,0:T(8,128)}, f32[512,6144]{1,0:T(8,128)}) custom-call(bf16[52,2,256,512]{3,2,1,0:T(8,128)(2,1)} %get-tuple-element.66.query_in.gate_in.pair_in.in_ref), custom_call_target="tpu_custom_call" | custom-call | tf_op jit(solution)/shard_map/widen_both/pallas_call | solution.py:806
  631.1 0.0 copy-start
  631.1 0.0 copy-start.1
  631.1 8.3 %widen.3 = f32[1536,2048]{1,0:T(8,128)} custom-call(bf16[52,2,256,512]{3,2,1,0:T(8,128)(2,1)} %get-tuple-element.66.query_in.gate_in.pair_in.in_ref), custom_call_target="tpu_custom_call" | custom-call | tf_op jit(solution)/shard_map/widen/pallas_call | solution.py:787
  639.4 0.0 copy-done
  639.4 1.0 copy.34
  640.4 0.0 copy-done.1
  640.4 1.0 copy.35
  (2 shorter events, 0.0 us)
Async XLA Ops:
  631.1 8.3 %copy-start = (bf16[256,2048]{1,0:T(8,128)(2,1)S(1)}, bf16[256,2048]{1,0:T(8,128)(2,1)}, u32[]{:S(2)}) copy-start(bf16[256,2048]{1,0:T(8,128)(2,1)} %get-tuple-element.94) | copy-start | bytes 3145732
  631.1 9.3 %copy-start.1 = (bf16[256,2048]{1,0:T(8,128)(2,1)S(1)}, bf16[256,2048]{1,0:T(8,128)(2,1)}, u32[]{:S(2)}) copy-start(bf16[256,2048]{1,0:T(8,128)(2,1)} %get-tuple-element.96) | copy-start | bytes 3145732
